TPU v7x, 128 devices: a whole 4x4x4 slice. The times are simulated.
128 devices in a mesh: gx: 8 (over x, y_hi), gy: 16 (over z, y_lo, core).
Axes of the slice: x: 4, y: 4 (y_hi: 2, y_lo: 2; y = y_hi * 2 + y_lo), z: 4, core: 2. Of those that a mesh axis runs over, the one named last changes fastest.
Arguments:
- probes: float32 [48, 96, 64, 128], P('gx', 'gy'), may hold values from -6 to 6
- pair_blocks: float32 [48, 96, 9, 128, 128], P('gx', 'gy'), may hold values from -0.09375 to 0.09375
- partners: int32 [48, 96, 9], P('gx', 'gy'), may hold values from 0 to 4607, as said below
- shifts: int32 [2, 48, 96, 9], P(None, 'gx', 'gy'), may hold values from -1 to 1, as said below
- counts: int32 [48, 96], P('gx', 'gy'), may hold values from 1 to 9, as said below
- kpoint: float32 [2], replicated, may hold values from -3.140625 to 3.140625
Outputs:
- last_vector: float32 [48, 96, 64, 128], P('gx', 'gy')
- intersections: float32 [3, 2, 32], replicated
Inputs may be any that keep to these rules, and one draw needn't show every extreme that they name: `partners`: slot 0 of cell (x, y) names the cell itself; slots 1 to 8 name its eight neighbouring cells (x + dx, y + dy) with dx, dy in -1..1 taken periodically modulo 48 and 96, each once, in no fixed order. shifts[0, x, y, s] = (x + dx - px) / 48 and shifts[1, x, y, s] = (y + dy - py) / 96 for the slot's offset (dx, dy) and partner cell (px, py). `counts`: slots at or beyond a cell's count are padding; some cell has all 9 slots live.
All inputs are finite; a program needn't handle non-finite values.
Results may differ from a plain program's by a relative error of at most 0.0001.
Values sent between devices are 32-bit elements; how exact they have to be, the bound alone decides.
No kernel may reach another device: no remote copies, remote signals or barrier semaphores. Data moves between devices by JAX's collectives and lax.ppermute only.
A program may use at most 128 MiB of HBM per device.

v0:
```python
import functools
import math

import jax
import jax.numpy as jnp
from jax import lax
from jax.sharding import Mesh
from jax.sharding import PartitionSpec as P

STEPS = 3
GX_GY = ("gx_0", "gx_1", "gy_0", "gy_1", "gy_2")
GX = ("gx_0", "gx_1")
GY = ("gy_0", "gy_1", "gy_2")


def with_halo(cells, sides, width):
    for axis, dim in sides:
        count = lax.axis_size(axis)
        head = lax.slice_in_dim(cells, 0, width, axis=dim)
        tail = lax.slice_in_dim(cells, cells.shape[dim] - width, cells.shape[dim], axis=dim)
        cells = jnp.concatenate(
            [
                lax.ppermute(tail, axis, [(i, (i + 1) % count) for i in range(count)]),
                cells,
                lax.ppermute(head, axis, [((i + 1) % count, i) for i in range(count)]),
            ],
            axis=dim,
        )
    return cells


def over_axes(x, axes):
    return functools.reduce(lax.psum, axes, x)


def intersection(first, other):
    half = first.shape[2] // 2
    first_re, first_im = (first[:, :, :half], first[:, :, half:])
    other_re, other_im = (other[:, :, :half], other[:, :, half:])
    real_part = jnp.sum(first_re * other_re + first_im * other_im, axis=(0, 1, 3))
    imag_part = jnp.sum(first_re * other_im - first_im * other_re, axis=(0, 1, 3))
    return jnp.stack([real_part, imag_part])


def extend(field):
    return with_halo(field, ((GX, 0), (GY, 1)), 1)


def shards(probes, pair_blocks, partners, shifts, counts, kpoint):
    cells_x, cells_y, width, block = probes.shape
    slot_total = pair_blocks.shape[2]
    half = width // 2
    cells = cells_x * cells_y
    total_x = cells_x * lax.axis_size(GX)
    total_y = cells_y * lax.axis_size(GY)
    start_x = lax.axis_index(GX) * cells_x
    start_y = lax.axis_index(GY) * cells_y
    partner_x = partners // total_y
    partner_y = partners % total_y
    local_x = jnp.mod(partner_x - start_x + 1, total_x)
    local_y = jnp.mod(partner_y - start_y + 1, total_y)
    flat_partner = (local_x * (cells_y + 2) + local_y).reshape(cells, slot_total)
    angle = kpoint[0] * shifts[0].astype(jnp.float32) + kpoint[1] * shifts[1].astype(jnp.float32)
    angle = angle.reshape(cells, slot_total)
    live = (jnp.arange(slot_total, dtype=jnp.int32)[None, :] < counts.reshape(cells, 1)).astype(
        jnp.float32
    )
    cosine = jnp.cos(angle) * live
    sine = jnp.sin(angle) * live
    blocks = pair_blocks.reshape(cells, slot_total, block, block)
    slot_bound = jnp.max(counts)

    def apply_hamiltonian(field):
        source = extend(field).reshape(-1, width, block)

        def accumulate(slot, sums):
            real_sum, imag_sum = sums
            piece = jnp.take(source, flat_partner[:, slot], axis=0)
            chosen = lax.dynamic_index_in_dim(blocks, slot, 1, keepdims=False)
            product = jnp.einsum("npb,nba->npa", piece, chosen, precision=lax.Precision.HIGHEST)
            cos_part = lax.dynamic_index_in_dim(cosine, slot, 1, keepdims=False)[:, None, None]
            sin_part = lax.dynamic_index_in_dim(sine, slot, 1, keepdims=False)[:, None, None]
            real_part = product[:, :half]
            imag_part = product[:, half:]
            return (
                real_sum + cos_part * real_part - sin_part * imag_part,
                imag_sum + sin_part * real_part + cos_part * imag_part,
            )

        zeros = jnp.zeros((cells, half, block), jnp.float32)
        real_sum, imag_sum = lax.fori_loop(0, slot_bound, accumulate, (zeros, zeros))
        return jnp.concatenate([real_sum, imag_sum], axis=1).reshape(field.shape)

    scale = 1.0 / math.sqrt(total_x * total_y * block)

    def reduce_one(field):
        return over_axes(intersection(probes, field), GX_GY) * scale

    before = probes
    current = apply_hamiltonian(probes)
    partial_list = []
    partial_list.append(reduce_one(current))
    for step in range(STEPS - 1):
        following = 2.0 * apply_hamiltonian(current) - before
        before, current = (current, following)
        partial_list.append(reduce_one(current))
    found = jnp.stack(partial_list)
    return (current, found)


def solution(mesh):
    torus = Mesh(mesh.devices.reshape(4, 2, 4, 2, 2), ("gx_0", "gx_1", "gy_0", "gy_1", "gy_2"))
    placed = (
        P(GX, GY, None, None),
        P(GX, GY, None, None, None),
        P(GX, GY, None),
        P(None, GX, GY, None),
        P(GX, GY),
        P(),
    )
    return jax.shard_map(
        shards, mesh=torus, in_specs=placed, out_specs=(P(GX, GY, None, None), P()), check_vma=False
    )
```

profile of v0, /device:TPU:1, one launch (start us, length us, event | category | flops | bytes accessed | tf_op | source)
XLA Modules:
  0.0 337.3 jit_solution(3291438338109798345)
XLA Ops:
  22.6 15.4 %copy.12 = f32[6,6,9,128,128]{4,3,1,0,2:T(8,128)} copy(f32[6,6,9,128,128]{4,3,2,1,0:T(8,128)} %param.15) | data formatting | bytes 42467328 | tf_op args[1]
  42.0 60.1 %while.36 = (s32[]{:T(128)}, f32[36,32,128]{2,1,0:T(8,128)}, f32[36,32,128]{2,1,0:T(8,128)}, s32[]{:T(128)}, f32[36,9]{0,1:T(8,128)S(1)}, /*index=5*/s32[36,9]{0...) while((s32[]{:T(128)}, f32[36,32,128]{2,1,0:T(8,128)}, ...), condition=%wide.region_2.4_spmd, body=%wide.region_1.3_spmd.sunk | while | flops 454460640 | bytes 20059900 | solution.py:91
  43.4 4.0 %fusion.62 = f32[36,64,128]{2,1,0:T(8,128)S(1)} fusion(f32[36,9,128,128]{3,2,0,1:T(8,128)} %get-tuple-element.535, s32[]{:T(128)S(6)} %select_n.106, f32[36,64,128]{2,1,0:T(8,128)S(1)} %gather_fusion, pred[36]{0:T(512)(128)(4,1)S(1)} %get-tuple-element.469), kind=kOutput, calls=%fused_computation.3.clone.1 | convolution fusion | flops 453279744 | bytes 4718632 | tf_op jit(solution)/shard_map/while/body/npb,nba->npa/dot_general | solution.py:80
  50.8 4.0 %fusion.62 = f32[36,64,128]{2,1,0:T(8,128)S(1)} fusion(f32[36,9,128,128]{3,2,0,1:T(8,128)} %get-tuple-element.535, s32[]{:T(128)S(6)} %select_n.106, f32[36,64,128]{2,1,0:T(8,128)S(1)} %gather_fusion, pred[36]{0:T(512)(128)(4,1)S(1)} %get-tuple-element.469), kind=kOutput, calls=%fused_computation.3.clone.1 | convolution fusion | flops 453279744 | bytes 4718632 | tf_op jit(solution)/shard_map/while/body/npb,nba->npa/dot_general | solution.py:80
  58.2 4.0 %fusion.62 = f32[36,64,128]{2,1,0:T(8,128)S(1)} fusion(f32[36,9,128,128]{3,2,0,1:T(8,128)} %get-tuple-element.535, s32[]{:T(128)S(6)} %select_n.106, f32[36,64,128]{2,1,0:T(8,128)S(1)} %gather_fusion, pred[36]{0:T(512)(128)(4,1)S(1)} %get-tuple-element.469), kind=kOutput, calls=%fused_computation.3.clone.1 | convolution fusion | flops 453279744 | bytes 4718632 | tf_op jit(solution)/shard_map/while/body/npb,nba->npa/dot_general | solution.py:80
  65.7 4.0 %fusion.62 = f32[36,64,128]{2,1,0:T(8,128)S(1)} fusion(f32[36,9,128,128]{3,2,0,1:T(8,128)} %get-tuple-element.535, s32[]{:T(128)S(6)} %select_n.106, f32[36,64,128]{2,1,0:T(8,128)S(1)} %gather_fusion, pred[36]{0:T(512)(128)(4,1)S(1)} %get-tuple-element.469), kind=kOutput, calls=%fused_computation.3.clone.1 | convolution fusion | flops 453279744 | bytes 4718632 | tf_op jit(solution)/shard_map/while/body/npb,nba->npa/dot_general | solution.py:80
  73.1 4.0 %fusion.62 = f32[36,64,128]{2,1,0:T(8,128)S(1)} fusion(f32[36,9,128,128]{3,2,0,1:T(8,128)} %get-tuple-element.535, s32[]{:T(128)S(6)} %select_n.106, f32[36,64,128]{2,1,0:T(8,128)S(1)} %gather_fusion, pred[36]{0:T(512)(128)(4,1)S(1)} %get-tuple-element.469), kind=kOutput, calls=%fused_computation.3.clone.1 | convolution fusion | flops 453279744 | bytes 4718632 | tf_op jit(solution)/shard_map/while/body/npb,nba->npa/dot_general | solution.py:80
  80.5 4.0 %fusion.62 = f32[36,64,128]{2,1,0:T(8,128)S(1)} fusion(f32[36,9,128,128]{3,2,0,1:T(8,128)} %get-tuple-element.535, s32[]{:T(128)S(6)} %select_n.106, f32[36,64,128]{2,1,0:T(8,128)S(1)} %gather_fusion, pred[36]{0:T(512)(128)(4,1)S(1)} %get-tuple-element.469), kind=kOutput, calls=%fused_computation.3.clone.1 | convolution fusion | flops 453279744 | bytes 4718632 | tf_op jit(solution)/shard_map/while/body/npb,nba->npa/dot_general | solution.py:80
  88.0 4.0 %fusion.62 = f32[36,64,128]{2,1,0:T(8,128)S(1)} fusion(f32[36,9,128,128]{3,2,0,1:T(8,128)} %get-tuple-element.535, s32[]{:T(128)S(6)} %select_n.106, f32[36,64,128]{2,1,0:T(8,128)S(1)} %gather_fusion, pred[36]{0:T(512)(128)(4,1)S(1)} %get-tuple-element.469), kind=kOutput, calls=%fused_computation.3.clone.1 | convolution fusion | flops 453279744 | bytes 4718632 | tf_op jit(solution)/shard_map/while/body/npb,nba->npa/dot_general | solution.py:80
  95.4 4.0 %fusion.62 = f32[36,64,128]{2,1,0:T(8,128)S(1)} fusion(f32[36,9,128,128]{3,2,0,1:T(8,128)} %get-tuple-element.535, s32[]{:T(128)S(6)} %select_n.106, f32[36,64,128]{2,1,0:T(8,128)S(1)} %gather_fusion, pred[36]{0:T(512)(128)(4,1)S(1)} %get-tuple-element.469), kind=kOutput, calls=%fused_computation.3.clone.1 | convolution fusion | flops 453279744 | bytes 4718632 | tf_op jit(solution)/shard_map/while/body/npb,nba->npa/dot_general | solution.py:80
  103.5 8.3 %collective-permute-start.4 = (f32[1,6,64,128]{3,2,1,0:T(8,128)S(1)}, f32[1,6,64,128]{3,2,1,0:T(8,128)S(1)}, u32[]{:S(2)}, u32[]{:S(2)}) collective-permute-start(f32[1,6,64,128]{3,2,1,0:T(8,128)S(1)} %get-tuple-element.290), channel_id=1, source_target_pairs={{0,16},{16,32},{32,48},{48,64},{64,80},{80,96},{96,112},{112,0},{1... | collective-permute-start | bytes 589832 | tf_op jit(solution)/shard_map/ppermute | solution.py:23
  119.9 4.7 %collective-permute-start.6 = (f32[8,1,64,128]{3,2,1,0:T(8,128)S(1)}, f32[8,1,64,128]{3,2,1,0:T(8,128)S(1)}, u32[]{:S(2)}, u32[]{:S(2)}) collective-permute-start(f32[8,1,64,128]{3,2,1,0:T(8,128)S(1)} %get-tuple-element.282), channel_id=1, source_target_pairs={{0,1},{1,2},{2,3},{3,4},{4,5},{5,6},{6,7},{7,8},{8,9},{9,10},{10,1... | collective-permute-start | bytes 786440 | tf_op jit(solution)/shard_map/ppermute | solution.py:23
  128.6 4.8 %collective-permute-done.7 = f32[8,1,64,128]{3,2,1,0:T(8,128)} collective-permute-done((f32[8,1,64,128]{3,2,1,0:T(8,128)S(1)}, f32[8,1,64,128]{3,2,1,0:T(8,128)}, u32[]{:S(2)}, u32[]{:S(2)}) %collective-permute-start.7) | collective-permute-done | bytes 262176 | tf_op jit(solution)/shard_map/ppermute | solution.py:25
  136.6 60.3 %while.37 = (s32[]{:T(128)}, f32[36,32,128]{2,1,0:T(8,128)}, f32[36,32,128]{2,1,0:T(8,128)}, s32[]{:T(128)}, f32[36,9]{0,1:T(8,128)S(1)}, /*index=5*/s32[36,9]{0...) while((s32[]{:T(128)}, f32[36,32,128]{2,1,0:T(8,128)}, ...), condition=%wide.region_4.6_spmd, body=%wide.region_3.5_spmd.sunk | while | flops 454460640 | bytes 20059900 | solution.py:91
  137.9 4.0 %fusion.66 = f32[36,64,128]{2,1,0:T(8,128)S(1)} fusion(f32[36,9,128,128]{3,2,0,1:T(8,128)} %get-tuple-element.571, s32[]{:T(128)S(6)} %select_n.108, f32[36,64,128]{2,1,0:T(8,128)S(1)} %gather_fusion.1, pred[36]{0:T(512)(128)(4,1)S(1)} %get-tuple-element.484), kind=kOutput, calls=%fused_computation.22.clone.1 | convolution fusion | flops 453279744 | bytes 4718632 | tf_op jit(solution)/shard_map/while/body/npb,nba->npa/dot_general | solution.py:80
  145.4 4.0 %fusion.66 = f32[36,64,128]{2,1,0:T(8,128)S(1)} fusion(f32[36,9,128,128]{3,2,0,1:T(8,128)} %get-tuple-element.571, s32[]{:T(128)S(6)} %select_n.108, f32[36,64,128]{2,1,0:T(8,128)S(1)} %gather_fusion.1, pred[36]{0:T(512)(128)(4,1)S(1)} %get-tuple-element.484), kind=kOutput, calls=%fused_computation.22.clone.1 | convolution fusion | flops 453279744 | bytes 4718632 | tf_op jit(solution)/shard_map/while/body/npb,nba->npa/dot_general | solution.py:80
  152.9 4.0 %fusion.66 = f32[36,64,128]{2,1,0:T(8,128)S(1)} fusion(f32[36,9,128,128]{3,2,0,1:T(8,128)} %get-tuple-element.571, s32[]{:T(128)S(6)} %select_n.108, f32[36,64,128]{2,1,0:T(8,128)S(1)} %gather_fusion.1, pred[36]{0:T(512)(128)(4,1)S(1)} %get-tuple-element.484), kind=kOutput, calls=%fused_computation.22.clone.1 | convolution fusion | flops 453279744 | bytes 4718632 | tf_op jit(solution)/shard_map/while/body/npb,nba->npa/dot_general | solution.py:80
  160.3 4.0 %fusion.66 = f32[36,64,128]{2,1,0:T(8,128)S(1)} fusion(f32[36,9,128,128]{3,2,0,1:T(8,128)} %get-tuple-element.571, s32[]{:T(128)S(6)} %select_n.108, f32[36,64,128]{2,1,0:T(8,128)S(1)} %gather_fusion.1, pred[36]{0:T(512)(128)(4,1)S(1)} %get-tuple-element.484), kind=kOutput, calls=%fused_computation.22.clone.1 | convolution fusion | flops 453279744 | bytes 4718632 | tf_op jit(solution)/shard_map/while/body/npb,nba->npa/dot_general | solution.py:80
  167.8 4.0 %fusion.66 = f32[36,64,128]{2,1,0:T(8,128)S(1)} fusion(f32[36,9,128,128]{3,2,0,1:T(8,128)} %get-tuple-element.571, s32[]{:T(128)S(6)} %select_n.108, f32[36,64,128]{2,1,0:T(8,128)S(1)} %gather_fusion.1, pred[36]{0:T(512)(128)(4,1)S(1)} %get-tuple-element.484), kind=kOutput, calls=%fused_computation.22.clone.1 | convolution fusion | flops 453279744 | bytes 4718632 | tf_op jit(solution)/shard_map/while/body/npb,nba->npa/dot_general | solution.py:80
  182.7 4.0 %fusion.66 = f32[36,64,128]{2,1,0:T(8,128)S(1)} fusion(f32[36,9,128,128]{3,2,0,1:T(8,128)} %get-tuple-element.571, s32[]{:T(128)S(6)} %select_n.108, f32[36,64,128]{2,1,0:T(8,128)S(1)} %gather_fusion.1, pred[36]{0:T(512)(128)(4,1)S(1)} %get-tuple-element.484), kind=kOutput, calls=%fused_computation.22.clone.1 | convolution fusion | flops 453279744 | bytes 4718632 | tf_op jit(solution)/shard_map/while/body/npb,nba->npa/dot_general | solution.py:80
  198.8 7.5 %collective-permute-start.8 = (f32[1,6,64,128]{3,2,1,0:T(8,128)S(1)}, f32[1,6,64,128]{3,2,1,0:T(8,128)S(1)}, u32[]{:S(2)}, u32[]{:S(2)}) collective-permute-start(f32[1,6,64,128]{3,2,1,0:T(8,128)S(1)} %get-tuple-element.288), channel_id=1, source_target_pairs={{0,16},{16,32},{32,48},{48,64},{64,80},{80,96},{96,112},{112,0},{1... | collective-permute-start | bytes 589832 | tf_op jit(solution)/shard_map/ppermute | solution.py:23
  206.4 4.4 %collective-permute-start.9 = (f32[1,6,64,128]{3,2,1,0:T(8,128)S(1)}, f32[1,6,64,128]{3,2,1,0:T(8,128)S(1)}, u32[]{:S(2)}, u32[]{:S(2)}) collective-permute-start(f32[1,6,64,128]{3,2,1,0:T(8,128)S(1)} %get-tuple-element.289), channel_id=1, source_target_pairs={{16,0},{32,16},{48,32},{64,48},{80,64},{96,80},{112,96},{0,112},{1... | collective-permute-start | bytes 589832 | tf_op jit(solution)/shard_map/ppermute | solution.py:25
  228.9 60.2 %while.38 = (s32[]{:T(128)}, f32[36,32,128]{2,1,0:T(8,128)}, f32[36,32,128]{2,1,0:T(8,128)}, s32[]{:T(128)}, f32[36,9]{0,1:T(8,128)S(1)}, /*index=5*/s32[36,9]{0...) while((s32[]{:T(128)}, f32[36,32,128]{2,1,0:T(8,128)}, ...), condition=%wide.region_6.8_spmd, body=%wide.region_5.7_spmd.sunk | while | flops 454460640 | bytes 20059900 | solution.py:91
  230.2 4.0 %fusion.70 = f32[36,64,128]{2,1,0:T(8,128)S(1)} fusion(f32[36,9,128,128]{3,2,0,1:T(8,128)} %get-tuple-element.607, s32[]{:T(128)S(6)} %select_n.110, f32[36,64,128]{2,1,0:T(8,128)S(1)} %gather_fusion.2, pred[36]{0:T(512)(128)(4,1)S(1)} %get-tuple-element.499), kind=kOutput, calls=%fused_computation.41.clone.1 | convolution fusion | flops 453279744 | bytes 4718632 | tf_op jit(solution)/shard_map/while/body/npb,nba->npa/dot_general | solution.py:80
  245.1 4.0 %fusion.70 = f32[36,64,128]{2,1,0:T(8,128)S(1)} fusion(f32[36,9,128,128]{3,2,0,1:T(8,128)} %get-tuple-element.607, s32[]{:T(128)S(6)} %select_n.110, f32[36,64,128]{2,1,0:T(8,128)S(1)} %gather_fusion.2, pred[36]{0:T(512)(128)(4,1)S(1)} %get-tuple-element.499), kind=kOutput, calls=%fused_computation.41.clone.1 | convolution fusion | flops 453279744 | bytes 4718632 | tf_op jit(solution)/shard_map/while/body/npb,nba->npa/dot_general | solution.py:80
  260.0 4.0 %fusion.70 = f32[36,64,128]{2,1,0:T(8,128)S(1)} fusion(f32[36,9,128,128]{3,2,0,1:T(8,128)} %get-tuple-element.607, s32[]{:T(128)S(6)} %select_n.110, f32[36,64,128]{2,1,0:T(8,128)S(1)} %gather_fusion.2, pred[36]{0:T(512)(128)(4,1)S(1)} %get-tuple-element.499), kind=kOutput, calls=%fused_computation.41.clone.1 | convolution fusion | flops 453279744 | bytes 4718632 | tf_op jit(solution)/shard_map/while/body/npb,nba->npa/dot_general | solution.py:80
  274.9 4.0 %fusion.70 = f32[36,64,128]{2,1,0:T(8,128)S(1)} fusion(f32[36,9,128,128]{3,2,0,1:T(8,128)} %get-tuple-element.607, s32[]{:T(128)S(6)} %select_n.110, f32[36,64,128]{2,1,0:T(8,128)S(1)} %gather_fusion.2, pred[36]{0:T(512)(128)(4,1)S(1)} %get-tuple-element.499), kind=kOutput, calls=%fused_computation.41.clone.1 | convolution fusion | flops 453279744 | bytes 4718632 | tf_op jit(solution)/shard_map/while/body/npb,nba->npa/dot_general | solution.py:80
  293.6 14.9 %all-reduce.1 = (f32[2,32]{1,0:T(2,128)S(1)}, f32[2,32]{1,0:T(2,128)S(1)}, f32[2,32]{1,0:T(2,128)S(1)}) all-reduce(f32[2,32]{1,0:T(2,128)S(1)} %pad_maximum_fusion.12, f32[2,32]{1,0:T(2,128)S(1)} %get-tuple-element.299, f32[2,32]{1,0:T(2,128)S(1)} %get-tuple-element.298), channel_id=1, replica_groups=mesh['gx_0'=4,'gx_1'=2,'gy_0'=4,'gy_1'=2,'gy_2'=2] {'gx_0'}, use_global_device_ids=true, to_apply=%region_23.25 | all-reduce | flops 192 | bytes 1536 | tf_op jit(solution)/shard_map/psum | solution.py:33
  308.4 6.8 %all-reduce.4 = (f32[2,32]{1,0:T(2,128)S(1)}, f32[2,32]{1,0:T(2,128)S(1)}, f32[2,32]{1,0:T(2,128)S(1)}) all-reduce(f32[2,32]{1,0:T(2,128)S(1)} %get-tuple-element.250, f32[2,32]{1,0:T(2,128)S(1)} %get-tuple-element.251, f32[2,32]{1,0:T(2,128)S(1)} %get-tuple-element.252), channel_id=1, replica_groups=mesh['gx_0'=4,'gx_1'=2,'gy_0'=4,'gy_1'=2,'gy_2'=2] {'gx_1'}, use_global_device_ids=true, to_apply=%region_24.26 | all-reduce | flops 192 | bytes 1536 | tf_op jit(solution)/shard_map/psum | solution.py:33
  315.2 7.6 %all-reduce = (f32[2,32]{1,0:T(2,128)S(1)}, f32[2,32]{1,0:T(2,128)S(1)}, f32[2,32]{1,0:T(2,128)S(1)}) all-reduce(f32[2,32]{1,0:T(2,128)S(1)} %get-tuple-element.259, f32[2,32]{1,0:T(2,128)S(1)} %get-tuple-element.260, f32[2,32]{1,0:T(2,128)S(1)} %get-tuple-element.261), channel_id=1, replica_groups=mesh['gx_0'=4,'gx_1'=2,'gy_0'=4,'gy_1'=2,'gy_2'=2] {'gy_0'}, use_global_device_ids=true, to_apply=%region_25.27 | all-reduce | flops 192 | bytes 1536 | tf_op jit(solution)/shard_map/psum | solution.py:33
  322.8 5.4 %all-reduce.3 = (f32[2,32]{1,0:T(2,128)S(1)}, f32[2,32]{1,0:T(2,128)S(1)}, f32[2,32]{1,0:T(2,128)S(1)}) all-reduce(f32[2,32]{1,0:T(2,128)S(1)} %get-tuple-element.247, f32[2,32]{1,0:T(2,128)S(1)} %get-tuple-element.248, f32[2,32]{1,0:T(2,128)S(1)} %get-tuple-element.249), channel_id=1, replica_groups=mesh['gx_0'=4,'gx_1'=2,'gy_0'=4,'gy_1'=2,'gy_2'=2] {'gy_1'}, use_global_device_ids=true, to_apply=%region_26.28 | all-reduce | flops 192 | bytes 1536 | tf_op jit(solution)/shard_map/psum | solution.py:33
  328.2 8.5 %all-reduce.2 = (f32[2,32]{1,0:T(2,128)S(1)}, f32[2,32]{1,0:T(2,128)S(1)}, f32[2,32]{1,0:T(2,128)S(1)}) all-reduce(f32[2,32]{1,0:T(2,128)S(1)} %get-tuple-element.256, f32[2,32]{1,0:T(2,128)S(1)} %get-tuple-element.257, f32[2,32]{1,0:T(2,128)S(1)} %get-tuple-element.258), channel_id=1, replica_groups=mesh['gx_0'=4,'gx_1'=2,'gy_0'=4,'gy_1'=2,'gy_2'=2] {'gy_2'}, use_global_device_ids=true, to_apply=%region_27.29 | all-reduce | flops 192 | bytes 1536 | tf_op jit(solution)/shard_map/psum | solution.py:33
  (412 shorter events, 157.1 us)
Async XLA Ops:
  0.6 12.8 %copy-start.17 = (f32[6,6,64,128]{3,2,1,0:T(8,128)S(1)}, f32[6,6,64,128]{3,2,1,0:T(8,128)}, u32[]{:S(2)}) copy-start(f32[6,6,64,128]{3,2,1,0:T(8,128)} %param.14) | copy-start | bytes 3538948
  1.8 11.6 %collective-permute-start = (f32[1,6,64,128]{3,2,1,0:T(8,128)S(1)}, f32[1,6,64,128]{3,2,1,0:T(8,128)S(1)}, u32[]{:S(2)}, u32[]{:S(2)}) collective-permute-start(f32[1,6,64,128]{3,2,1,0:T(8,128)S(1)} %get-tuple-element.293), channel_id=1, source_target_pairs={{0,16},{16,32},{32,48},{48,64},{64,80},{80,96},{96,112},{112,0},{1... | collective-permute-start | bytes 589832 | tf_op jit(solution)/shard_map/ppermute | solution.py:23
  5.6 11.8 %collective-permute-start.1 = (f32[1,6,64,128]{3,2,1,0:T(8,128)S(1)}, f32[1,6,64,128]{3,2,1,0:T(8,128)S(1)}, u32[]{:S(2)}, u32[]{:S(2)}) collective-permute-start(f32[1,6,64,128]{3,2,1,0:T(8,128)S(1)} %get-tuple-element.292), channel_id=1, source_target_pairs={{16,0},{32,16},{48,32},{64,48},{80,64},{96,80},{112,96},{0,112},{1... | collective-permute-start | bytes 589832 | tf_op jit(solution)/shard_map/ppermute | solution.py:25
  13.5 6.7 %copy-start.26 = (s32[2,6,6,9]{3,0,2,1:T(2,128)S(1)}, s32[2,6,6,9]{3,0,2,1:T(2,128)}, u32[]{:S(2)}) copy-start(s32[2,6,6,9]{3,0,2,1:T(2,128)} %param.17) | copy-start | bytes 7780
  13.5 8.8 %copy-start.27 = (s32[6,6]{1,0:T(8,128)S(1)}, s32[6,6]{1,0:T(8,128)}, u32[]{:S(2)}) copy-start(s32[6,6]{1,0:T(8,128)} %param.18) | copy-start | bytes 436
  18.6 20.1 %collective-permute-start.2 = (f32[8,1,64,128]{3,2,1,0:T(8,128)S(1)}, f32[8,1,64,128]{3,2,1,0:T(8,128)S(1)}, u32[]{:S(2)}, u32[]{:S(2)}) collective-permute-start(f32[8,1,64,128]{3,2,1,0:T(8,128)S(1)} %get-tuple-element.284), channel_id=1, source_target_pairs={{0,1},{1,2},{2,3},{3,4},{4,5},{5,6},{6,7},{7,8},{8,9},{9,10},{10,1... | collective-permute-start | bytes 786440 | tf_op jit(solution)/shard_map/ppermute | solution.py:23
  20.2 18.5 %collective-permute-start.3 = (f32[8,1,64,128]{3,2,1,0:T(8,128)S(1)}, f32[8,1,64,128]{3,2,1,0:T(8,128)S(1)}, u32[]{:S(2)}, u32[]{:S(2)}) collective-permute-start(f32[8,1,64,128]{3,2,1,0:T(8,128)S(1)} %get-tuple-element.285), channel_id=1, source_target_pairs={{1,0},{2,1},{3,2},{4,3},{5,4},{6,5},{7,6},{8,7},{9,8},{10,9},{11,1... | collective-permute-start | bytes 786440 | tf_op jit(solution)/shard_map/ppermute | solution.py:25
  43.3 4.1 %copy-start.4 = (f32[36,32,128]{2,1,0:T(8,128)S(1)}, f32[36,32,128]{2,1,0:T(8,128)}, u32[]{:S(2)}) copy-start(f32[36,32,128]{2,1,0:T(8,128)} %get-tuple-element.517) | copy-start | bytes 1769476 | tf_op jit(solution)/shard_map/while
  50.8 4.1 %copy-start.4 = (f32[36,32,128]{2,1,0:T(8,128)S(1)}, f32[36,32,128]{2,1,0:T(8,128)}, u32[]{:S(2)}) copy-start(f32[36,32,128]{2,1,0:T(8,128)} %get-tuple-element.517) | copy-start | bytes 1769476 | tf_op jit(solution)/shard_map/while
  58.2 4.1 %copy-start.4 = (f32[36,32,128]{2,1,0:T(8,128)S(1)}, f32[36,32,128]{2,1,0:T(8,128)}, u32[]{:S(2)}) copy-start(f32[36,32,128]{2,1,0:T(8,128)} %get-tuple-element.517) | copy-start | bytes 1769476 | tf_op jit(solution)/shard_map/while
  65.6 4.1 %copy-start.4 = (f32[36,32,128]{2,1,0:T(8,128)S(1)}, f32[36,32,128]{2,1,0:T(8,128)}, u32[]{:S(2)}) copy-start(f32[36,32,128]{2,1,0:T(8,128)} %get-tuple-element.517) | copy-start | bytes 1769476 | tf_op jit(solution)/shard_map/while
  73.1 4.1 %copy-start.4 = (f32[36,32,128]{2,1,0:T(8,128)S(1)}, f32[36,32,128]{2,1,0:T(8,128)}, u32[]{:S(2)}) copy-start(f32[36,32,128]{2,1,0:T(8,128)} %get-tuple-element.517) | copy-start | bytes 1769476 | tf_op jit(solution)/shard_map/while
  80.5 4.1 %copy-start.4 = (f32[36,32,128]{2,1,0:T(8,128)S(1)}, f32[36,32,128]{2,1,0:T(8,128)}, u32[]{:S(2)}) copy-start(f32[36,32,128]{2,1,0:T(8,128)} %get-tuple-element.517) | copy-start | bytes 1769476 | tf_op jit(solution)/shard_map/while
  88.0 4.1 %copy-start.4 = (f32[36,32,128]{2,1,0:T(8,128)S(1)}, f32[36,32,128]{2,1,0:T(8,128)}, u32[]{:S(2)}) copy-start(f32[36,32,128]{2,1,0:T(8,128)} %get-tuple-element.517) | copy-start | bytes 1769476 | tf_op jit(solution)/shard_map/while
  95.4 4.1 %copy-start.4 = (f32[36,32,128]{2,1,0:T(8,128)S(1)}, f32[36,32,128]{2,1,0:T(8,128)}, u32[]{:S(2)}) copy-start(f32[36,32,128]{2,1,0:T(8,128)} %get-tuple-element.517) | copy-start | bytes 1769476 | tf_op jit(solution)/shard_map/while
  103.4 30.0 %copy-start.13 = (f32[36,64,128]{2,1,0:T(8,128)}, f32[36,64,128]{2,1,0:T(8,128)S(1)}, u32[]{:S(2)}) copy-start(f32[36,64,128]{2,1,0:T(8,128)S(1)} %constant_dynamic-update-slice_fusion.3) | copy-start | bytes 3538948
  103.5 13.6 %collective-permute-start.4 = (f32[1,6,64,128]{3,2,1,0:T(8,128)S(1)}, f32[1,6,64,128]{3,2,1,0:T(8,128)S(1)}, u32[]{:S(2)}, u32[]{:S(2)}) collective-permute-start(f32[1,6,64,128]{3,2,1,0:T(8,128)S(1)} %get-tuple-element.290), channel_id=1, source_target_pairs={{0,16},{16,32},{32,48},{48,64},{64,80},{80,96},{96,112},{112,0},{1... | collective-permute-start | bytes 589832 | tf_op jit(solution)/shard_map/ppermute | solution.py:23
  111.8 7.4 %collective-permute-start.5 = (f32[1,6,64,128]{3,2,1,0:T(8,128)S(1)}, f32[1,6,64,128]{3,2,1,0:T(8,128)S(1)}, u32[]{:S(2)}, u32[]{:S(2)}) collective-permute-start(f32[1,6,64,128]{3,2,1,0:T(8,128)S(1)} %get-tuple-element.291), channel_id=1, source_target_pairs={{16,0},{32,16},{48,32},{64,48},{80,64},{96,80},{112,96},{0,112},{1... | collective-permute-start | bytes 589832 | tf_op jit(solution)/shard_map/ppermute | solution.py:25
  119.9 8.0 %collective-permute-start.6 = (f32[8,1,64,128]{3,2,1,0:T(8,128)S(1)}, f32[8,1,64,128]{3,2,1,0:T(8,128)S(1)}, u32[]{:S(2)}, u32[]{:S(2)}) collective-permute-start(f32[8,1,64,128]{3,2,1,0:T(8,128)S(1)} %get-tuple-element.282), channel_id=1, source_target_pairs={{0,1},{1,2},{2,3},{3,4},{4,5},{5,6},{6,7},{7,8},{8,9},{9,10},{10,1... | collective-permute-start | bytes 786440 | tf_op jit(solution)/shard_map/ppermute | solution.py:23
  124.6 8.9 %collective-permute-start.7 = (f32[8,1,64,128]{3,2,1,0:T(8,128)S(1)}, f32[8,1,64,128]{3,2,1,0:T(8,128)}, u32[]{:S(2)}, u32[]{:S(2)}) collective-permute-start(f32[8,1,64,128]{3,2,1,0:T(8,128)S(1)} %get-tuple-element.283), channel_id=1, source_target_pairs={{1,0},{2,1},{3,2},{4,3},{5,4},{6,5},{7,6},{8,7},{9,8},{10,9},{11,1... | collective-permute-start | bytes 786440 | tf_op jit(solution)/shard_map/ppermute | solution.py:25
  137.9 4.1 %copy-start.9 = (f32[36,32,128]{2,1,0:T(8,128)S(1)}, f32[36,32,128]{2,1,0:T(8,128)}, u32[]{:S(2)}) copy-start(f32[36,32,128]{2,1,0:T(8,128)} %get-tuple-element.553) | copy-start | bytes 1769476 | tf_op jit(solution)/shard_map/while
  137.9 4.1 %copy-start.11 = (f32[36,32,128]{2,1,0:T(8,128)S(1)}, f32[36,32,128]{2,1,0:T(8,128)}, u32[]{:S(2)}) copy-start(f32[36,32,128]{2,1,0:T(8,128)} %get-tuple-element.554) | copy-start | bytes 1769476 | tf_op jit(solution)/shard_map/while
  182.7 4.1 %copy-start.9 = (f32[36,32,128]{2,1,0:T(8,128)S(1)}, f32[36,32,128]{2,1,0:T(8,128)}, u32[]{:S(2)}) copy-start(f32[36,32,128]{2,1,0:T(8,128)} %get-tuple-element.553) | copy-start | bytes 1769476 | tf_op jit(solution)/shard_map/while
  182.7 4.1 %copy-start.11 = (f32[36,32,128]{2,1,0:T(8,128)S(1)}, f32[36,32,128]{2,1,0:T(8,128)}, u32[]{:S(2)}) copy-start(f32[36,32,128]{2,1,0:T(8,128)} %get-tuple-element.554) | copy-start | bytes 1769476 | tf_op jit(solution)/shard_map/while
  198.8 27.0 %copy-start.15 = (f32[6,6,64,128]{3,2,1,0:T(8,128)}, f32[6,6,64,128]{3,2,1,0:T(8,128)S(1)}, u32[]{:S(2)}) copy-start(f32[6,6,64,128]{3,2,1,0:T(8,128)S(1)} %sub.47) | copy-start | bytes 3538948
  198.8 14.8 %collective-permute-start.8 = (f32[1,6,64,128]{3,2,1,0:T(8,128)S(1)}, f32[1,6,64,128]{3,2,1,0:T(8,128)S(1)}, u32[]{:S(2)}, u32[]{:S(2)}) collective-permute-start(f32[1,6,64,128]{3,2,1,0:T(8,128)S(1)} %get-tuple-element.288), channel_id=1, source_target_pairs={{0,16},{16,32},{32,48},{48,64},{64,80},{80,96},{96,112},{112,0},{1... | collective-permute-start | bytes 589832 | tf_op jit(solution)/shard_map/ppermute | solution.py:23
  206.4 8.1 %collective-permute-start.9 = (f32[1,6,64,128]{3,2,1,0:T(8,128)S(1)}, f32[1,6,64,128]{3,2,1,0:T(8,128)S(1)}, u32[]{:S(2)}, u32[]{:S(2)}) collective-permute-start(f32[1,6,64,128]{3,2,1,0:T(8,128)S(1)} %get-tuple-element.289), channel_id=1, source_target_pairs={{16,0},{32,16},{48,32},{64,48},{80,64},{96,80},{112,96},{0,112},{1... | collective-permute-start | bytes 589832 | tf_op jit(solution)/shard_map/ppermute | solution.py:25
  215.2 6.7 %collective-permute-start.10 = (f32[8,1,64,128]{3,2,1,0:T(8,128)S(1)}, f32[8,1,64,128]{3,2,1,0:T(8,128)S(1)}, u32[]{:S(2)}, u32[]{:S(2)}) collective-permute-start(f32[8,1,64,128]{3,2,1,0:T(8,128)S(1)} %get-tuple-element.280), channel_id=1, source_target_pairs={{0,1},{1,2},{2,3},{3,4},{4,5},{5,6},{6,7},{7,8},{8,9},{9,10},{10,1... | collective-permute-start | bytes 786440 | tf_op jit(solution)/shard_map/ppermute | solution.py:23
  217.4 8.4 %collective-permute-start.11 = (f32[8,1,64,128]{3,2,1,0:T(8,128)S(1)}, f32[8,1,64,128]{3,2,1,0:T(8,128)}, u32[]{:S(2)}, u32[]{:S(2)}) collective-permute-start(f32[8,1,64,128]{3,2,1,0:T(8,128)S(1)} %get-tuple-element.281), channel_id=1, source_target_pairs={{1,0},{2,1},{3,2},{4,3},{5,4},{6,5},{7,6},{8,7},{9,8},{10,9},{11,1... | collective-permute-start | bytes 786440 | tf_op jit(solution)/shard_map/ppermute | solution.py:25
  245.1 4.1 %copy-start = (f32[36,32,128]{2,1,0:T(8,128)S(1)}, f32[36,32,128]{2,1,0:T(8,128)}, u32[]{:S(2)}) copy-start(f32[36,32,128]{2,1,0:T(8,128)} %get-tuple-element.589) | copy-start | bytes 1769476 | tf_op jit(solution)/shard_map/while
  245.1 4.1 %copy-start.2 = (f32[36,32,128]{2,1,0:T(8,128)S(1)}, f32[36,32,128]{2,1,0:T(8,128)}, u32[]{:S(2)}) copy-start(f32[36,32,128]{2,1,0:T(8,128)} %get-tuple-element.590) | copy-start | bytes 1769476 | tf_op jit(solution)/shard_map/while
  274.9 4.1 %copy-start = (f32[36,32,128]{2,1,0:T(8,128)S(1)}, f32[36,32,128]{2,1,0:T(8,128)}, u32[]{:S(2)}) copy-start(f32[36,32,128]{2,1,0:T(8,128)} %get-tuple-element.589) | copy-start | bytes 1769476 | tf_op jit(solution)/shard_map/while
  (92 other events, 186.5 us)
where the time goes:
time: 338 us; the launch traced here: 337 us
  matrix products  96.2 us (28%)
  local copies, waits for them, and re-layouts  86.2 us (26%)
  blocking collectives  43.1 us (13%)
  starting transfers between devices  41.2 us (12%)
  waiting for transfers between devices  27.7 us (8%)
  other arithmetic  23.1 us (7%)
  loops' own time  18.9 us (6%)
    dot_general x24, matrix products, accumulate(): jnp.einsum('npb,nba->npa', piece, chosen, precision=lax.Precision.HIGHEST)  96.2 us
    psum x5, blocking collectives, over_axes(): return functools.reduce(lax.psum, axes, x)  43.1 us
    while x192, local copies, waits for them, and re-layouts  40 us
    ppermute x6, starting transfers between devices, with_halo(): lax.ppermute(tail, axis, [(i, (i + 1) % count) for i in range(count)])  28.1 us
    unnamed x36, local copies, waits for them, and re-layouts  22.5 us
    another operation x3, loops' own time, apply_hamiltonian(): lax.fori_loop(0, slot_bound, accumulate, (zeros, zeros))  18.9 us
    gather x24, local copies, waits for them, and re-layouts, accumulate(): piece = jnp.take(source, flat_partner[:, slot], axis=0)  15 us
    ppermute x6, waiting for transfers between devices, with_halo(): lax.ppermute(head, axis, [((i + 1) % count, i) for i in range(count)])  14.7 us
  transfers between devices with their start and end apart: 12, of which 10 were waited for; matrix products, arithmetic and copies ran while one was open for 6% of the time, Pallas kernels for 0%

commit v1 on v0

v1 whole, which is shorter than its diff:
```python
import math

import jax
import jax.numpy as jnp
from jax import lax
from jax.experimental import pallas as pl
from jax.experimental.pallas import tpu as pltpu
from jax.sharding import PartitionSpec as P

AXES = ("gx", "gy")
F32 = jnp.float32
BF16 = jnp.bfloat16
VMEM = pl.BlockSpec(memory_space=pltpu.VMEM)
SMEM = pl.BlockSpec(memory_space=pltpu.SMEM)


def split_kernel(sizes, shape, kpoint, partners, counts, source, out, turn, blocks, arrived):
    cells_x, cells_y = shape
    total_x, total_y = sizes[0] * cells_x, sizes[1] * cells_y
    cells, slots, block, _ = blocks.shape
    loads = [pltpu.make_async_copy(source.at[i], blocks.at[i], arrived.at[i]) for i in range(cells)]
    for load in loads:
        load.start()
    me_x, me_y = lax.axis_index("gx"), lax.axis_index("gy")

    reach = 20
    scale = -(-(1 << reach) // total_y)
    assert all(p * scale >> reach == p // total_y for p in range(total_x * total_y))

    def offset(place, start, total):
        step = place - start + 1
        return jnp.where(step < 0, step + total, jnp.where(step > 2, step - total, step))

    def body(i, carry):
        x, y = i // cells_y, i % cells_y
        pltpu.make_async_copy(source.at[i], blocks.at[i], arrived.at[i]).wait()
        live = counts[x, y]
        for s in range(slots):
            partner = partners[x, y, s]
            place_x = lax.shift_right_logical(partner * scale, reach)
            along_x = offset(place_x, me_x * cells_x + x, total_x)
            along_y = offset(partner - place_x * total_y, me_y * cells_y + y, total_y)
            row = pl.multiple_of((along_x * 3 + along_y) * block, block)
            value = jnp.where(s < live, blocks[i, s], 0.0)
            high = value.astype(BF16)
            out[i, pl.ds(row, block), 0:block] = high
            out[i, pl.ds(row, block), block : 2 * block] = (value - high.astype(F32)).astype(BF16)
        return carry

    lax.fori_loop(0, cells, body, 0)

    wrap_left = jnp.where(me_x == 0, -1.0, 0.0)
    wrap_right = jnp.where(me_x == sizes[0] - 1, 1.0, 0.0)
    wrap_low = jnp.where(me_y == 0, -1.0, 0.0)
    wrap_high = jnp.where(me_y == sizes[1] - 1, 1.0, 0.0)
    wrap_outer = jnp.where(me_y % 2 == 1, wrap_high, wrap_low)
    zero = jnp.zeros_like(wrap_outer)
    sides = [(wrap_left, zero), (wrap_right, zero), (zero, wrap_outer)]
    sides += [(wrap_left, wrap_outer), (wrap_right, wrap_outer)]
    for k, (along_x, along_y) in enumerate(sides):
        angle = jnp.full(turn.shape[1:], kpoint[0] * along_x + kpoint[1] * along_y, F32)
        turn[2 * k] = jnp.cos(angle)
        turn[2 * k + 1] = jnp.sin(angle)


def put(ext, x, y, value):
    rows, block = value.shape
    high = value.astype(BF16)
    lanes = pl.ds(pl.multiple_of(y * block, block), block)
    ext[x, 0:rows, lanes] = high
    ext[x, rows : 2 * rows, lanes] = (value - high.astype(F32)).astype(BF16)


def turned(value, cos, sin):
    half = value.shape[0] // 2
    re, im = value[:half], value[half:]
    return jnp.concatenate([cos * re - sin * im, sin * re + cos * im], axis=0)


def apply_cell(ext, blocks, x, y, cells_y):
    block = blocks.shape[2] // 2
    rows = ext.shape[1] // 2
    lanes = pl.ds(pl.multiple_of(y * block, block), 3 * block)
    left = jnp.concatenate([ext[x + d, :, lanes] for d in range(3)], axis=1)
    full = jnp.dot(left, blocks[x * cells_y + y], preferred_element_type=F32)
    return (full[rows:, block:] + full[rows:, :block]) + (full[:rows, block:] + full[:rows, :block])


def update(first, ext, blocks, probes, before, new, at, sums, x, y, cells_y):
    i = x * cells_y + y
    value = apply_cell(ext, blocks, x, y, cells_y)
    if not first:
        value = 2.0 * value - before[i]
    new[at(i)] = value
    half = value.shape[0] // 2
    start = probes[i]
    sums[0] += start[:half] * value[:half] + start[half:] * value[half:]
    sums[1] += start[:half] * value[half:] - start[half:] * value[:half]
    return value


def inner_kernel(first, shape, field, blocks, probes, before, new, sums, ext):
    cells_x, cells_y = shape
    for x in range(cells_x):
        for y in range(cells_y):
            put(ext, x + 1, y + 1, field[x * cells_y + y])
    sums[...] = jnp.zeros_like(sums)
    width = cells_y - 2

    def body(k, carry):
        update(
            first, ext, blocks, probes, before, new, lambda i: k, sums, 1 + k // width, 1 + k % width, cells_y
        )
        return carry

    lax.fori_loop(0, (cells_x - 2) * width, body, 0, unroll=4)


def rim_kernel(
    first, shape, turn, field, blocks, probes, before, inner, inner_sums,
    left, right, outer, low, high, close,
    new, sums, e_left, e_right, e_outer, e_low, e_high, e_close, ext,
):
    cells_x, cells_y = shape
    odd = lax.axis_index("gy") % 2
    y_outer, y_close = odd * (cells_y + 1), (1 - odd) * (cells_y + 1)
    for x in range(cells_x):
        for y in range(cells_y):
            put(ext, x + 1, y + 1, field[x * cells_y + y])
    for y in range(cells_y):
        put(ext, 0, y + 1, turned(left[y], turn[0], turn[1]))
        put(ext, cells_x + 1, y + 1, turned(right[y], turn[2], turn[3]))
    for x in range(cells_x):
        put(ext, x + 1, y_outer, turned(outer[x], turn[4], turn[5]))
        put(ext, x + 1, y_close, close[x])
    put(ext, 0, y_outer, turned(low[0], turn[6], turn[7]))
    put(ext, cells_x + 1, y_outer, turned(high[0], turn[8], turn[9]))
    put(ext, 0, y_close, turned(close[cells_x], turn[0], turn[1]))
    put(ext, cells_x + 1, y_close, turned(close[cells_x + 1], turn[2], turn[3]))
    sums[...] = inner_sums[...]
    width = cells_y - 2
    for k in range((cells_x - 2) * width):
        new[(1 + k // width) * cells_y + 1 + k % width] = inner[k]

    def body(k, carry):
        across = k < 2 * cells_y
        rest = k - 2 * cells_y
        x = jnp.where(across, (k // cells_y) * (cells_x - 1), 1 + rest // 2)
        y = jnp.where(across, k % cells_y, (rest % 2) * (cells_y - 1))
        update(first, ext, blocks, probes, before, new, lambda i: i, sums, x, y, cells_y)
        return carry

    lax.fori_loop(0, 2 * cells_y + 2 * (cells_x - 2), body, 0, unroll=5)
    edges(shape, odd, new, e_left, e_right, e_outer, e_low, e_high, e_close)


def edges(shape, odd, field, e_left, e_right, e_outer, e_low, e_high, e_close):
    cells_x, cells_y = shape
    last = (cells_x - 1) * cells_y
    c_outer, c_close = odd * (cells_y - 1), (1 - odd) * (cells_y - 1)
    for y in range(cells_y):
        e_left[y] = field[last + y]
        e_right[y] = field[y]
    for x in range(cells_x):
        e_outer[x] = field[x * cells_y + c_outer]
        e_close[x] = field[x * cells_y + c_close]
    e_low[0] = field[last + c_outer]
    e_high[0] = field[c_outer]


def edge_kernel(shape, field, *outs):
    edges(shape, lax.axis_index("gy") % 2, field, *outs)


def corner_kernel(left, right, outer, low, high, close, done, out):
    near = (1 - lax.axis_index("gy") % 2) * (left.shape[0] - 1)
    cells_x = close.shape[0]
    for x in range(cells_x):
        out[x] = close[x]
    out[cells_x] = left[near]
    out[cells_x + 1] = right[near]


def pack_kernel(scale, first, second, third, out):
    terms = jnp.concatenate([r[k] for r in (first, second, third) for k in range(2)], axis=0)
    ones = jnp.full((8, terms.shape[1]), scale, F32)
    row = lax.dot_general(
        ones, terms, (((1,), (1,)), ((), ())), precision=lax.Precision.HIGHEST, preferred_element_type=F32
    )
    lanes = out.shape[2]
    row = jnp.concatenate([row, jnp.zeros((8, 2 * lanes - row.shape[1]), F32)], axis=1)
    out[:, 0, :] = jnp.broadcast_to(row[0:1, :lanes], (out.shape[0], lanes))
    out[:, 1, :] = jnp.broadcast_to(row[0:1, lanes:], (out.shape[0], lanes))


def params(mib):
    return pltpu.CompilerParams(vmem_limit_bytes=mib << 20)


def shards(sizes, probes, pair_blocks, partners, shifts, counts, kpoint):
    size_x, size_y = sizes
    cells_x, cells_y, width, block = probes.shape
    shape = (cells_x, cells_y)
    slots = pair_blocks.shape[2]
    cells = cells_x * cells_y
    half = width // 2
    total_x, total_y = cells_x * size_x, cells_y * size_y
    def table(move):
        pairs = []
        for i in range(size_x):
            for j in range(size_y):
                a, b = move(i, j)
                pairs.append((i * size_y + j, (a % size_x) * size_y + b % size_y))
        return pairs

    def over(j):
        return j + 1 if j % 2 else j - 1

    moves = dict(
        left=table(lambda i, j: (i + 1, j)),
        right=table(lambda i, j: (i - 1, j)),
        outer=table(lambda i, j: (i, over(j))),
        low=table(lambda i, j: (i + 1, over(j))),
        high=table(lambda i, j: (i - 1, over(j))),
    )

    field = probes.reshape(cells, width, block)
    raw = pair_blocks.reshape(cells, slots, block, block)
    cell = (width, block)
    edge_shapes = [
        jax.ShapeDtypeStruct((n,) + cell, F32) for n in (cells_y, cells_y, cells_x, 1, 1, cells_x)
    ]
    field_shape = jax.ShapeDtypeStruct((cells,) + cell, F32)
    inner_shape = jax.ShapeDtypeStruct(((cells_x - 2) * (cells_y - 2),) + cell, F32)
    sums_shape = jax.ShapeDtypeStruct((2, half, block), F32)
    scratch = [pltpu.VMEM((cells_x + 2, 2 * width, (cells_y + 2) * block), BF16)]

    sides = pl.pallas_call(
        lambda *r: edge_kernel(shape, *r),
        out_shape=edge_shapes, in_specs=[VMEM], out_specs=[VMEM] * 6,
        compiler_params=params(1), name="edges",
    )(field)

    blocks, turn = pl.pallas_call(
        lambda *r: split_kernel(sizes, shape, *r),
        out_shape=[
            jax.ShapeDtypeStruct((cells, slots * block, 2 * block), BF16),
            jax.ShapeDtypeStruct((10, half, block), F32),
        ],
        in_specs=[SMEM, SMEM, SMEM, pl.BlockSpec(memory_space=pl.ANY)], out_specs=[VMEM] * 2,
        scratch_shapes=[pltpu.VMEM(raw.shape, F32), pltpu.SemaphoreType.DMA((cells,))],
        compiler_params=params(22), name="split",
        cost_estimate=pl.CostEstimate(flops=4 * raw.size, bytes_accessed=8 * raw.size, transcendentals=0),
    )(kpoint, partners, counts, pltpu.with_memory_space_constraint(raw, pltpu.HBM))

    flops = 8 * width * block * block * slots

    def step(first, field, before, sides):
        *sides, close = sides
        halo = [lax.ppermute(s, AXES, moves[n]) for n, s in zip(names, sides)]
        inner, inner_sums = pl.pallas_call(
            lambda *r: inner_kernel(first, shape, *r),
            out_shape=[inner_shape, sums_shape], in_specs=[VMEM] * 4, out_specs=[VMEM] * 2,
            scratch_shapes=scratch, compiler_params=params(6), name="inner",
            cost_estimate=pl.CostEstimate(flops=16 * flops, bytes_accessed=0, transcendentals=0),
        )(field, blocks, probes_flat, before)
        close = pl.pallas_call(
            corner_kernel, out_shape=jax.ShapeDtypeStruct((cells_x + 2,) + cell, F32),
            in_specs=[VMEM] * 7, out_specs=VMEM, compiler_params=params(1), name="corner",
        )(*halo, close, inner_sums)
        close = lax.ppermute(close, AXES, table(lambda i, j: (i, j ^ 1)))
        out = pl.pallas_call(
            lambda *r: rim_kernel(first, shape, *r),
            out_shape=[field_shape, sums_shape] + edge_shapes,
            in_specs=[VMEM] * 13, out_specs=[VMEM] * 8,
            scratch_shapes=scratch, compiler_params=params(8), name="rim",
            cost_estimate=pl.CostEstimate(flops=20 * flops, bytes_accessed=0, transcendentals=0),
        )(turn, field, blocks, probes_flat, before, inner, inner_sums,
          *halo, close)
        return out[0], out[1], out[2:]

    probes_flat = field
    names = ("left", "right", "outer", "low", "high")
    before, found = field, []
    for n in range(3):
        new, sums, sides = step(n == 0, field, before, sides)
        found.append(sums)
        before, field = field, new

    scale = 1.0 / math.sqrt(total_x * total_y * block)
    spread = pl.pallas_call(
        lambda *r: pack_kernel(scale, *r),
        out_shape=jax.ShapeDtypeStruct((size_x * size_y, 2, 128), F32),
        in_specs=[VMEM] * 3, out_specs=VMEM, compiler_params=params(2), name="pack",
    )(*found)
    total = jnp.sum(lax.all_to_all(spread, AXES, 0, 0), axis=0).reshape(-1)
    total = total[: 3 * 2 * half].reshape(3, 2, half)
    return field.reshape(probes.shape), total


def solution(mesh):
    sizes = (mesh.shape["gx"], mesh.shape["gy"])
    placed = (
        P("gx", "gy", None, None),
        P("gx", "gy", None, None, None),
        P("gx", "gy", None),
        P(None, "gx", "gy", None),
        P("gx", "gy"),
        P(),
    )
    return jax.shard_map(
        lambda *a: shards(sizes, *a), mesh=mesh, in_specs=placed,
        out_specs=(P("gx", "gy", None, None), P()), check_vma=False,
    )
```

time: 338 us -> 99.2 us (0.29)
  matrix products: 96.2 us -> 0 us
  local copies, waits for them, and re-layouts: 86.2 us -> 1.95 us
  Pallas kernels: 0 us -> 27.7 us
  blocking collectives: 43.1 us -> 16.4 us
  other arithmetic: 23.1 us -> 0.14 us
  waiting for transfers between devices: 27.7 us -> 7.55 us
  loops' own time: 18.9 us -> 0 us
    dot_general x24 -> x0, matrix products: 96.2 us -> none  [accumulate(): jnp.einsum('npb,nba->npa', piece, chosen, precision=lax.Precision.HIGHEST)]
    psum x5 -> x0, blocking collectives: 43.1 us -> none  [over_axes(): return functools.reduce(lax.psum, axes, x)]
    while x195 -> x0, local copies, waits for them, and re-layouts: 40.3 us -> none
    pallas_call x0 -> x12, Pallas kernels: none -> 27.7 us  [the longest x3 10.9 us: step(): pl.pallas_call(lambda *r: rim_kernel(first, shape, *r), out_shape=[field_...]
    unnamed x36 -> x10, local copies, waits for them, and re-layouts: 22.5 us -> 1.28 us
    ppermute x12 -> x18, waiting for transfers between devices: 27.7 us -> 7.55 us  [the longest x15 4.06 us: step(): halo = [lax.ppermute(s, AXES, moves[n]) for n, s in zip(names, sides)]]
    another operation x3 -> x0, loops' own time: 18.9 us -> none  [apply_hamiltonian(): lax.fori_loop(0, slot_bound, accumulate, (zeros, zeros))]
    all_to_all x0 -> x1, blocking collectives: none -> 16.4 us  [shards(): total = jnp.sum(lax.all_to_all(spread, AXES, 0, 0), axis=0).reshape(-1)]
  transfers between devices with their start and end apart: 12 -> 18, of which waited for: 10 -> 6; matrix products, arithmetic and copies ran while one was open for 6% -> 0% of each run, Pallas kernels for 0% -> 16%
where the time goes in v1:
time: 99.2 us; the launch traced here: 99 us
  starting transfers between devices  44.4 us (45%)
  Pallas kernels  27.7 us (28%)
  blocking collectives  16.4 us (17%)
  waiting for transfers between devices  7.55 us (8%)
  local copies, waits for them, and re-layouts  1.95 us (2%)
    ppermute x15, starting transfers between devices, step(): halo = [lax.ppermute(s, AXES, moves[n]) for n, s in zip(names, sides)]  34.9 us
    all_to_all x1, blocking collectives, shards(): total = jnp.sum(lax.all_to_all(spread, AXES, 0, 0), axis=0).reshape(-1)  16.4 us
    pallas_call x3, Pallas kernels, step(): pl.pallas_call(lambda *r: rim_kernel(first, shape, *r), out_shape=[field_...  10.9 us
    ppermute x3, starting transfers between devices, step(): close = lax.ppermute(close, AXES, table(lambda i, j: (i, j ^ 1)))  9.5 us
    pallas_call x1, Pallas kernels, shards(): pl.pallas_call(lambda *r: split_kernel(sizes, shape, *r), out_shape=[jax....  8.86 us
    pallas_call x3, Pallas kernels, step(): pl.pallas_call(lambda *r: inner_kernel(first, shape, *r), out_shape=[inne...  7.46 us
    ppermute x15, waiting for transfers between devices, step(): halo = [lax.ppermute(s, AXES, moves[n]) for n, s in zip(names, sides)]  4.06 us
    ppermute x3, waiting for transfers between devices, step(): close = lax.ppermute(close, AXES, table(lambda i, j: (i, j ^ 1)))  3.49 us
  transfers between devices with their start and end apart: 18, of which 6 were waited for; matrix products, arithmetic and copies ran while one was open for 0% of the time, Pallas kernels for 16%

profile of v1, /device:TPU:1, one launch (start us, length us, event | category | flops | bytes accessed | tf_op | source)
XLA Modules:
  0.0 99.0 jit_solution(9927128342564822014)
XLA Ops:
  0.7 1.3 %copy-done = f32[6,6,64,128]{3,2,1,0:T(8,128)S(1)} copy-done((f32[6,6,64,128]{3,2,1,0:T(8,128)S(1)}, f32[6,6,64,128]{3,2,1,0:T(8,128)}, u32[]{:S(2)}) %copy-start) | copy-done | bytes 1179672
  2.0 3.8 %collective-permute-start = (f32[6,64,128]{2,1,0:T(8,128)S(1)}, f32[6,64,128]{2,1,0:T(8,128)S(1)}, u32[]{:S(2)}, u32[]{:S(2)}) collective-permute-start(f32[6,64,128]{2,1,0:T(8,128)S(1)} %get-tuple-element.38), channel_id=1, source_target_pairs={{0,16},{1,17},{2,18},{3,19},{4,20},{5,21},{6,22},{7,23},{8,24},{9,... | collective-permute-start | bytes 589832 | tf_op jit(solution)/shard_map/ppermute | solution.py:260
  5.8 2.3 %collective-permute-start.1 = (f32[6,64,128]{2,1,0:T(8,128)S(1)}, f32[6,64,128]{2,1,0:T(8,128)S(1)}, u32[]{:S(2)}, u32[]{:S(2)}) collective-permute-start(f32[6,64,128]{2,1,0:T(8,128)S(1)} %get-tuple-element.39), channel_id=1, source_target_pairs={{0,112},{1,113},{2,114},{3,115},{4,116},{5,117},{6,118},{7,119},{8... | collective-permute-start | bytes 589832 | tf_op jit(solution)/shard_map/ppermute | solution.py:260
  8.1 2.3 %collective-permute-start.2 = (f32[6,64,128]{2,1,0:T(8,128)S(1)}, f32[6,64,128]{2,1,0:T(8,128)S(1)}, u32[]{:S(2)}, u32[]{:S(2)}) collective-permute-start(f32[6,64,128]{2,1,0:T(8,128)S(1)} %get-tuple-element.40), channel_id=1, source_target_pairs={{0,15},{1,2},{2,1},{3,4},{4,3},{5,6},{6,5},{7,8},{8,7},{9,10},{10,... | collective-permute-start | bytes 589832 | tf_op jit(solution)/shard_map/ppermute | solution.py:260
  10.4 5.1 %collective-permute-start.4 = (f32[1,64,128]{2,1,0:T(8,128)S(1)}, f32[1,64,128]{2,1,0:T(8,128)S(1)}, u32[]{:S(2)}, u32[]{:S(2)}) collective-permute-start(f32[1,64,128]{2,1,0:T(8,128)S(1)} %get-tuple-element.42), channel_id=1, source_target_pairs={{0,127},{1,114},{2,113},{3,116},{4,115},{5,118},{6,117},{7,120},{8... | collective-permute-start | bytes 98312 | tf_op jit(solution)/shard_map/ppermute | solution.py:260
  15.5 8.9 %split.1 = (bf16[36,1152,256]{2,1,0:T(8,128)(2,1)S(1)}, f32[10,32,128]{2,1,0:T(8,128)S(1)}) custom-call(f32[2]{0:T(128)S(1)} %copy-done.4, s32[6,6,9]{2,1,0:T(8,128)S(1)} %copy-done.2, s32[6,6]{1,0:T(8,128)S(1)} %copy-done.3, f32[36,9,128,128]{3,2,1,0:T(8,128)} %bitcast.16), custom_call_target="tpu_custom_call" | custom-call | flops 21233664 | bytes 42467328 | tf_op jit(solution)/shard_map/split/pallas_call | solution.py:244
  24.3 2.5 %inner.3 = (f32[16,64,128]{2,1,0:T(8,128)S(1)}, f32[2,32,128]{2,1,0:T(8,128)S(1)}) custom-call(f32[36,64,128]{2,1,0:T(8,128)S(1)} %bitcast.4, bf16[36,1152,256]{2,1,0:T(8,128)(2,1)S(1)} %get-tuple-element.35.r_1_.r_2_, f32[36,64,128]{2,1,0:T(8,128)S(1)} %bitcast.5, f32[36,64,128]{2,1,0:T(8,128)S(1)} %bitcast.6), custom_call_target="tpu_custom_call" | custom-call | flops 1207959552 | tf_op jit(solution)/shard_map/inner/pallas_call | solution.py:261
  26.9 4.9 %collective-permute-start.5 = (f32[8,64,128]{2,1,0:T(8,128)S(1)}, f32[8,64,128]{2,1,0:T(8,128)S(1)}, u32[]{:S(2)}, u32[]{:S(2)}) collective-permute-start(f32[8,64,128]{2,1,0:T(8,128)S(1)} %corner.3), channel_id=1, source_target_pairs={{0,1},{1,0},{2,3},{3,2},{4,5},{5,4},{6,7},{7,6},{8,9},{9,8},{10,11... | collective-permute-start | bytes 786440 | tf_op jit(solution)/shard_map/ppermute | solution.py:271
  31.8 1.2 %collective-permute-done.5.r_12_ = f32[8,64,128]{2,1,0:T(8,128)S(1)} collective-permute-done((f32[8,64,128]{2,1,0:T(8,128)S(1)}, f32[8,64,128]{2,1,0:T(8,128)S(1)}, u32[]{:S(2)}, u32[]{:S(2)}) %collective-permute-start.5) | collective-permute-done | bytes 262176 | tf_op jit(solution)/shard_map/ppermute | solution.py:271
  33.0 3.2 %rim.3 = (f32[36,64,128]{2,1,0:T(8,128)S(1)}, f32[2,32,128]{2,1,0:T(8,128)S(1)}, f32[6,64,128]{2,1,0:T(8,128)S(1)}, f32[6,64,128]{2,1,0:T(8,128)S(1)}, f32[6,64,...) custom-call(f32[10,32,128]{2,1,0:T(8,128)S(1)} %get-tuple-element.34.r_0_, ...), custom_call_target="tpu_custom_call" | custom-call | flops 1509949440 | tf_op jit(solution)/shard_map/rim/pallas_call | solution.py:272
  36.3 5.1 %collective-permute-start.7 = (f32[6,64,128]{2,1,0:T(8,128)S(1)}, f32[6,64,128]{2,1,0:T(8,128)S(1)}, u32[]{:S(2)}, u32[]{:S(2)}) collective-permute-start(f32[6,64,128]{2,1,0:T(8,128)S(1)} %get-tuple-element.48), channel_id=1, source_target_pairs={{0,112},{1,113},{2,114},{3,115},{4,116},{5,117},{6,118},{7,119},{8... | collective-permute-start | bytes 589832 | tf_op jit(solution)/shard_map/ppermute | solution.py:260
  41.4 5.1 %collective-permute-start.10 = (f32[1,64,128]{2,1,0:T(8,128)S(1)}, f32[1,64,128]{2,1,0:T(8,128)S(1)}, u32[]{:S(2)}, u32[]{:S(2)}) collective-permute-start(f32[1,64,128]{2,1,0:T(8,128)S(1)} %get-tuple-element.51), channel_id=1, source_target_pairs={{0,127},{1,114},{2,113},{3,116},{4,115},{5,118},{6,117},{7,120},{8... | collective-permute-start | bytes 98312 | tf_op jit(solution)/shard_map/ppermute | solution.py:260
  46.4 2.5 %inner.4 = (f32[16,64,128]{2,1,0:T(8,128)S(1)}, f32[2,32,128]{2,1,0:T(8,128)S(1)}) custom-call(f32[36,64,128]{2,1,0:T(8,128)S(1)} %get-tuple-element.44.r_0_.r_1_.r_3_.r_4_, bf16[36,1152,256]{2,1,0:T(8,128)(2,1)S(1)} %get-tuple-element.35.r_1_.r_2_, f32[36,64,128]{2,1,0:T(8,128)S(1)} %bitcast.10, f32[36,64,128]{2,1,0:T(8,128)S(1)} %bitcast.11), custom_call_target="tpu_custom_call" | custom-call | flops 1207959552 | tf_op jit(solution)/shard_map/inner/pallas_call | solution.py:261
  48.9 1.5 %collective-permute-done.10.high.r_11_ = f32[1,64,128]{2,1,0:T(8,128)S(1)} collective-permute-done((f32[1,64,128]{2,1,0:T(8,128)S(1)}, f32[1,64,128]{2,1,0:T(8,128)S(1)}, u32[]{:S(2)}, u32[]{:S(2)}) %collective-permute-start.10) | collective-permute-done | bytes 32800 | tf_op jit(solution)/shard_map/ppermute | solution.py:260
  50.4 1.7 %collective-permute-start.11 = (f32[8,64,128]{2,1,0:T(8,128)S(1)}, f32[8,64,128]{2,1,0:T(8,128)S(1)}, u32[]{:S(2)}, u32[]{:S(2)}) collective-permute-start(f32[8,64,128]{2,1,0:T(8,128)S(1)} %corner.4), channel_id=1, source_target_pairs={{0,1},{1,0},{2,3},{3,2},{4,5},{5,4},{6,7},{7,6},{8,9},{9,8},{10,11... | collective-permute-start | bytes 786440 | tf_op jit(solution)/shard_map/ppermute | solution.py:271
  52.1 1.2 %collective-permute-done.11.r_12_ = f32[8,64,128]{2,1,0:T(8,128)S(1)} collective-permute-done((f32[8,64,128]{2,1,0:T(8,128)S(1)}, f32[8,64,128]{2,1,0:T(8,128)S(1)}, u32[]{:S(2)}, u32[]{:S(2)}) %collective-permute-start.11) | collective-permute-done | bytes 262176 | tf_op jit(solution)/shard_map/ppermute | solution.py:271
  53.3 3.2 %rim.4 = (f32[36,64,128]{2,1,0:T(8,128)S(1)}, f32[2,32,128]{2,1,0:T(8,128)S(1)}, f32[6,64,128]{2,1,0:T(8,128)S(1)}, f32[6,64,128]{2,1,0:T(8,128)S(1)}, f32[6,64,...) custom-call(f32[10,32,128]{2,1,0:T(8,128)S(1)} %get-tuple-element.34.r_0_, ...), custom_call_target="tpu_custom_call" | custom-call | flops 1509949440 | tf_op jit(solution)/shard_map/rim/pallas_call | solution.py:272
  56.5 1.3 %collective-permute-start.12 = (f32[6,64,128]{2,1,0:T(8,128)S(1)}, f32[6,64,128]{2,1,0:T(8,128)S(1)}, u32[]{:S(2)}, u32[]{:S(2)}) collective-permute-start(f32[6,64,128]{2,1,0:T(8,128)S(1)} %get-tuple-element.56), channel_id=1, source_target_pairs={{0,16},{1,17},{2,18},{3,19},{4,20},{5,21},{6,22},{7,23},{8,24},{9,... | collective-permute-start | bytes 589832 | tf_op jit(solution)/shard_map/ppermute | solution.py:260
  57.8 4.4 %collective-permute-start.13 = (f32[6,64,128]{2,1,0:T(8,128)S(1)}, f32[6,64,128]{2,1,0:T(8,128)S(1)}, u32[]{:S(2)}, u32[]{:S(2)}) collective-permute-start(f32[6,64,128]{2,1,0:T(8,128)S(1)} %get-tuple-element.57), channel_id=1, source_target_pairs={{0,112},{1,113},{2,114},{3,115},{4,116},{5,117},{6,118},{7,119},{8... | collective-permute-start | bytes 589832 | tf_op jit(solution)/shard_map/ppermute | solution.py:260
  62.3 0.5 collective-permute-start.14
  62.8 5.1 %collective-permute-start.16 = (f32[1,64,128]{2,1,0:T(8,128)S(1)}, f32[1,64,128]{2,1,0:T(8,128)S(1)}, u32[]{:S(2)}, u32[]{:S(2)}) collective-permute-start(f32[1,64,128]{2,1,0:T(8,128)S(1)} %get-tuple-element.60), channel_id=1, source_target_pairs={{0,127},{1,114},{2,113},{3,116},{4,115},{5,118},{6,117},{7,120},{8... | collective-permute-start | bytes 98312 | tf_op jit(solution)/shard_map/ppermute | solution.py:260
  67.8 2.5 %inner.5 = (f32[16,64,128]{2,1,0:T(8,128)S(1)}, f32[2,32,128]{2,1,0:T(8,128)S(1)}) custom-call(f32[36,64,128]{2,1,0:T(8,128)S(1)} %get-tuple-element.53.r_0_.r_1_, bf16[36,1152,256]{2,1,0:T(8,128)(2,1)S(1)} %get-tuple-element.35.r_1_.r_2_, f32[36,64,128]{2,1,0:T(8,128)S(1)} %bitcast.14, f32[36,64,128]{2,1,0:T(8,128)S(1)} %get-tuple-element.44.r_0_.r_1_.r_3_.r_4_), custom_call_target="tpu_custom_call" | custom-call | flops 1207959552 | tf_op jit(solution)/shard_map/inner/pallas_call | solution.py:261
  70.3 1.6 %collective-permute-done.16.high.r_11_ = f32[1,64,128]{2,1,0:T(8,128)S(1)} collective-permute-done((f32[1,64,128]{2,1,0:T(8,128)S(1)}, f32[1,64,128]{2,1,0:T(8,128)S(1)}, u32[]{:S(2)}, u32[]{:S(2)}) %collective-permute-start.16) | collective-permute-done | bytes 32800 | tf_op jit(solution)/shard_map/ppermute | solution.py:260
  71.9 1.0 %collective-permute-done.14.outer.r_9_ = f32[6,64,128]{2,1,0:T(8,128)S(1)} collective-permute-done((f32[6,64,128]{2,1,0:T(8,128)S(1)}, f32[6,64,128]{2,1,0:T(8,128)S(1)}, u32[]{:S(2)}, u32[]{:S(2)}) %collective-permute-start.14) | collective-permute-done | bytes 196640 | tf_op jit(solution)/shard_map/ppermute | solution.py:260
  72.9 2.9 %collective-permute-start.17 = (f32[8,64,128]{2,1,0:T(8,128)S(1)}, f32[8,64,128]{2,1,0:T(8,128)S(1)}, u32[]{:S(2)}, u32[]{:S(2)}) collective-permute-start(f32[8,64,128]{2,1,0:T(8,128)S(1)} %corner.5), channel_id=1, source_target_pairs={{0,1},{1,0},{2,3},{3,2},{4,5},{5,4},{6,7},{7,6},{8,9},{9,8},{10,11... | collective-permute-start | bytes 786440 | tf_op jit(solution)/shard_map/ppermute | solution.py:271
  75.8 1.2 %collective-permute-done.17.r_12_ = f32[8,64,128]{2,1,0:T(8,128)S(1)} collective-permute-done((f32[8,64,128]{2,1,0:T(8,128)S(1)}, f32[8,64,128]{2,1,0:T(8,128)S(1)}, u32[]{:S(2)}, u32[]{:S(2)}) %collective-permute-start.17) | collective-permute-done | bytes 262176 | tf_op jit(solution)/shard_map/ppermute | solution.py:271
  77.0 4.5 %rim.5 = (f32[36,64,128]{2,1,0:T(8,128)}, f32[2,32,128]{2,1,0:T(8,128)S(1)}, f32[6,64,128]{2,1,0:T(8,128)}, f32[6,64,128]{2,1,0:T(8,128)}, f32[6,64,128]{2,1,0:T...) custom-call(f32[10,32,128]{2,1,0:T(8,128)S(1)} %get-tuple-element.34.r_0_, ...), custom_call_target="tpu_custom_call" | custom-call | flops 1509949440 | tf_op jit(solution)/shard_map/rim/pallas_call | solution.py:272
  81.4 0.3 pack.1
  81.8 16.4 %all_to_all.5 = f32[128,2,128]{2,1,0:T(2,128)S(1)} all-to-all(f32[128,2,128]{2,1,0:T(2,128)S(1)} %pack.1), channel_id=1, replica_groups=mesh['gx'=8,'gy'=16] {'gx','gy'}, dimensions={0} | all-to-all | bytes 262144 | tf_op jit(solution)/shard_map/all_to_all | solution.py:296
  98.2 0.1 reduce_sum.9
  98.3 0.1 slice.6
  98.4 0.6 slice.8
  (30 shorter events, 0.3 us)
Async XLA Ops:
  0.6 14.8 %copy-start.4 = (f32[2]{0:T(128)S(1)}, f32[2]{0:T(128)}, u32[]{:S(2)}) copy-start(f32[2]{0:T(128)} %r_0_.1) | copy-start | bytes 28
  0.6 1.3 %copy-start = (f32[6,6,64,128]{3,2,1,0:T(8,128)S(1)}, f32[6,6,64,128]{3,2,1,0:T(8,128)}, u32[]{:S(2)}) copy-start(f32[6,6,64,128]{3,2,1,0:T(8,128)} %param.6) | copy-start | bytes 3538948
  1.9 13.5 %copy-start.2 = (s32[6,6,9]{2,1,0:T(8,128)S(1)}, s32[6,6,9]{2,1,0:T(8,128)}, u32[]{:S(2)}) copy-start(s32[6,6,9]{2,1,0:T(8,128)} %r_1_.1) | copy-start | bytes 3892
  1.9 13.5 %copy-start.3 = (s32[6,6]{1,0:T(8,128)S(1)}, s32[6,6]{1,0:T(8,128)}, u32[]{:S(2)}) copy-start(s32[6,6]{1,0:T(8,128)} %r_2_.1) | copy-start | bytes 436
  2.0 24.9 %collective-permute-start = (f32[6,64,128]{2,1,0:T(8,128)S(1)}, f32[6,64,128]{2,1,0:T(8,128)S(1)}, u32[]{:S(2)}, u32[]{:S(2)}) collective-permute-start(f32[6,64,128]{2,1,0:T(8,128)S(1)} %get-tuple-element.38), channel_id=1, source_target_pairs={{0,16},{1,17},{2,18},{3,19},{4,20},{5,21},{6,22},{7,23},{8,24},{9,... | collective-permute-start | bytes 589832 | tf_op jit(solution)/shard_map/ppermute | solution.py:260
  5.8 21.1 %collective-permute-start.1 = (f32[6,64,128]{2,1,0:T(8,128)S(1)}, f32[6,64,128]{2,1,0:T(8,128)S(1)}, u32[]{:S(2)}, u32[]{:S(2)}) collective-permute-start(f32[6,64,128]{2,1,0:T(8,128)S(1)} %get-tuple-element.39), channel_id=1, source_target_pairs={{0,112},{1,113},{2,114},{3,115},{4,116},{5,117},{6,118},{7,119},{8... | collective-permute-start | bytes 589832 | tf_op jit(solution)/shard_map/ppermute | solution.py:260
  8.1 18.8 %collective-permute-start.2 = (f32[6,64,128]{2,1,0:T(8,128)S(1)}, f32[6,64,128]{2,1,0:T(8,128)S(1)}, u32[]{:S(2)}, u32[]{:S(2)}) collective-permute-start(f32[6,64,128]{2,1,0:T(8,128)S(1)} %get-tuple-element.40), channel_id=1, source_target_pairs={{0,15},{1,2},{2,1},{3,4},{4,3},{5,6},{6,5},{7,8},{8,7},{9,10},{10,... | collective-permute-start | bytes 589832 | tf_op jit(solution)/shard_map/ppermute | solution.py:260
  10.4 16.4 %collective-permute-start.3 = (f32[1,64,128]{2,1,0:T(8,128)S(1)}, f32[1,64,128]{2,1,0:T(8,128)S(1)}, u32[]{:S(2)}, u32[]{:S(2)}) collective-permute-start(f32[1,64,128]{2,1,0:T(8,128)S(1)} %get-tuple-element.41), channel_id=1, source_target_pairs={{0,31},{1,18},{2,17},{3,20},{4,19},{5,22},{6,21},{7,24},{8,23},{9,... | collective-permute-start | bytes 98312 | tf_op jit(solution)/shard_map/ppermute | solution.py:260
  10.4 16.4 %collective-permute-start.4 = (f32[1,64,128]{2,1,0:T(8,128)S(1)}, f32[1,64,128]{2,1,0:T(8,128)S(1)}, u32[]{:S(2)}, u32[]{:S(2)}) collective-permute-start(f32[1,64,128]{2,1,0:T(8,128)S(1)} %get-tuple-element.42), channel_id=1, source_target_pairs={{0,127},{1,114},{2,113},{3,116},{4,115},{5,118},{6,117},{7,120},{8... | collective-permute-start | bytes 98312 | tf_op jit(solution)/shard_map/ppermute | solution.py:260
  15.5 8.9 %copy-start.1 = (f32[6,6,64,128]{3,2,1,0:T(8,128)S(1)}, f32[6,6,64,128]{3,2,1,0:T(8,128)}, u32[]{:S(2)}) copy-start(f32[6,6,64,128]{3,2,1,0:T(8,128)} %param.6) | copy-start | bytes 3538948
  26.9 6.1 %collective-permute-start.5 = (f32[8,64,128]{2,1,0:T(8,128)S(1)}, f32[8,64,128]{2,1,0:T(8,128)S(1)}, u32[]{:S(2)}, u32[]{:S(2)}) collective-permute-start(f32[8,64,128]{2,1,0:T(8,128)S(1)} %corner.3), channel_id=1, source_target_pairs={{0,1},{1,0},{2,3},{3,2},{4,5},{5,4},{6,7},{7,6},{8,9},{9,8},{10,11... | collective-permute-start | bytes 786440 | tf_op jit(solution)/shard_map/ppermute | solution.py:271
  36.2 14.2 %collective-permute-start.6 = (f32[6,64,128]{2,1,0:T(8,128)S(1)}, f32[6,64,128]{2,1,0:T(8,128)S(1)}, u32[]{:S(2)}, u32[]{:S(2)}) collective-permute-start(f32[6,64,128]{2,1,0:T(8,128)S(1)} %get-tuple-element.47), channel_id=1, source_target_pairs={{0,16},{1,17},{2,18},{3,19},{4,20},{5,21},{6,22},{7,23},{8,24},{9,... | collective-permute-start | bytes 589832 | tf_op jit(solution)/shard_map/ppermute | solution.py:260
  36.3 14.1 %collective-permute-start.7 = (f32[6,64,128]{2,1,0:T(8,128)S(1)}, f32[6,64,128]{2,1,0:T(8,128)S(1)}, u32[]{:S(2)}, u32[]{:S(2)}) collective-permute-start(f32[6,64,128]{2,1,0:T(8,128)S(1)} %get-tuple-element.48), channel_id=1, source_target_pairs={{0,112},{1,113},{2,114},{3,115},{4,116},{5,117},{6,118},{7,119},{8... | collective-permute-start | bytes 589832 | tf_op jit(solution)/shard_map/ppermute | solution.py:260
  41.4 9.1 %collective-permute-start.8 = (f32[6,64,128]{2,1,0:T(8,128)S(1)}, f32[6,64,128]{2,1,0:T(8,128)S(1)}, u32[]{:S(2)}, u32[]{:S(2)}) collective-permute-start(f32[6,64,128]{2,1,0:T(8,128)S(1)} %get-tuple-element.49), channel_id=1, source_target_pairs={{0,15},{1,2},{2,1},{3,4},{4,3},{5,6},{6,5},{7,8},{8,7},{9,10},{10,... | collective-permute-start | bytes 589832 | tf_op jit(solution)/shard_map/ppermute | solution.py:260
  41.4 7.6 %collective-permute-start.9 = (f32[1,64,128]{2,1,0:T(8,128)S(1)}, f32[1,64,128]{2,1,0:T(8,128)S(1)}, u32[]{:S(2)}, u32[]{:S(2)}) collective-permute-start(f32[1,64,128]{2,1,0:T(8,128)S(1)} %get-tuple-element.50), channel_id=1, source_target_pairs={{0,31},{1,18},{2,17},{3,20},{4,19},{5,22},{6,21},{7,24},{8,23},{9,... | collective-permute-start | bytes 98312 | tf_op jit(solution)/shard_map/ppermute | solution.py:260
  41.4 9.0 %collective-permute-start.10 = (f32[1,64,128]{2,1,0:T(8,128)S(1)}, f32[1,64,128]{2,1,0:T(8,128)S(1)}, u32[]{:S(2)}, u32[]{:S(2)}) collective-permute-start(f32[1,64,128]{2,1,0:T(8,128)S(1)} %get-tuple-element.51), channel_id=1, source_target_pairs={{0,127},{1,114},{2,113},{3,116},{4,115},{5,118},{6,117},{7,120},{8... | collective-permute-start | bytes 98312 | tf_op jit(solution)/shard_map/ppermute | solution.py:260
  50.4 2.9 %collective-permute-start.11 = (f32[8,64,128]{2,1,0:T(8,128)S(1)}, f32[8,64,128]{2,1,0:T(8,128)S(1)}, u32[]{:S(2)}, u32[]{:S(2)}) collective-permute-start(f32[8,64,128]{2,1,0:T(8,128)S(1)} %corner.4), channel_id=1, source_target_pairs={{0,1},{1,0},{2,3},{3,2},{4,5},{5,4},{6,7},{7,6},{8,9},{9,8},{10,11... | collective-permute-start | bytes 786440 | tf_op jit(solution)/shard_map/ppermute | solution.py:271
  56.5 15.4 %collective-permute-start.12 = (f32[6,64,128]{2,1,0:T(8,128)S(1)}, f32[6,64,128]{2,1,0:T(8,128)S(1)}, u32[]{:S(2)}, u32[]{:S(2)}) collective-permute-start(f32[6,64,128]{2,1,0:T(8,128)S(1)} %get-tuple-element.56), channel_id=1, source_target_pairs={{0,16},{1,17},{2,18},{3,19},{4,20},{5,21},{6,22},{7,23},{8,24},{9,... | collective-permute-start | bytes 589832 | tf_op jit(solution)/shard_map/ppermute | solution.py:260
  57.8 14.1 %collective-permute-start.13 = (f32[6,64,128]{2,1,0:T(8,128)S(1)}, f32[6,64,128]{2,1,0:T(8,128)S(1)}, u32[]{:S(2)}, u32[]{:S(2)}) collective-permute-start(f32[6,64,128]{2,1,0:T(8,128)S(1)} %get-tuple-element.57), channel_id=1, source_target_pairs={{0,112},{1,113},{2,114},{3,115},{4,116},{5,117},{6,118},{7,119},{8... | collective-permute-start | bytes 589832 | tf_op jit(solution)/shard_map/ppermute | solution.py:260
  62.3 10.6 %collective-permute-start.14 = (f32[6,64,128]{2,1,0:T(8,128)S(1)}, f32[6,64,128]{2,1,0:T(8,128)S(1)}, u32[]{:S(2)}, u32[]{:S(2)}) collective-permute-start(f32[6,64,128]{2,1,0:T(8,128)S(1)} %get-tuple-element.58), channel_id=1, source_target_pairs={{0,15},{1,2},{2,1},{3,4},{4,3},{5,6},{6,5},{7,8},{8,7},{9,10},{10,... | collective-permute-start | bytes 589832 | tf_op jit(solution)/shard_map/ppermute | solution.py:260
  62.8 7.6 %collective-permute-start.15 = (f32[1,64,128]{2,1,0:T(8,128)S(1)}, f32[1,64,128]{2,1,0:T(8,128)S(1)}, u32[]{:S(2)}, u32[]{:S(2)}) collective-permute-start(f32[1,64,128]{2,1,0:T(8,128)S(1)} %get-tuple-element.59), channel_id=1, source_target_pairs={{0,31},{1,18},{2,17},{3,20},{4,19},{5,22},{6,21},{7,24},{8,23},{9,... | collective-permute-start | bytes 98312 | tf_op jit(solution)/shard_map/ppermute | solution.py:260
  62.8 9.1 %collective-permute-start.16 = (f32[1,64,128]{2,1,0:T(8,128)S(1)}, f32[1,64,128]{2,1,0:T(8,128)S(1)}, u32[]{:S(2)}, u32[]{:S(2)}) collective-permute-start(f32[1,64,128]{2,1,0:T(8,128)S(1)} %get-tuple-element.60), channel_id=1, source_target_pairs={{0,127},{1,114},{2,113},{3,116},{4,115},{5,118},{6,117},{7,120},{8... | collective-permute-start | bytes 98312 | tf_op jit(solution)/shard_map/ppermute | solution.py:260
  72.9 4.0 %collective-permute-start.17 = (f32[8,64,128]{2,1,0:T(8,128)S(1)}, f32[8,64,128]{2,1,0:T(8,128)S(1)}, u32[]{:S(2)}, u32[]{:S(2)}) collective-permute-start(f32[8,64,128]{2,1,0:T(8,128)S(1)} %corner.5), channel_id=1, source_target_pairs={{0,1},{1,0},{2,3},{3,2},{4,5},{5,4},{6,7},{7,6},{8,9},{9,8},{10,11... | collective-permute-start | bytes 786440 | tf_op jit(solution)/shard_map/ppermute | solution.py:271

commit v2 on v1

--- a/solution.py
+++ b/solution.py
@@ -77,81 +77,119 @@
     return jnp.concatenate([cos * re - sin * im, sin * re + cos * im], axis=0)
 
 
+def fold(full, rows, block):
+    return (full[rows:, block:] + full[rows:, :block]) + (full[:rows, block:] + full[:rows, :block])
+
+
 def apply_cell(ext, blocks, x, y, cells_y):
     block = blocks.shape[2] // 2
-    rows = ext.shape[1] // 2
     lanes = pl.ds(pl.multiple_of(y * block, block), 3 * block)
     left = jnp.concatenate([ext[x + d, :, lanes] for d in range(3)], axis=1)
     full = jnp.dot(left, blocks[x * cells_y + y], preferred_element_type=F32)
-    return (full[rows:, block:] + full[rows:, :block]) + (full[:rows, block:] + full[:rows, :block])
-
-
-def update(first, ext, blocks, probes, before, new, at, sums, x, y, cells_y):
-    i = x * cells_y + y
-    value = apply_cell(ext, blocks, x, y, cells_y)
-    if not first:
-        value = 2.0 * value - before[i]
-    new[at(i)] = value
+    return fold(full, ext.shape[1] // 2, block)
+
+
+def apply_part(ext, blocks, x, y, shape, local):
+    cells_x, cells_y = shape
+    block = blocks.shape[2] // 2
+    left, right = [], []
+    for k in range(9):
+        a, b = x + k // 3, y + k % 3
+        if (1 <= a <= cells_x and 1 <= b <= cells_y) == local:
+            left.append(ext[a, :, b * block : (b + 1) * block])
+            right.append(blocks[x * cells_y + y, k * block : (k + 1) * block, :])
+    full = jnp.dot(
+        jnp.concatenate(left, axis=1), jnp.concatenate(right, axis=0), preferred_element_type=F32
+    )
+    return fold(full, ext.shape[1] // 2, block)
+
+
+def rim_cells(shape):
+    cells_x, cells_y = shape
+    return [
+        (x, y) for x in range(cells_x) for y in range(cells_y)
+        if x in (0, cells_x - 1) or y in (0, cells_y - 1)
+    ]
+
+
+def terms(start, value):
     half = value.shape[0] // 2
-    start = probes[i]
-    sums[0] += start[:half] * value[:half] + start[half:] * value[half:]
-    sums[1] += start[:half] * value[half:] - start[half:] * value[:half]
-    return value
-
-
-def inner_kernel(first, shape, field, blocks, probes, before, new, sums, ext):
+    real = start[:half] * value[:half] + start[half:] * value[half:]
+    return real, start[:half] * value[half:] - start[half:] * value[:half]
+
+
+def put_field(ext, field, shape):
     cells_x, cells_y = shape
     for x in range(cells_x):
         for y in range(cells_y):
             put(ext, x + 1, y + 1, field[x * cells_y + y])
+
+
+def inner_kernel(first, shape, field, blocks, probes, before, done, out, sums, ext):
+    cells_x, cells_y = shape
+    put_field(ext, field, shape)
     sums[...] = jnp.zeros_like(sums)
     width = cells_y - 2
 
     def body(k, carry):
-        update(
-            first, ext, blocks, probes, before, new, lambda i: k, sums, 1 + k // width, 1 + k % width, cells_y
-        )
+        x, y = 1 + k // width, 1 + k % width
+        i = x * cells_y + y
+        value = apply_cell(ext, blocks, x, y, cells_y)
+        if not first:
+            value = 2.0 * value - before[i]
+        out[k] = value
+        real, imag = terms(probes[i], value)
+        sums[0] += real
+        sums[1] += imag
         return carry
 
     lax.fori_loop(0, (cells_x - 2) * width, body, 0, unroll=4)
 
 
+def local_kernel(shape, field, blocks, done, out, ext):
+    put_field(ext, field, shape)
+    for k, (x, y) in enumerate(rim_cells(shape)):
+        out[k] = apply_part(ext, blocks, x, y, shape, True)
+
+
 def rim_kernel(
-    first, shape, turn, field, blocks, probes, before, inner, inner_sums,
-    left, right, outer, low, high, close,
-    new, sums, e_left, e_right, e_outer, e_low, e_high, e_close, ext,
+    first, shape, turn, blocks, probes, before, inner, inner_sums, local, left, right, outer, close, *rest
 ):
     cells_x, cells_y = shape
+    if first:
+        low, high = outer.at[cells_x], outer.at[cells_x + 1]
+    else:
+        low, high, *rest = rest
+        low, high = low.at[0], high.at[0]
+    new, sums, *sides, ext = rest
     odd = lax.axis_index("gy") % 2
     y_outer, y_close = odd * (cells_y + 1), (1 - odd) * (cells_y + 1)
-    for x in range(cells_x):
-        for y in range(cells_y):
-            put(ext, x + 1, y + 1, field[x * cells_y + y])
     for y in range(cells_y):
         put(ext, 0, y + 1, turned(left[y], turn[0], turn[1]))
         put(ext, cells_x + 1, y + 1, turned(right[y], turn[2], turn[3]))
     for x in range(cells_x):
         put(ext, x + 1, y_outer, turned(outer[x], turn[4], turn[5]))
         put(ext, x + 1, y_close, close[x])
-    put(ext, 0, y_outer, turned(low[0], turn[6], turn[7]))
-    put(ext, cells_x + 1, y_outer, turned(high[0], turn[8], turn[9]))
+    put(ext, 0, y_outer, turned(low[...], turn[6], turn[7]))
+    put(ext, cells_x + 1, y_outer, turned(high[...], turn[8], turn[9]))
     put(ext, 0, y_close, turned(close[cells_x], turn[0], turn[1]))
     put(ext, cells_x + 1, y_close, turned(close[cells_x + 1], turn[2], turn[3]))
-    sums[...] = inner_sums[...]
     width = cells_y - 2
     for k in range((cells_x - 2) * width):
         new[(1 + k // width) * cells_y + 1 + k % width] = inner[k]
-
-    def body(k, carry):
-        across = k < 2 * cells_y
-        rest = k - 2 * cells_y
-        x = jnp.where(across, (k // cells_y) * (cells_x - 1), 1 + rest // 2)
-        y = jnp.where(across, k % cells_y, (rest % 2) * (cells_y - 1))
-        update(first, ext, blocks, probes, before, new, lambda i: i, sums, x, y, cells_y)
-        return carry
-
-    lax.fori_loop(0, 2 * cells_y + 2 * (cells_x - 2), body, 0, unroll=5)
-    edges(shape, odd, new, e_left, e_right, e_outer, e_low, e_high, e_close)
+    real_sum, imag_sum = inner_sums[0], inner_sums[1]
+    for k, (x, y) in enumerate(rim_cells(shape)):
+        i = x * cells_y + y
+        value = local[k] + apply_part(ext, blocks, x, y, shape, False)
+        if not first:
+            value = 2.0 * value - before[i]
+        new[i] = value
+        real, imag = terms(probes[i], value)
+        real_sum, imag_sum = real_sum + real, imag_sum + imag
+    sums[0] = real_sum
+    sums[1] = imag_sum
+    if sides:
+        edges(shape, odd, new, *sides)
 
 
 def edges(shape, odd, field, e_left, e_right, e_outer, e_low, e_high, e_close):
@@ -168,11 +206,29 @@
     e_high[0] = field[c_outer]
 
 
-def edge_kernel(shape, field, *outs):
-    edges(shape, lax.axis_index("gy") % 2, field, *outs)
-
-
-def corner_kernel(left, right, outer, low, high, close, done, out):
+def edge_kernel(field, left, right, arrived):
+    loads = [
+        pltpu.make_async_copy(field.at[field.shape[0] - 1], left, arrived.at[0]),
+        pltpu.make_async_copy(field.at[0], right, arrived.at[1]),
+    ]
+    for load in loads:
+        load.start()
+    for load in loads:
+        load.wait()
+
+
+def first_pack_kernel(shape, field, left, right, done, outer, close):
+    cells_x, cells_y = shape
+    odd = lax.axis_index("gy") % 2
+    c_outer, c_close = odd * (cells_y - 1), (1 - odd) * (cells_y - 1)
+    for out, c in ((outer, c_outer), (close, c_close)):
+        for x in range(cells_x):
+            out[x] = field[x * cells_y + c]
+        out[cells_x] = left[c]
+        out[cells_x + 1] = right[c]
+
+
+def pack_close_kernel(left, right, outer, low, high, close, done, out):
     near = (1 - lax.axis_index("gy") % 2) * (left.shape[0] - 1)
     cells_x = close.shape[0]
     for x in range(cells_x):
@@ -216,13 +272,17 @@
     def over(j):
         return j + 1 if j % 2 else j - 1
 
-    moves = dict(
-        left=table(lambda i, j: (i + 1, j)),
-        right=table(lambda i, j: (i - 1, j)),
-        outer=table(lambda i, j: (i, over(j))),
-        low=table(lambda i, j: (i + 1, over(j))),
-        high=table(lambda i, j: (i - 1, over(j))),
-    )
+    moves = [
+        table(lambda i, j: (i + 1, j)),
+        table(lambda i, j: (i - 1, j)),
+        table(lambda i, j: (i, over(j))),
+        table(lambda i, j: (i + 1, over(j))),
+        table(lambda i, j: (i - 1, over(j))),
+    ]
+    on_chip = table(lambda i, j: (i, j ^ 1))
+
+    def send(value, move):
+        return lax.ppermute(value, AXES, move)
 
     field = probes.reshape(cells, width, block)
     raw = pair_blocks.reshape(cells, slots, block, block)
@@ -235,11 +295,18 @@
     sums_shape = jax.ShapeDtypeStruct((2, half, block), F32)
     scratch = [pltpu.VMEM((cells_x + 2, 2 * width, (cells_y + 2) * block), BF16)]
 
+    cells_shape = lambda n: jax.ShapeDtypeStruct((n,) + cell, F32)
+    call = lambda body, ins, outs, mib, name, **more: pl.pallas_call(
+        body, out_shape=outs, in_specs=[VMEM] * ins, out_specs=[VMEM] * len(outs),
+        compiler_params=params(mib), name=name, **more,
+    )
     sides = pl.pallas_call(
-        lambda *r: edge_kernel(shape, *r),
-        out_shape=edge_shapes, in_specs=[VMEM], out_specs=[VMEM] * 6,
+        edge_kernel,
+        out_shape=[cells_shape(cells_y)] * 2,
+        in_specs=[pl.BlockSpec(memory_space=pl.ANY)], out_specs=[VMEM] * 2,
+        scratch_shapes=[pltpu.SemaphoreType.DMA((2,))],
         compiler_params=params(1), name="edges",
-    )(field)
+    )(pltpu.with_memory_space_constraint(probes.reshape(cells_x, cells_y, width, block), pltpu.HBM))
 
     blocks, turn = pl.pallas_call(
         lambda *r: split_kernel(sizes, shape, *r),
@@ -255,37 +322,60 @@
 
     flops = 8 * width * block * block * slots
 
-    def step(first, field, before, sides):
+    rim = len(rim_cells(shape))
+
+    def cost(cells):
+        return pl.CostEstimate(flops=cells * flops, bytes_accessed=0, transcendentals=0)
+
+    def inner(first, field, before, after):
+        return call(
+            lambda *r: inner_kernel(first, shape, *r), 5, [inner_shape, sums_shape], 6, "inner",
+            scratch_shapes=scratch, cost_estimate=cost(16),
+        )(field, blocks, probes_flat, before, after)
+
+    def local(field, after):
+        return call(
+            lambda *r: local_kernel(shape, *r), 3, [cells_shape(rim)], 6, "local",
+            scratch_shapes=scratch, cost_estimate=cost(12),
+        )(field, blocks, after)
+
+    def outside(first, last, before, parts, halo):
+        outs = [field_shape, sums_shape] + ([] if last else edge_shapes)
+        return call(
+            lambda *r: rim_kernel(first, shape, *r), 7 + len(halo), outs, 6, "rim",
+            scratch_shapes=scratch, cost_estimate=cost(8),
+        )(turn, blocks, probes_flat, before, *parts, *halo)
+
+    def first_step(field, sides):
+        left, right = send(sides[0], moves[0]), send(sides[1], moves[1])
+        outer, close = call(
+            lambda *r: first_pack_kernel(shape, *r), 4, [cells_shape(cells_x + 2)] * 2, 1, "pack_sides"
+        )(field, left, right, turn)
+        after = outer
+        outer, close = send(outer, moves[2]), send(close, on_chip)
+        parts = [*inner(True, field, field, after), *local(field, after)]
+        return outside(True, False, field, parts, [left, right, outer, close])
+
+    def step(last, field, before, sides):
         *sides, close = sides
-        halo = [lax.ppermute(s, AXES, moves[n]) for n, s in zip(names, sides)]
-        inner, inner_sums = pl.pallas_call(
-            lambda *r: inner_kernel(first, shape, *r),
-            out_shape=[inner_shape, sums_shape], in_specs=[VMEM] * 4, out_specs=[VMEM] * 2,
-            scratch_shapes=scratch, compiler_params=params(6), name="inner",
-            cost_estimate=pl.CostEstimate(flops=16 * flops, bytes_accessed=0, transcendentals=0),
-        )(field, blocks, probes_flat, before)
-        close = pl.pallas_call(
-            corner_kernel, out_shape=jax.ShapeDtypeStruct((cells_x + 2,) + cell, F32),
-            in_specs=[VMEM] * 7, out_specs=VMEM, compiler_params=params(1), name="corner",
-        )(*halo, close, inner_sums)
-        close = lax.ppermute(close, AXES, table(lambda i, j: (i, j ^ 1)))
-        out = pl.pallas_call(
-            lambda *r: rim_kernel(first, shape, *r),
-            out_shape=[field_shape, sums_shape] + edge_shapes,
-            in_specs=[VMEM] * 13, out_specs=[VMEM] * 8,
-            scratch_shapes=scratch, compiler_params=params(8), name="rim",
-            cost_estimate=pl.CostEstimate(flops=20 * flops, bytes_accessed=0, transcendentals=0),
-        )(turn, field, blocks, probes_flat, before, inner, inner_sums,
-          *halo, close)
-        return out[0], out[1], out[2:]
+        halo = [send(s, m) for s, m in zip(sides, moves)]
+        parts = inner(False, field, before, field)
+        (close,) = call(
+            pack_close_kernel, 7, [cells_shape(cells_x + 2)], 1, "pack_close"
+        )(*halo, close, parts[1])
+        after = close
+        close = send(close, on_chip)
+        parts = [*parts, *local(field, after)]
+        left, right, outer, low, high = halo
+        return outside(False, last, before, parts, [left, right, outer, close, low, high])
 
     probes_flat = field
-    names = ("left", "right", "outer", "low", "high")
-    before, found = field, []
-    for n in range(3):
-        new, sums, sides = step(n == 0, field, before, sides)
+    new, sums, *sides = first_step(field, sides)
+    before, field, found = field, new, [sums]
+    for n in range(1, 3):
+        new, sums, *sides = step(n == 2, field, before, sides)
+        before, field = field, new
         found.append(sums)
-        before, field = field, new
 
     scale = 1.0 / math.sqrt(total_x * total_y * block)
     spread = pl.pallas_call(

time: 99.2 us -> 89.7 us (0.904)
  starting transfers between devices: 44.4 us -> 36.5 us
  Pallas kernels: 27.7 us -> 25.9 us
  local copies, waits for them, and re-layouts: 1.95 us -> 0.68 us
  blocking collectives: 16.4 us -> 17.5 us
    ppermute x18 -> x16, starting transfers between devices: 44.4 us -> 36.5 us  [send(): return lax.ppermute(value, AXES, move)]
    pallas_call x10 -> x13, Pallas kernels: 18.5 us -> 16.7 us  [the longest x3 7.46 us: inner(): call(lambda *r: inner_kernel(first, shape, *r), 5, [inner_shape, sums_sha...]
    unnamed x10 -> x8, local copies, waits for them, and re-layouts: 1.28 us -> 0.02 us
    all_to_all x1, blocking collectives: 16.4 us -> 17.5 us  [shards(): total = jnp.sum(lax.all_to_all(spread, AXES, 0, 0), axis=0).reshape(-1)]
    ppermute x18 -> x16, waiting for transfers between devices: 7.55 us -> 8.02 us  [send(): return lax.ppermute(value, AXES, move)]
  transfers between devices with their start and end apart: 18 -> 16, of which waited for: 6 -> 4; matrix products, arithmetic and copies ran while one was open for 0% -> 0% of each run, Pallas kernels for 16% -> 22%
where the time goes in v2:
time: 89.7 us; the launch traced here: 89.6 us
  starting transfers between devices  36.5 us (41%)
  Pallas kernels  25.9 us (29%)
  blocking collectives  17.5 us (20%)
  waiting for transfers between devices  8.02 us (9%)
    ppermute x16, starting transfers between devices, send(): return lax.ppermute(value, AXES, move)  36.5 us
    all_to_all x1, blocking collectives, shards(): total = jnp.sum(lax.all_to_all(spread, AXES, 0, 0), axis=0).reshape(-1)  17.5 us
    pallas_call x1, Pallas kernels, shards(): pl.pallas_call(lambda *r: split_kernel(sizes, shape, *r), out_shape=[jax....  8.86 us
    ppermute x16, waiting for transfers between devices, send(): return lax.ppermute(value, AXES, move)  8.02 us
    pallas_call x3, Pallas kernels, inner(): call(lambda *r: inner_kernel(first, shape, *r), 5, [inner_shape, sums_sha...  7.46 us
    pallas_call x3, Pallas kernels, outside(): call(lambda *r: rim_kernel(first, shape, *r), 7 + len(halo), outs, 6, 'ri...  4.7 us
    pallas_call x3, Pallas kernels, local(): call(lambda *r: local_kernel(shape, *r), 3, [cells_shape(rim)], 6, 'local...  3.41 us
  transfers between devices with their start and end apart: 16, of which 4 were waited for; matrix products, arithmetic and copies ran while one was open for 0% of the time, Pallas kernels for 22%

profile of v2, /device:TPU:1, one launch (start us, length us, event | category | flops | bytes accessed | tf_op | source)
XLA Modules:
  0.0 89.6 jit_solution(12614617189380190636)
XLA Ops:
  0.7 1.1 %edges.1 = (f32[6,64,128]{2,1,0:T(8,128)S(1)}, f32[6,64,128]{2,1,0:T(8,128)S(1)}) custom-call(f32[6,6,64,128]{3,2,1,0:T(8,128)} %field.1), custom_call_target="tpu_custom_call" | custom-call | tf_op jit(solution)/shard_map/edges/pallas_call | solution.py:303
  1.7 3.8 %collective-permute-start = (f32[6,64,128]{2,1,0:T(8,128)S(1)}, f32[6,64,128]{2,1,0:T(8,128)S(1)}, u32[]{:S(2)}, u32[]{:S(2)}) collective-permute-start(f32[6,64,128]{2,1,0:T(8,128)S(1)} %get-tuple-element.34), channel_id=1, source_target_pairs={{0,16},{1,17},{2,18},{3,19},{4,20},{5,21},{6,22},{7,23},{8,24},{9,... | collective-permute-start | bytes 589832 | tf_op jit(solution)/shard_map/ppermute | solution.py:285
  5.5 2.3 %collective-permute-start.1 = (f32[6,64,128]{2,1,0:T(8,128)S(1)}, f32[6,64,128]{2,1,0:T(8,128)S(1)}, u32[]{:S(2)}, u32[]{:S(2)}) collective-permute-start(f32[6,64,128]{2,1,0:T(8,128)S(1)} %get-tuple-element.35), channel_id=1, source_target_pairs={{0,112},{1,113},{2,114},{3,115},{4,116},{5,117},{6,118},{7,119},{8... | collective-permute-start | bytes 589832 | tf_op jit(solution)/shard_map/ppermute | solution.py:285
  7.8 8.9 %split.1 = (bf16[36,1152,256]{2,1,0:T(8,128)(2,1)S(1)}, f32[10,32,128]{2,1,0:T(8,128)S(1)}) custom-call(f32[2]{0:T(128)S(1)} %copy-done.3, s32[6,6,9]{2,1,0:T(8,128)S(1)} %copy-done.1, s32[6,6]{1,0:T(8,128)S(1)} %copy-done.2, f32[36,9,128,128]{3,2,1,0:T(8,128)} %bitcast.16), custom_call_target="tpu_custom_call" | custom-call | flops 21233664 | bytes 42467328 | tf_op jit(solution)/shard_map/split/pallas_call | solution.py:311
  16.7 0.6 collective-permute-done.1.r_2_.r_8_
  17.3 0.6 collective-permute-start.3
  17.9 1.3 %collective-permute-start.2 = (f32[8,64,128]{2,1,0:T(8,128)S(1)}, f32[8,64,128]{2,1,0:T(8,128)S(1)}, u32[]{:S(2)}, u32[]{:S(2)}) collective-permute-start(f32[8,64,128]{2,1,0:T(8,128)S(1)} %get-tuple-element.36.r_4_.r_2_), channel_id=1, source_target_pairs={{0,15},{1,2},{2,1},{3,4},{4,3},{5,6},{6,5},{7,8},{8,7},{9,10},{10,... | collective-permute-start | bytes 786440 | tf_op jit(solution)/shard_map/ppermute | solution.py:285
  19.3 1.1 %local.3.r_6_ = f32[20,64,128]{2,1,0:T(8,128)S(1)} custom-call(f32[36,64,128]{2,1,0:T(8,128)S(1)} %bitcast.4, bf16[36,1152,256]{2,1,0:T(8,128)(2,1)S(1)} %get-tuple-element.33.r_1_, f32[8,64,128]{2,1,0:T(8,128)S(1)} %get-tuple-element.36.r_4_.r_2_), custom_call_target="tpu_custom_call" | custom-call | flops 905969664 | tf_op jit(solution)/shard_map/local/pallas_call | solution.py:337
  20.4 2.5 %inner.3 = (f32[16,64,128]{2,1,0:T(8,128)S(1)}, f32[2,32,128]{2,1,0:T(8,128)S(1)}) custom-call(f32[36,64,128]{2,1,0:T(8,128)S(1)} %bitcast.5, bf16[36,1152,256]{2,1,0:T(8,128)(2,1)S(1)} %get-tuple-element.33.r_1_, f32[36,64,128]{2,1,0:T(8,128)S(1)} %bitcast.6, f32[36,64,128]{2,1,0:T(8,128)S(1)} %bitcast.7, f32[8,64,128]{2,1,0:T(8,128)S(1)} %get-tuple-element.36.r_4_.r_2_), custom_call_target="tpu_custom_call" | custom-call | flops 1207959552 | tf_op jit(solution)/shard_map/inner/pallas_call | solution.py:331
  22.9 3.1 %collective-permute-done.2.r_9_ = f32[8,64,128]{2,1,0:T(8,128)S(1)} collective-permute-done((f32[8,64,128]{2,1,0:T(8,128)S(1)}, f32[8,64,128]{2,1,0:T(8,128)S(1)}, u32[]{:S(2)}, u32[]{:S(2)}) %collective-permute-start.2) | collective-permute-done | bytes 262176 | tf_op jit(solution)/shard_map/ppermute | solution.py:285
  26.0 1.3 %rim.3 = (f32[36,64,128]{2,1,0:T(8,128)S(1)}, f32[2,32,128]{2,1,0:T(8,128)S(1)}, f32[6,64,128]{2,1,0:T(8,128)S(1)}, f32[6,64,128]{2,1,0:T(8,128)S(1)}, f32[6,64,...) custom-call(f32[10,32,128]{2,1,0:T(8,128)S(1)} %get-tuple-element.32.r_3_.r, ...), custom_call_target="tpu_custom_call" | custom-call | flops 603979776 | tf_op jit(solution)/shard_map/rim/pallas_call | solution.py:344
  27.3 1.0 %collective-permute-start.4 = (f32[6,64,128]{2,1,0:T(8,128)S(1)}, f32[6,64,128]{2,1,0:T(8,128)S(1)}, u32[]{:S(2)}, u32[]{:S(2)}) collective-permute-start(f32[6,64,128]{2,1,0:T(8,128)S(1)} %get-tuple-element.43), channel_id=1, source_target_pairs={{0,16},{1,17},{2,18},{3,19},{4,20},{5,21},{6,22},{7,23},{8,24},{9,... | collective-permute-start | bytes 589832 | tf_op jit(solution)/shard_map/ppermute | solution.py:285
  28.3 4.1 %collective-permute-start.5 = (f32[6,64,128]{2,1,0:T(8,128)S(1)}, f32[6,64,128]{2,1,0:T(8,128)S(1)}, u32[]{:S(2)}, u32[]{:S(2)}) collective-permute-start(f32[6,64,128]{2,1,0:T(8,128)S(1)} %get-tuple-element.44), channel_id=1, source_target_pairs={{0,112},{1,113},{2,114},{3,115},{4,116},{5,117},{6,118},{7,119},{8... | collective-permute-start | bytes 589832 | tf_op jit(solution)/shard_map/ppermute | solution.py:285
  32.4 0.1 collective-permute-start.6
  32.5 5.1 %collective-permute-start.8 = (f32[1,64,128]{2,1,0:T(8,128)S(1)}, f32[1,64,128]{2,1,0:T(8,128)S(1)}, u32[]{:S(2)}, u32[]{:S(2)}) collective-permute-start(f32[1,64,128]{2,1,0:T(8,128)S(1)} %get-tuple-element.47), channel_id=1, source_target_pairs={{0,127},{1,114},{2,113},{3,116},{4,115},{5,118},{6,117},{7,120},{8... | collective-permute-start | bytes 98312 | tf_op jit(solution)/shard_map/ppermute | solution.py:285
  37.6 2.5 %inner.4 = (f32[16,64,128]{2,1,0:T(8,128)S(1)}, f32[2,32,128]{2,1,0:T(8,128)S(1)}) custom-call(f32[36,64,128]{2,1,0:T(8,128)S(1)} %get-tuple-element.40.r_0_.r_4_.r_3_, bf16[36,1152,256]{2,1,0:T(8,128)(2,1)S(1)} %get-tuple-element.33.r_1_, f32[36,64,128]{2,1,0:T(8,128)S(1)} %bitcast.10, f32[36,64,128]{2,1,0:T(8,128)S(1)} %bitcast.11, ...), custom_call_target="tpu_custom_call" | custom-call | flops 1207959552 | tf_op jit(solution)/shard_map/inner/pallas_call | solution.py:331
  40.1 1.4 %collective-permute-done.8.high.r_12_ = f32[1,64,128]{2,1,0:T(8,128)S(1)} collective-permute-done((f32[1,64,128]{2,1,0:T(8,128)S(1)}, f32[1,64,128]{2,1,0:T(8,128)S(1)}, u32[]{:S(2)}, u32[]{:S(2)}) %collective-permute-start.8) | collective-permute-done | bytes 32800 | tf_op jit(solution)/shard_map/ppermute | solution.py:285
  41.5 5.8 %collective-permute-start.9 = (f32[8,64,128]{2,1,0:T(8,128)S(1)}, f32[8,64,128]{2,1,0:T(8,128)S(1)}, u32[]{:S(2)}, u32[]{:S(2)}) collective-permute-start(f32[8,64,128]{2,1,0:T(8,128)S(1)} %pack_close.2.r_2_), channel_id=1, source_target_pairs={{0,1},{1,0},{2,3},{3,2},{4,5},{5,4},{6,7},{7,6},{8,9},{9,8},{10,11... | collective-permute-start | bytes 786440 | tf_op jit(solution)/shard_map/ppermute | solution.py:285
  47.3 1.1 %local.4.r_6_ = f32[20,64,128]{2,1,0:T(8,128)S(1)} custom-call(f32[36,64,128]{2,1,0:T(8,128)S(1)} %get-tuple-element.40.r_0_.r_4_.r_3_, bf16[36,1152,256]{2,1,0:T(8,128)(2,1)S(1)} %get-tuple-element.33.r_1_, f32[8,64,128]{2,1,0:T(8,128)S(1)} %pack_close.2.r_2_), custom_call_target="tpu_custom_call" | custom-call | flops 905969664 | tf_op jit(solution)/shard_map/local/pallas_call | solution.py:337
  48.5 1.3 %rim.4 = (f32[36,64,128]{2,1,0:T(8,128)S(1)}, f32[2,32,128]{2,1,0:T(8,128)S(1)}, f32[6,64,128]{2,1,0:T(8,128)S(1)}, f32[6,64,128]{2,1,0:T(8,128)S(1)}, f32[6,64,...) custom-call(f32[10,32,128]{2,1,0:T(8,128)S(1)} %get-tuple-element.32.r_3_.r, ...), custom_call_target="tpu_custom_call" | custom-call | flops 603979776 | tf_op jit(solution)/shard_map/rim/pallas_call | solution.py:344
  49.7 1.9 %collective-permute-start.10 = (f32[6,64,128]{2,1,0:T(8,128)S(1)}, f32[6,64,128]{2,1,0:T(8,128)S(1)}, u32[]{:S(2)}, u32[]{:S(2)}) collective-permute-start(f32[6,64,128]{2,1,0:T(8,128)S(1)} %get-tuple-element.52), channel_id=1, source_target_pairs={{0,16},{1,17},{2,18},{3,19},{4,20},{5,21},{6,22},{7,23},{8,24},{9,... | collective-permute-start | bytes 589832 | tf_op jit(solution)/shard_map/ppermute | solution.py:285
  51.6 3.4 %collective-permute-start.11 = (f32[6,64,128]{2,1,0:T(8,128)S(1)}, f32[6,64,128]{2,1,0:T(8,128)S(1)}, u32[]{:S(2)}, u32[]{:S(2)}) collective-permute-start(f32[6,64,128]{2,1,0:T(8,128)S(1)} %get-tuple-element.53), channel_id=1, source_target_pairs={{0,112},{1,113},{2,114},{3,115},{4,116},{5,117},{6,118},{7,119},{8... | collective-permute-start | bytes 589832 | tf_op jit(solution)/shard_map/ppermute | solution.py:285
  55.1 5.0 %collective-permute-start.14 = (f32[1,64,128]{2,1,0:T(8,128)S(1)}, f32[1,64,128]{2,1,0:T(8,128)S(1)}, u32[]{:S(2)}, u32[]{:S(2)}) collective-permute-start(f32[1,64,128]{2,1,0:T(8,128)S(1)} %get-tuple-element.56), channel_id=1, source_target_pairs={{0,127},{1,114},{2,113},{3,116},{4,115},{5,118},{6,117},{7,120},{8... | collective-permute-start | bytes 98312 | tf_op jit(solution)/shard_map/ppermute | solution.py:285
  60.1 2.5 %inner.5 = (f32[16,64,128]{2,1,0:T(8,128)S(1)}, f32[2,32,128]{2,1,0:T(8,128)S(1)}) custom-call(f32[36,64,128]{2,1,0:T(8,128)S(1)} %get-tuple-element.49.r_0_.r_4_, bf16[36,1152,256]{2,1,0:T(8,128)(2,1)S(1)} %get-tuple-element.33.r_1_, f32[36,64,128]{2,1,0:T(8,128)S(1)} %bitcast.14, f32[36,64,128]{2,1,0:T(8,128)S(1)} %get-tuple-element.40.r_0_.r_4_.r_3_, ...), custom_call_target="tpu_custom_call" | custom-call | flops 1207959552 | tf_op jit(solution)/shard_map/inner/pallas_call | solution.py:331
  62.6 2.9 %collective-permute-done.14.high.r_12_ = f32[1,64,128]{2,1,0:T(8,128)S(1)} collective-permute-done((f32[1,64,128]{2,1,0:T(8,128)S(1)}, f32[1,64,128]{2,1,0:T(8,128)S(1)}, u32[]{:S(2)}, u32[]{:S(2)}) %collective-permute-start.14) | collective-permute-done | bytes 32800 | tf_op jit(solution)/shard_map/ppermute | solution.py:285
  65.5 2.1 %collective-permute-start.15 = (f32[8,64,128]{2,1,0:T(8,128)S(1)}, f32[8,64,128]{2,1,0:T(8,128)S(1)}, u32[]{:S(2)}, u32[]{:S(2)}) collective-permute-start(f32[8,64,128]{2,1,0:T(8,128)S(1)} %pack_close.3.r_2_), channel_id=1, source_target_pairs={{0,1},{1,0},{2,3},{3,2},{4,5},{5,4},{6,7},{7,6},{8,9},{9,8},{10,11... | collective-permute-start | bytes 786440 | tf_op jit(solution)/shard_map/ppermute | solution.py:285
  67.6 1.1 %local.5.r_6_ = f32[20,64,128]{2,1,0:T(8,128)S(1)} custom-call(f32[36,64,128]{2,1,0:T(8,128)S(1)} %get-tuple-element.49.r_0_.r_4_, bf16[36,1152,256]{2,1,0:T(8,128)(2,1)S(1)} %get-tuple-element.33.r_1_, f32[8,64,128]{2,1,0:T(8,128)S(1)} %pack_close.3.r_2_), custom_call_target="tpu_custom_call" | custom-call | flops 905969664 | tf_op jit(solution)/shard_map/local/pallas_call | solution.py:337
  68.8 2.2 %rim.5 = (f32[36,64,128]{2,1,0:T(8,128)}, f32[2,32,128]{2,1,0:T(8,128)S(1)}) custom-call(f32[10,32,128]{2,1,0:T(8,128)S(1)} %get-tuple-element.32.r_3_.r_0_, bf16[36,1152,256]{2,1,0:T(8,128)(2,1)S(1)} %get-tuple-element.33.r_1_, f32[36,64,128]{2,1,0:T(8,128)S(1)} %bitcast.15, f32[36,64,128]{2,1,0:T(8,128)S(1)} %get-tuple-element.40.r_0_.r_4_.r_3_, ...), custom_call_target="tpu_custom_call" | custom-call | flops 603979776 | tf_op jit(solution)/shard_map/rim/pallas_call | solution.py:344
  70.9 0.3 pack.1
  71.3 17.5 %all_to_all.5 = f32[128,2,128]{2,1,0:T(2,128)S(1)} all-to-all(f32[128,2,128]{2,1,0:T(2,128)S(1)} %pack.1), channel_id=1, replica_groups=mesh['gx'=8,'gy'=16] {'gx','gy'}, dimensions={0} | all-to-all | bytes 262144 | tf_op jit(solution)/shard_map/all_to_all | solution.py:386
  88.8 0.1 reduce_sum.9
  89.0 0.6 slice.8
  (27 shorter events, 0.3 us)
Async XLA Ops:
  0.6 7.2 %copy-start.3 = (f32[2]{0:T(128)S(1)}, f32[2]{0:T(128)}, u32[]{:S(2)}) copy-start(f32[2]{0:T(128)} %r_0_.1) | copy-start | bytes 28
  0.6 7.2 %copy-start.2 = (s32[6,6]{1,0:T(8,128)S(1)}, s32[6,6]{1,0:T(8,128)}, u32[]{:S(2)}) copy-start(s32[6,6]{1,0:T(8,128)} %r_2_.1) | copy-start | bytes 436
  0.7 7.2 %copy-start.1 = (s32[6,6,9]{2,1,0:T(8,128)S(1)}, s32[6,6,9]{2,1,0:T(8,128)}, u32[]{:S(2)}) copy-start(s32[6,6,9]{2,1,0:T(8,128)} %r_1_.1) | copy-start | bytes 3892
  1.7 15.0 %collective-permute-start = (f32[6,64,128]{2,1,0:T(8,128)S(1)}, f32[6,64,128]{2,1,0:T(8,128)S(1)}, u32[]{:S(2)}, u32[]{:S(2)}) collective-permute-start(f32[6,64,128]{2,1,0:T(8,128)S(1)} %get-tuple-element.34), channel_id=1, source_target_pairs={{0,16},{1,17},{2,18},{3,19},{4,20},{5,21},{6,22},{7,23},{8,24},{9,... | collective-permute-start | bytes 589832 | tf_op jit(solution)/shard_map/ppermute | solution.py:285
  5.5 11.8 %collective-permute-start.1 = (f32[6,64,128]{2,1,0:T(8,128)S(1)}, f32[6,64,128]{2,1,0:T(8,128)S(1)}, u32[]{:S(2)}, u32[]{:S(2)}) collective-permute-start(f32[6,64,128]{2,1,0:T(8,128)S(1)} %get-tuple-element.35), channel_id=1, source_target_pairs={{0,112},{1,113},{2,114},{3,115},{4,116},{5,117},{6,118},{7,119},{8... | collective-permute-start | bytes 589832 | tf_op jit(solution)/shard_map/ppermute | solution.py:285
  7.8 9.5 %copy-start = (f32[6,6,64,128]{3,2,1,0:T(8,128)S(1)}, f32[6,6,64,128]{3,2,1,0:T(8,128)}, u32[]{:S(2)}) copy-start(f32[6,6,64,128]{3,2,1,0:T(8,128)} %field.1) | copy-start | bytes 3538948
  17.3 5.5 %collective-permute-start.3 = (f32[8,64,128]{2,1,0:T(8,128)S(1)}, f32[8,64,128]{2,1,0:T(8,128)S(1)}, u32[]{:S(2)}, u32[]{:S(2)}) collective-permute-start(f32[8,64,128]{2,1,0:T(8,128)S(1)} %get-tuple-element.39), channel_id=1, source_target_pairs={{0,1},{1,0},{2,3},{3,2},{4,5},{5,4},{6,7},{7,6},{8,9},{9,8},{10,11... | collective-permute-start | bytes 786440 | tf_op jit(solution)/shard_map/ppermute | solution.py:285
  17.9 8.1 %collective-permute-start.2 = (f32[8,64,128]{2,1,0:T(8,128)S(1)}, f32[8,64,128]{2,1,0:T(8,128)S(1)}, u32[]{:S(2)}, u32[]{:S(2)}) collective-permute-start(f32[8,64,128]{2,1,0:T(8,128)S(1)} %get-tuple-element.36.r_4_.r_2_), channel_id=1, source_target_pairs={{0,15},{1,2},{2,1},{3,4},{4,3},{5,6},{6,5},{7,8},{8,7},{9,10},{10,... | collective-permute-start | bytes 786440 | tf_op jit(solution)/shard_map/ppermute | solution.py:285
  27.3 14.2 %collective-permute-start.4 = (f32[6,64,128]{2,1,0:T(8,128)S(1)}, f32[6,64,128]{2,1,0:T(8,128)S(1)}, u32[]{:S(2)}, u32[]{:S(2)}) collective-permute-start(f32[6,64,128]{2,1,0:T(8,128)S(1)} %get-tuple-element.43), channel_id=1, source_target_pairs={{0,16},{1,17},{2,18},{3,19},{4,20},{5,21},{6,22},{7,23},{8,24},{9,... | collective-permute-start | bytes 589832 | tf_op jit(solution)/shard_map/ppermute | solution.py:285
  28.3 13.2 %collective-permute-start.5 = (f32[6,64,128]{2,1,0:T(8,128)S(1)}, f32[6,64,128]{2,1,0:T(8,128)S(1)}, u32[]{:S(2)}, u32[]{:S(2)}) collective-permute-start(f32[6,64,128]{2,1,0:T(8,128)S(1)} %get-tuple-element.44), channel_id=1, source_target_pairs={{0,112},{1,113},{2,114},{3,115},{4,116},{5,117},{6,118},{7,119},{8... | collective-permute-start | bytes 589832 | tf_op jit(solution)/shard_map/ppermute | solution.py:285
  32.4 9.0 %collective-permute-start.6 = (f32[6,64,128]{2,1,0:T(8,128)S(1)}, f32[6,64,128]{2,1,0:T(8,128)S(1)}, u32[]{:S(2)}, u32[]{:S(2)}) collective-permute-start(f32[6,64,128]{2,1,0:T(8,128)S(1)} %get-tuple-element.45), channel_id=1, source_target_pairs={{0,15},{1,2},{2,1},{3,4},{4,3},{5,6},{6,5},{7,8},{8,7},{9,10},{10,... | collective-permute-start | bytes 589832 | tf_op jit(solution)/shard_map/ppermute | solution.py:285
  32.5 7.6 %collective-permute-start.7 = (f32[1,64,128]{2,1,0:T(8,128)S(1)}, f32[1,64,128]{2,1,0:T(8,128)S(1)}, u32[]{:S(2)}, u32[]{:S(2)}) collective-permute-start(f32[1,64,128]{2,1,0:T(8,128)S(1)} %get-tuple-element.46), channel_id=1, source_target_pairs={{0,31},{1,18},{2,17},{3,20},{4,19},{5,22},{6,21},{7,24},{8,23},{9,... | collective-permute-start | bytes 98312 | tf_op jit(solution)/shard_map/ppermute | solution.py:285
  32.5 8.9 %collective-permute-start.8 = (f32[1,64,128]{2,1,0:T(8,128)S(1)}, f32[1,64,128]{2,1,0:T(8,128)S(1)}, u32[]{:S(2)}, u32[]{:S(2)}) collective-permute-start(f32[1,64,128]{2,1,0:T(8,128)S(1)} %get-tuple-element.47), channel_id=1, source_target_pairs={{0,127},{1,114},{2,113},{3,116},{4,115},{5,118},{6,117},{7,120},{8... | collective-permute-start | bytes 98312 | tf_op jit(solution)/shard_map/ppermute | solution.py:285
  41.5 6.9 %collective-permute-start.9 = (f32[8,64,128]{2,1,0:T(8,128)S(1)}, f32[8,64,128]{2,1,0:T(8,128)S(1)}, u32[]{:S(2)}, u32[]{:S(2)}) collective-permute-start(f32[8,64,128]{2,1,0:T(8,128)S(1)} %pack_close.2.r_2_), channel_id=1, source_target_pairs={{0,1},{1,0},{2,3},{3,2},{4,5},{5,4},{6,7},{7,6},{8,9},{9,8},{10,11... | collective-permute-start | bytes 786440 | tf_op jit(solution)/shard_map/ppermute | solution.py:285
  49.7 15.8 %collective-permute-start.10 = (f32[6,64,128]{2,1,0:T(8,128)S(1)}, f32[6,64,128]{2,1,0:T(8,128)S(1)}, u32[]{:S(2)}, u32[]{:S(2)}) collective-permute-start(f32[6,64,128]{2,1,0:T(8,128)S(1)} %get-tuple-element.52), channel_id=1, source_target_pairs={{0,16},{1,17},{2,18},{3,19},{4,20},{5,21},{6,22},{7,23},{8,24},{9,... | collective-permute-start | bytes 589832 | tf_op jit(solution)/shard_map/ppermute | solution.py:285
  51.6 13.9 %collective-permute-start.11 = (f32[6,64,128]{2,1,0:T(8,128)S(1)}, f32[6,64,128]{2,1,0:T(8,128)S(1)}, u32[]{:S(2)}, u32[]{:S(2)}) collective-permute-start(f32[6,64,128]{2,1,0:T(8,128)S(1)} %get-tuple-element.53), channel_id=1, source_target_pairs={{0,112},{1,113},{2,114},{3,115},{4,116},{5,117},{6,118},{7,119},{8... | collective-permute-start | bytes 589832 | tf_op jit(solution)/shard_map/ppermute | solution.py:285
  55.0 10.5 %collective-permute-start.12 = (f32[6,64,128]{2,1,0:T(8,128)S(1)}, f32[6,64,128]{2,1,0:T(8,128)S(1)}, u32[]{:S(2)}, u32[]{:S(2)}) collective-permute-start(f32[6,64,128]{2,1,0:T(8,128)S(1)} %get-tuple-element.54), channel_id=1, source_target_pairs={{0,15},{1,2},{2,1},{3,4},{4,3},{5,6},{6,5},{7,8},{8,7},{9,10},{10,... | collective-permute-start | bytes 589832 | tf_op jit(solution)/shard_map/ppermute | solution.py:285
  55.0 7.6 %collective-permute-start.13 = (f32[1,64,128]{2,1,0:T(8,128)S(1)}, f32[1,64,128]{2,1,0:T(8,128)S(1)}, u32[]{:S(2)}, u32[]{:S(2)}) collective-permute-start(f32[1,64,128]{2,1,0:T(8,128)S(1)} %get-tuple-element.55), channel_id=1, source_target_pairs={{0,31},{1,18},{2,17},{3,20},{4,19},{5,22},{6,21},{7,24},{8,23},{9,... | collective-permute-start | bytes 98312 | tf_op jit(solution)/shard_map/ppermute | solution.py:285
  55.1 10.4 %collective-permute-start.14 = (f32[1,64,128]{2,1,0:T(8,128)S(1)}, f32[1,64,128]{2,1,0:T(8,128)S(1)}, u32[]{:S(2)}, u32[]{:S(2)}) collective-permute-start(f32[1,64,128]{2,1,0:T(8,128)S(1)} %get-tuple-element.56), channel_id=1, source_target_pairs={{0,127},{1,114},{2,113},{3,116},{4,115},{5,118},{6,117},{7,120},{8... | collective-permute-start | bytes 98312 | tf_op jit(solution)/shard_map/ppermute | solution.py:285
  65.5 3.2 %collective-permute-start.15 = (f32[8,64,128]{2,1,0:T(8,128)S(1)}, f32[8,64,128]{2,1,0:T(8,128)S(1)}, u32[]{:S(2)}, u32[]{:S(2)}) collective-permute-start(f32[8,64,128]{2,1,0:T(8,128)S(1)} %pack_close.3.r_2_), channel_id=1, source_target_pairs={{0,1},{1,0},{2,3},{3,2},{4,5},{5,4},{6,7},{7,6},{8,9},{9,8},{10,11... | collective-permute-start | bytes 786440 | tf_op jit(solution)/shard_map/ppermute | solution.py:285

commit v3 on v2

--- a/solution.py
+++ b/solution.py
@@ -157,7 +157,8 @@
 ):
     cells_x, cells_y = shape
     if first:
-        low, high = outer.at[cells_x], outer.at[cells_x + 1]
+        low, *rest = rest
+        low, high = low.at[0], low.at[1]
     else:
         low, high, *rest = rest
         low, high = low.at[0], high.at[0]
@@ -206,11 +207,12 @@
     e_high[0] = field[c_outer]
 
 
-def edge_kernel(field, left, right, arrived):
-    loads = [
-        pltpu.make_async_copy(field.at[field.shape[0] - 1], left, arrived.at[0]),
-        pltpu.make_async_copy(field.at[0], right, arrived.at[1]),
-    ]
+def edge_kernel(shape, field, left, right, outer, arrived):
+    cells_x, cells_y = shape
+    c_outer = (lax.axis_index("gy") % 2) * (cells_y - 1)
+    pairs = [(field.at[cells_x - 1], left), (field.at[0], right)]
+    pairs += [(field.at[x, c_outer], outer.at[x]) for x in range(cells_x)]
+    loads = [pltpu.make_async_copy(*pair, arrived.at[k]) for k, pair in enumerate(pairs)]
     for load in loads:
         load.start()
     for load in loads:
@@ -221,11 +223,12 @@
     cells_x, cells_y = shape
     odd = lax.axis_index("gy") % 2
     c_outer, c_close = odd * (cells_y - 1), (1 - odd) * (cells_y - 1)
-    for out, c in ((outer, c_outer), (close, c_close)):
-        for x in range(cells_x):
-            out[x] = field[x * cells_y + c]
-        out[cells_x] = left[c]
-        out[cells_x + 1] = right[c]
+    outer[0] = left[c_outer]
+    outer[1] = right[c_outer]
+    for x in range(cells_x):
+        close[x] = field[x * cells_y + c_close]
+    close[cells_x] = left[c_close]
+    close[cells_x + 1] = right[c_close]
 
 
 def pack_close_kernel(left, right, outer, low, high, close, done, out):
@@ -301,10 +304,10 @@
         compiler_params=params(mib), name=name, **more,
     )
     sides = pl.pallas_call(
-        edge_kernel,
-        out_shape=[cells_shape(cells_y)] * 2,
-        in_specs=[pl.BlockSpec(memory_space=pl.ANY)], out_specs=[VMEM] * 2,
-        scratch_shapes=[pltpu.SemaphoreType.DMA((2,))],
+        lambda *r: edge_kernel(shape, *r),
+        out_shape=[cells_shape(cells_y)] * 2 + [cells_shape(cells_x)],
+        in_specs=[pl.BlockSpec(memory_space=pl.ANY)], out_specs=[VMEM] * 3,
+        scratch_shapes=[pltpu.SemaphoreType.DMA((2 + cells_x,))],
         compiler_params=params(1), name="edges",
     )(pltpu.with_memory_space_constraint(probes.reshape(cells_x, cells_y, width, block), pltpu.HBM))
 
@@ -347,14 +350,15 @@
         )(turn, blocks, probes_flat, before, *parts, *halo)
 
     def first_step(field, sides):
-        left, right = send(sides[0], moves[0]), send(sides[1], moves[1])
-        outer, close = call(
-            lambda *r: first_pack_kernel(shape, *r), 4, [cells_shape(cells_x + 2)] * 2, 1, "pack_sides"
-        )(field, left, right, turn)
-        after = outer
-        outer, close = send(outer, moves[2]), send(close, on_chip)
-        parts = [*inner(True, field, field, after), *local(field, after)]
-        return outside(True, False, field, parts, [left, right, outer, close])
+        halo = [send(s, m) for s, m in zip(sides, moves)]
+        corners, close = call(
+            lambda *r: first_pack_kernel(shape, *r), 4, [cells_shape(2), cells_shape(cells_x + 2)], 1,
+            "pack_sides",
+        )(field, *halo[:2], turn)
+        after = corners
+        corners, close = send(corners, moves[2]), send(close, on_chip)
+        parts = [*inner(True, field, field, halo[2]), *local(field, after)]
+        return outside(True, False, field, parts, [*halo, close, corners])
 
     def step(last, field, before, sides):
         *sides, close = sides

time: 89.7 us -> 88.2 us (0.983)
  waiting for transfers between devices: 8.02 us -> 3.72 us
  starting transfers between devices: 36.5 us -> 38.7 us
    ppermute x16 -> x17, waiting for transfers between devices: 8.02 us -> 3.72 us  [send(): return lax.ppermute(value, AXES, move)]
    ppermute x16 -> x17, starting transfers between devices: 36.5 us -> 38.7 us  [send(): return lax.ppermute(value, AXES, move)]
  transfers between devices with their start and end apart: 16 -> 17, of which waited for: 4 -> 5; matrix products, arithmetic and copies ran while one was open for 0% -> 0% of each run, Pallas kernels for 22% -> 22%
where the time goes in v3:
time: 88.2 us; the launch traced here: 88 us
  starting transfers between devices  38.7 us (44%)
  Pallas kernels  26 us (29%)
  blocking collectives  18 us (20%)
  waiting for transfers between devices  3.72 us (4%)
    ppermute x17, starting transfers between devices, send(): return lax.ppermute(value, AXES, move)  38.7 us
    all_to_all x1, blocking collectives, shards(): total = jnp.sum(lax.all_to_all(spread, AXES, 0, 0), axis=0).reshape(-1)  18 us
    pallas_call x1, Pallas kernels, shards(): pl.pallas_call(lambda *r: split_kernel(sizes, shape, *r), out_shape=[jax....  8.86 us
    pallas_call x3, Pallas kernels, inner(): call(lambda *r: inner_kernel(first, shape, *r), 5, [inner_shape, sums_sha...  7.47 us
    pallas_call x3, Pallas kernels, outside(): call(lambda *r: rim_kernel(first, shape, *r), 7 + len(halo), outs, 6, 'ri...  4.7 us
    ppermute x17, waiting for transfers between devices, send(): return lax.ppermute(value, AXES, move)  3.72 us
    pallas_call x3, Pallas kernels, local(): call(lambda *r: local_kernel(shape, *r), 3, [cells_shape(rim)], 6, 'local...  3.41 us
  transfers between devices with their start and end apart: 17, of which 5 were waited for; matrix products, arithmetic and copies ran while one was open for 0% of the time, Pallas kernels for 22%

profile of v3, /device:TPU:1, one launch (start us, length us, event | category | flops | bytes accessed | tf_op | source)
XLA Modules:
  0.0 88.0 jit_solution(5197693084111815380)
XLA Ops:
  0.7 1.1 %edges.1 = (f32[6,64,128]{2,1,0:T(8,128)S(1)}, f32[6,64,128]{2,1,0:T(8,128)S(1)}, f32[6,64,128]{2,1,0:T(8,128)S(1)}) custom-call(f32[6,6,64,128]{3,2,1,0:T(8,128)} %r_0_.3), custom_call_target="tpu_custom_call" | custom-call | tf_op jit(solution)/shard_map/edges/pallas_call | solution.py:306
  1.8 3.8 %collective-permute-start.1 = (f32[6,64,128]{2,1,0:T(8,128)S(1)}, f32[6,64,128]{2,1,0:T(8,128)S(1)}, u32[]{:S(2)}, u32[]{:S(2)}) collective-permute-start(f32[6,64,128]{2,1,0:T(8,128)S(1)} %get-tuple-element.38), channel_id=1, source_target_pairs={{0,16},{1,17},{2,18},{3,19},{4,20},{5,21},{6,22},{7,23},{8,24},{9,... | collective-permute-start | bytes 589832 | tf_op jit(solution)/shard_map/ppermute | solution.py:288
  5.6 2.3 %collective-permute-start.2 = (f32[6,64,128]{2,1,0:T(8,128)S(1)}, f32[6,64,128]{2,1,0:T(8,128)S(1)}, u32[]{:S(2)}, u32[]{:S(2)}) collective-permute-start(f32[6,64,128]{2,1,0:T(8,128)S(1)} %get-tuple-element.39), channel_id=1, source_target_pairs={{0,112},{1,113},{2,114},{3,115},{4,116},{5,117},{6,118},{7,119},{8... | collective-permute-start | bytes 589832 | tf_op jit(solution)/shard_map/ppermute | solution.py:288
  7.9 2.3 %collective-permute-start = (f32[6,64,128]{2,1,0:T(8,128)S(1)}, f32[6,64,128]{2,1,0:T(8,128)S(1)}, u32[]{:S(2)}, u32[]{:S(2)}) collective-permute-start(f32[6,64,128]{2,1,0:T(8,128)S(1)} %get-tuple-element.35), channel_id=1, source_target_pairs={{0,15},{1,2},{2,1},{3,4},{4,3},{5,6},{6,5},{7,8},{8,7},{9,10},{10,... | collective-permute-start | bytes 589832 | tf_op jit(solution)/shard_map/ppermute | solution.py:288
  10.2 8.9 %split.1 = (bf16[36,1152,256]{2,1,0:T(8,128)(2,1)S(1)}, f32[10,32,128]{2,1,0:T(8,128)S(1)}) custom-call(f32[2]{0:T(128)S(1)} %copy-done.3, s32[6,6,9]{2,1,0:T(8,128)S(1)} %copy-done.1, s32[6,6]{1,0:T(8,128)S(1)} %copy-done.2, f32[36,9,128,128]{3,2,1,0:T(8,128)} %bitcast.16), custom_call_target="tpu_custom_call" | custom-call | flops 21233664 | bytes 42467328 | tf_op jit(solution)/shard_map/split/pallas_call | solution.py:314
  19.1 2.8 %collective-permute-start.3 = (f32[8,64,128]{2,1,0:T(8,128)S(1)}, f32[8,64,128]{2,1,0:T(8,128)S(1)}, u32[]{:S(2)}, u32[]{:S(2)}) collective-permute-start(f32[8,64,128]{2,1,0:T(8,128)S(1)} %get-tuple-element.41), channel_id=1, source_target_pairs={{0,1},{1,0},{2,3},{3,2},{4,5},{5,4},{6,7},{7,6},{8,9},{9,8},{10,11... | collective-permute-start | bytes 786440 | tf_op jit(solution)/shard_map/ppermute | solution.py:288
  22.0 2.5 %inner.3 = (f32[16,64,128]{2,1,0:T(8,128)S(1)}, f32[2,32,128]{2,1,0:T(8,128)S(1)}) custom-call(f32[36,64,128]{2,1,0:T(8,128)S(1)} %bitcast.4, bf16[36,1152,256]{2,1,0:T(8,128)(2,1)S(1)} %get-tuple-element.34.r_1_, f32[36,64,128]{2,1,0:T(8,128)S(1)} %bitcast.5, f32[36,64,128]{2,1,0:T(8,128)S(1)} %bitcast.6, f32[6,64,128]{2,1,0:T(8,128)S(1)} %collective-permute-done.r_4_.r_9_), custom_call_target="tpu_custom_call" | custom-call | flops 1207959552 | tf_op jit(solution)/shard_map/inner/pallas_call | solution.py:334
  24.5 1.1 %local.3.r_6_ = f32[20,64,128]{2,1,0:T(8,128)S(1)} custom-call(f32[36,64,128]{2,1,0:T(8,128)S(1)} %bitcast.7, bf16[36,1152,256]{2,1,0:T(8,128)(2,1)S(1)} %get-tuple-element.34.r_1_, f32[2,64,128]{2,1,0:T(8,128)S(1)} %get-tuple-element.40.r_2_), custom_call_target="tpu_custom_call" | custom-call | flops 905969664 | tf_op jit(solution)/shard_map/local/pallas_call | solution.py:340
  25.7 1.3 %rim.3 = (f32[36,64,128]{2,1,0:T(8,128)S(1)}, f32[2,32,128]{2,1,0:T(8,128)S(1)}, f32[6,64,128]{2,1,0:T(8,128)S(1)}, f32[6,64,128]{2,1,0:T(8,128)S(1)}, f32[6,64,...) custom-call(f32[10,32,128]{2,1,0:T(8,128)S(1)} %get-tuple-element.33.r_3_.r, ...), custom_call_target="tpu_custom_call" | custom-call | flops 603979776 | tf_op jit(solution)/shard_map/rim/pallas_call | solution.py:347
  26.9 1.5 %collective-permute-start.5 = (f32[6,64,128]{2,1,0:T(8,128)S(1)}, f32[6,64,128]{2,1,0:T(8,128)S(1)}, u32[]{:S(2)}, u32[]{:S(2)}) collective-permute-start(f32[6,64,128]{2,1,0:T(8,128)S(1)} %get-tuple-element.45), channel_id=1, source_target_pairs={{0,16},{1,17},{2,18},{3,19},{4,20},{5,21},{6,22},{7,23},{8,24},{9,... | collective-permute-start | bytes 589832 | tf_op jit(solution)/shard_map/ppermute | solution.py:288
  28.4 3.6 %collective-permute-start.6 = (f32[6,64,128]{2,1,0:T(8,128)S(1)}, f32[6,64,128]{2,1,0:T(8,128)S(1)}, u32[]{:S(2)}, u32[]{:S(2)}) collective-permute-start(f32[6,64,128]{2,1,0:T(8,128)S(1)} %get-tuple-element.46), channel_id=1, source_target_pairs={{0,112},{1,113},{2,114},{3,115},{4,116},{5,117},{6,118},{7,119},{8... | collective-permute-start | bytes 589832 | tf_op jit(solution)/shard_map/ppermute | solution.py:288
  32.1 2.3 %collective-permute-start.7 = (f32[6,64,128]{2,1,0:T(8,128)S(1)}, f32[6,64,128]{2,1,0:T(8,128)S(1)}, u32[]{:S(2)}, u32[]{:S(2)}) collective-permute-start(f32[6,64,128]{2,1,0:T(8,128)S(1)} %get-tuple-element.47), channel_id=1, source_target_pairs={{0,15},{1,2},{2,1},{3,4},{4,3},{5,6},{6,5},{7,8},{8,7},{9,10},{10,... | collective-permute-start | bytes 589832 | tf_op jit(solution)/shard_map/ppermute | solution.py:288
  34.4 5.1 %collective-permute-start.9 = (f32[1,64,128]{2,1,0:T(8,128)S(1)}, f32[1,64,128]{2,1,0:T(8,128)S(1)}, u32[]{:S(2)}, u32[]{:S(2)}) collective-permute-start(f32[1,64,128]{2,1,0:T(8,128)S(1)} %get-tuple-element.49), channel_id=1, source_target_pairs={{0,127},{1,114},{2,113},{3,116},{4,115},{5,118},{6,117},{7,120},{8... | collective-permute-start | bytes 98312 | tf_op jit(solution)/shard_map/ppermute | solution.py:288
  39.4 2.5 %inner.4 = (f32[16,64,128]{2,1,0:T(8,128)S(1)}, f32[2,32,128]{2,1,0:T(8,128)S(1)}) custom-call(f32[36,64,128]{2,1,0:T(8,128)S(1)} %get-tuple-element.42.r_0_.r_4_.r_3_, bf16[36,1152,256]{2,1,0:T(8,128)(2,1)S(1)} %get-tuple-element.34.r_1_, f32[36,64,128]{2,1,0:T(8,128)S(1)} %bitcast.10, f32[36,64,128]{2,1,0:T(8,128)S(1)} %bitcast.11, ...), custom_call_target="tpu_custom_call" | custom-call | flops 1207959552 | tf_op jit(solution)/shard_map/inner/pallas_call | solution.py:334
  41.9 0.6 collective-permute-done.9.high.r_12_
  42.5 3.3 %collective-permute-start.10 = (f32[8,64,128]{2,1,0:T(8,128)S(1)}, f32[8,64,128]{2,1,0:T(8,128)S(1)}, u32[]{:S(2)}, u32[]{:S(2)}) collective-permute-start(f32[8,64,128]{2,1,0:T(8,128)S(1)} %pack_close.2.r_2_), channel_id=1, source_target_pairs={{0,1},{1,0},{2,3},{3,2},{4,5},{5,4},{6,7},{7,6},{8,9},{9,8},{10,11... | collective-permute-start | bytes 786440 | tf_op jit(solution)/shard_map/ppermute | solution.py:288
  45.8 1.1 %local.4.r_6_ = f32[20,64,128]{2,1,0:T(8,128)S(1)} custom-call(f32[36,64,128]{2,1,0:T(8,128)S(1)} %get-tuple-element.42.r_0_.r_4_.r_3_, bf16[36,1152,256]{2,1,0:T(8,128)(2,1)S(1)} %get-tuple-element.34.r_1_, f32[8,64,128]{2,1,0:T(8,128)S(1)} %pack_close.2.r_2_), custom_call_target="tpu_custom_call" | custom-call | flops 905969664 | tf_op jit(solution)/shard_map/local/pallas_call | solution.py:340
  47.0 1.3 %rim.4 = (f32[36,64,128]{2,1,0:T(8,128)S(1)}, f32[2,32,128]{2,1,0:T(8,128)S(1)}, f32[6,64,128]{2,1,0:T(8,128)S(1)}, f32[6,64,128]{2,1,0:T(8,128)S(1)}, f32[6,64,...) custom-call(f32[10,32,128]{2,1,0:T(8,128)S(1)} %get-tuple-element.33.r_3_.r, ...), custom_call_target="tpu_custom_call" | custom-call | flops 603979776 | tf_op jit(solution)/shard_map/rim/pallas_call | solution.py:347
  48.3 2.3 %collective-permute-start.11 = (f32[6,64,128]{2,1,0:T(8,128)S(1)}, f32[6,64,128]{2,1,0:T(8,128)S(1)}, u32[]{:S(2)}, u32[]{:S(2)}) collective-permute-start(f32[6,64,128]{2,1,0:T(8,128)S(1)} %get-tuple-element.54), channel_id=1, source_target_pairs={{0,16},{1,17},{2,18},{3,19},{4,20},{5,21},{6,22},{7,23},{8,24},{9,... | collective-permute-start | bytes 589832 | tf_op jit(solution)/shard_map/ppermute | solution.py:288
  50.6 2.9 %collective-permute-start.12 = (f32[6,64,128]{2,1,0:T(8,128)S(1)}, f32[6,64,128]{2,1,0:T(8,128)S(1)}, u32[]{:S(2)}, u32[]{:S(2)}) collective-permute-start(f32[6,64,128]{2,1,0:T(8,128)S(1)} %get-tuple-element.55), channel_id=1, source_target_pairs={{0,112},{1,113},{2,114},{3,115},{4,116},{5,117},{6,118},{7,119},{8... | collective-permute-start | bytes 589832 | tf_op jit(solution)/shard_map/ppermute | solution.py:288
  53.5 0.5 collective-permute-start.13
  54.1 4.9 %collective-permute-start.15 = (f32[1,64,128]{2,1,0:T(8,128)S(1)}, f32[1,64,128]{2,1,0:T(8,128)S(1)}, u32[]{:S(2)}, u32[]{:S(2)}) collective-permute-start(f32[1,64,128]{2,1,0:T(8,128)S(1)} %get-tuple-element.58), channel_id=1, source_target_pairs={{0,127},{1,114},{2,113},{3,116},{4,115},{5,118},{6,117},{7,120},{8... | collective-permute-start | bytes 98312 | tf_op jit(solution)/shard_map/ppermute | solution.py:288
  59.0 2.5 %inner.5 = (f32[16,64,128]{2,1,0:T(8,128)S(1)}, f32[2,32,128]{2,1,0:T(8,128)S(1)}) custom-call(f32[36,64,128]{2,1,0:T(8,128)S(1)} %get-tuple-element.51.r_0_.r_4_, bf16[36,1152,256]{2,1,0:T(8,128)(2,1)S(1)} %get-tuple-element.34.r_1_, f32[36,64,128]{2,1,0:T(8,128)S(1)} %bitcast.14, f32[36,64,128]{2,1,0:T(8,128)S(1)} %get-tuple-element.42.r_0_.r_4_.r_3_, ...), custom_call_target="tpu_custom_call" | custom-call | flops 1207959552 | tf_op jit(solution)/shard_map/inner/pallas_call | solution.py:334
  61.5 0.2 collective-permute-done.14.low.r_11_
  61.7 2.7 %collective-permute-done.15.high.r_12_ = f32[1,64,128]{2,1,0:T(8,128)S(1)} collective-permute-done((f32[1,64,128]{2,1,0:T(8,128)S(1)}, f32[1,64,128]{2,1,0:T(8,128)S(1)}, u32[]{:S(2)}, u32[]{:S(2)}) %collective-permute-start.15) | collective-permute-done | bytes 32800 | tf_op jit(solution)/shard_map/ppermute | solution.py:288
  64.4 0.2 collective-permute-done.13.outer.r_9_
  64.6 1.0 %collective-permute-start.16 = (f32[8,64,128]{2,1,0:T(8,128)S(1)}, f32[8,64,128]{2,1,0:T(8,128)S(1)}, u32[]{:S(2)}, u32[]{:S(2)}) collective-permute-start(f32[8,64,128]{2,1,0:T(8,128)S(1)} %pack_close.3.r_2_), channel_id=1, source_target_pairs={{0,1},{1,0},{2,3},{3,2},{4,5},{5,4},{6,7},{7,6},{8,9},{9,8},{10,11... | collective-permute-start | bytes 786440 | tf_op jit(solution)/shard_map/ppermute | solution.py:288
  65.5 1.1 %local.5.r_6_ = f32[20,64,128]{2,1,0:T(8,128)S(1)} custom-call(f32[36,64,128]{2,1,0:T(8,128)S(1)} %get-tuple-element.51.r_0_.r_4_, bf16[36,1152,256]{2,1,0:T(8,128)(2,1)S(1)} %get-tuple-element.34.r_1_, f32[8,64,128]{2,1,0:T(8,128)S(1)} %pack_close.3.r_2_), custom_call_target="tpu_custom_call" | custom-call | flops 905969664 | tf_op jit(solution)/shard_map/local/pallas_call | solution.py:340
  66.7 2.2 %rim.5 = (f32[36,64,128]{2,1,0:T(8,128)}, f32[2,32,128]{2,1,0:T(8,128)S(1)}) custom-call(f32[10,32,128]{2,1,0:T(8,128)S(1)} %get-tuple-element.33.r_3_.r_0_, bf16[36,1152,256]{2,1,0:T(8,128)(2,1)S(1)} %get-tuple-element.34.r_1_, f32[36,64,128]{2,1,0:T(8,128)S(1)} %bitcast.15, f32[36,64,128]{2,1,0:T(8,128)S(1)} %get-tuple-element.42.r_0_.r_4_.r_3_, ...), custom_call_target="tpu_custom_call" | custom-call | flops 603979776 | tf_op jit(solution)/shard_map/rim/pallas_call | solution.py:347
  68.9 0.3 pack.1
  69.2 18.0 %all_to_all.5 = f32[128,2,128]{2,1,0:T(2,128)S(1)} all-to-all(f32[128,2,128]{2,1,0:T(2,128)S(1)} %pack.1), channel_id=1, replica_groups=mesh['gx'=8,'gy'=16] {'gx','gy'}, dimensions={0} | all-to-all | bytes 262144 | tf_op jit(solution)/shard_map/all_to_all | solution.py:390
  87.4 0.6 slice.8
  (29 shorter events, 0.6 us)
Async XLA Ops:
  0.6 9.6 %copy-start.3 = (f32[2]{0:T(128)S(1)}, f32[2]{0:T(128)}, u32[]{:S(2)}) copy-start(f32[2]{0:T(128)} %r_0_.2) | copy-start | bytes 28
  0.6 9.5 %copy-start.2 = (s32[6,6]{1,0:T(8,128)S(1)}, s32[6,6]{1,0:T(8,128)}, u32[]{:S(2)}) copy-start(s32[6,6]{1,0:T(8,128)} %r_2_.1) | copy-start | bytes 436
  0.7 9.5 %copy-start.1 = (s32[6,6,9]{2,1,0:T(8,128)S(1)}, s32[6,6,9]{2,1,0:T(8,128)}, u32[]{:S(2)}) copy-start(s32[6,6,9]{2,1,0:T(8,128)} %r_1_.1) | copy-start | bytes 3892
  1.8 17.3 %collective-permute-start.1 = (f32[6,64,128]{2,1,0:T(8,128)S(1)}, f32[6,64,128]{2,1,0:T(8,128)S(1)}, u32[]{:S(2)}, u32[]{:S(2)}) collective-permute-start(f32[6,64,128]{2,1,0:T(8,128)S(1)} %get-tuple-element.38), channel_id=1, source_target_pairs={{0,16},{1,17},{2,18},{3,19},{4,20},{5,21},{6,22},{7,23},{8,24},{9,... | collective-permute-start | bytes 589832 | tf_op jit(solution)/shard_map/ppermute | solution.py:288
  5.6 13.5 %collective-permute-start.2 = (f32[6,64,128]{2,1,0:T(8,128)S(1)}, f32[6,64,128]{2,1,0:T(8,128)S(1)}, u32[]{:S(2)}, u32[]{:S(2)}) collective-permute-start(f32[6,64,128]{2,1,0:T(8,128)S(1)} %get-tuple-element.39), channel_id=1, source_target_pairs={{0,112},{1,113},{2,114},{3,115},{4,116},{5,117},{6,118},{7,119},{8... | collective-permute-start | bytes 589832 | tf_op jit(solution)/shard_map/ppermute | solution.py:288
  7.9 14.1 %collective-permute-start = (f32[6,64,128]{2,1,0:T(8,128)S(1)}, f32[6,64,128]{2,1,0:T(8,128)S(1)}, u32[]{:S(2)}, u32[]{:S(2)}) collective-permute-start(f32[6,64,128]{2,1,0:T(8,128)S(1)} %get-tuple-element.35), channel_id=1, source_target_pairs={{0,15},{1,2},{2,1},{3,4},{4,3},{5,6},{6,5},{7,8},{8,7},{9,10},{10,... | collective-permute-start | bytes 589832 | tf_op jit(solution)/shard_map/ppermute | solution.py:288
  10.2 8.9 %copy-start = (f32[6,6,64,128]{3,2,1,0:T(8,128)S(1)}, f32[6,6,64,128]{3,2,1,0:T(8,128)}, u32[]{:S(2)}) copy-start(f32[6,6,64,128]{3,2,1,0:T(8,128)} %r_0_.3) | copy-start | bytes 3538948
  19.1 6.5 %collective-permute-start.3 = (f32[8,64,128]{2,1,0:T(8,128)S(1)}, f32[8,64,128]{2,1,0:T(8,128)S(1)}, u32[]{:S(2)}, u32[]{:S(2)}) collective-permute-start(f32[8,64,128]{2,1,0:T(8,128)S(1)} %get-tuple-element.41), channel_id=1, source_target_pairs={{0,1},{1,0},{2,3},{3,2},{4,5},{5,4},{6,7},{7,6},{8,9},{9,8},{10,11... | collective-permute-start | bytes 786440 | tf_op jit(solution)/shard_map/ppermute | solution.py:288
  22.0 3.7 %collective-permute-start.4 = (f32[2,64,128]{2,1,0:T(8,128)S(1)}, f32[2,64,128]{2,1,0:T(8,128)S(1)}, u32[]{:S(2)}, u32[]{:S(2)}) collective-permute-start(f32[2,64,128]{2,1,0:T(8,128)S(1)} %get-tuple-element.40.r_2_), channel_id=1, source_target_pairs={{0,15},{1,2},{2,1},{3,4},{4,3},{5,6},{6,5},{7,8},{8,7},{9,10},{10,... | collective-permute-start | bytes 196616 | tf_op jit(solution)/shard_map/ppermute | solution.py:288
  26.9 15.6 %collective-permute-start.5 = (f32[6,64,128]{2,1,0:T(8,128)S(1)}, f32[6,64,128]{2,1,0:T(8,128)S(1)}, u32[]{:S(2)}, u32[]{:S(2)}) collective-permute-start(f32[6,64,128]{2,1,0:T(8,128)S(1)} %get-tuple-element.45), channel_id=1, source_target_pairs={{0,16},{1,17},{2,18},{3,19},{4,20},{5,21},{6,22},{7,23},{8,24},{9,... | collective-permute-start | bytes 589832 | tf_op jit(solution)/shard_map/ppermute | solution.py:288
  28.4 14.1 %collective-permute-start.6 = (f32[6,64,128]{2,1,0:T(8,128)S(1)}, f32[6,64,128]{2,1,0:T(8,128)S(1)}, u32[]{:S(2)}, u32[]{:S(2)}) collective-permute-start(f32[6,64,128]{2,1,0:T(8,128)S(1)} %get-tuple-element.46), channel_id=1, source_target_pairs={{0,112},{1,113},{2,114},{3,115},{4,116},{5,117},{6,118},{7,119},{8... | collective-permute-start | bytes 589832 | tf_op jit(solution)/shard_map/ppermute | solution.py:288
  32.1 10.4 %collective-permute-start.7 = (f32[6,64,128]{2,1,0:T(8,128)S(1)}, f32[6,64,128]{2,1,0:T(8,128)S(1)}, u32[]{:S(2)}, u32[]{:S(2)}) collective-permute-start(f32[6,64,128]{2,1,0:T(8,128)S(1)} %get-tuple-element.47), channel_id=1, source_target_pairs={{0,15},{1,2},{2,1},{3,4},{4,3},{5,6},{6,5},{7,8},{8,7},{9,10},{10,... | collective-permute-start | bytes 589832 | tf_op jit(solution)/shard_map/ppermute | solution.py:288
  34.3 7.6 %collective-permute-start.8 = (f32[1,64,128]{2,1,0:T(8,128)S(1)}, f32[1,64,128]{2,1,0:T(8,128)S(1)}, u32[]{:S(2)}, u32[]{:S(2)}) collective-permute-start(f32[1,64,128]{2,1,0:T(8,128)S(1)} %get-tuple-element.48), channel_id=1, source_target_pairs={{0,31},{1,18},{2,17},{3,20},{4,19},{5,22},{6,21},{7,24},{8,23},{9,... | collective-permute-start | bytes 98312 | tf_op jit(solution)/shard_map/ppermute | solution.py:288
  34.4 8.1 %collective-permute-start.9 = (f32[1,64,128]{2,1,0:T(8,128)S(1)}, f32[1,64,128]{2,1,0:T(8,128)S(1)}, u32[]{:S(2)}, u32[]{:S(2)}) collective-permute-start(f32[1,64,128]{2,1,0:T(8,128)S(1)} %get-tuple-element.49), channel_id=1, source_target_pairs={{0,127},{1,114},{2,113},{3,116},{4,115},{5,118},{6,117},{7,120},{8... | collective-permute-start | bytes 98312 | tf_op jit(solution)/shard_map/ppermute | solution.py:288
  42.5 4.5 %collective-permute-start.10 = (f32[8,64,128]{2,1,0:T(8,128)S(1)}, f32[8,64,128]{2,1,0:T(8,128)S(1)}, u32[]{:S(2)}, u32[]{:S(2)}) collective-permute-start(f32[8,64,128]{2,1,0:T(8,128)S(1)} %pack_close.2.r_2_), channel_id=1, source_target_pairs={{0,1},{1,0},{2,3},{3,2},{4,5},{5,4},{6,7},{7,6},{8,9},{9,8},{10,11... | collective-permute-start | bytes 786440 | tf_op jit(solution)/shard_map/ppermute | solution.py:288
  48.3 16.1 %collective-permute-start.11 = (f32[6,64,128]{2,1,0:T(8,128)S(1)}, f32[6,64,128]{2,1,0:T(8,128)S(1)}, u32[]{:S(2)}, u32[]{:S(2)}) collective-permute-start(f32[6,64,128]{2,1,0:T(8,128)S(1)} %get-tuple-element.54), channel_id=1, source_target_pairs={{0,16},{1,17},{2,18},{3,19},{4,20},{5,21},{6,22},{7,23},{8,24},{9,... | collective-permute-start | bytes 589832 | tf_op jit(solution)/shard_map/ppermute | solution.py:288
  50.6 13.8 %collective-permute-start.12 = (f32[6,64,128]{2,1,0:T(8,128)S(1)}, f32[6,64,128]{2,1,0:T(8,128)S(1)}, u32[]{:S(2)}, u32[]{:S(2)}) collective-permute-start(f32[6,64,128]{2,1,0:T(8,128)S(1)} %get-tuple-element.55), channel_id=1, source_target_pairs={{0,112},{1,113},{2,114},{3,115},{4,116},{5,117},{6,118},{7,119},{8... | collective-permute-start | bytes 589832 | tf_op jit(solution)/shard_map/ppermute | solution.py:288
  53.5 11.1 %collective-permute-start.13 = (f32[6,64,128]{2,1,0:T(8,128)S(1)}, f32[6,64,128]{2,1,0:T(8,128)S(1)}, u32[]{:S(2)}, u32[]{:S(2)}) collective-permute-start(f32[6,64,128]{2,1,0:T(8,128)S(1)} %get-tuple-element.56), channel_id=1, source_target_pairs={{0,15},{1,2},{2,1},{3,4},{4,3},{5,6},{6,5},{7,8},{8,7},{9,10},{10,... | collective-permute-start | bytes 589832 | tf_op jit(solution)/shard_map/ppermute | solution.py:288
  54.0 7.8 %collective-permute-start.14 = (f32[1,64,128]{2,1,0:T(8,128)S(1)}, f32[1,64,128]{2,1,0:T(8,128)S(1)}, u32[]{:S(2)}, u32[]{:S(2)}) collective-permute-start(f32[1,64,128]{2,1,0:T(8,128)S(1)} %get-tuple-element.57), channel_id=1, source_target_pairs={{0,31},{1,18},{2,17},{3,20},{4,19},{5,22},{6,21},{7,24},{8,23},{9,... | collective-permute-start | bytes 98312 | tf_op jit(solution)/shard_map/ppermute | solution.py:288
  54.1 10.3 %collective-permute-start.15 = (f32[1,64,128]{2,1,0:T(8,128)S(1)}, f32[1,64,128]{2,1,0:T(8,128)S(1)}, u32[]{:S(2)}, u32[]{:S(2)}) collective-permute-start(f32[1,64,128]{2,1,0:T(8,128)S(1)} %get-tuple-element.58), channel_id=1, source_target_pairs={{0,127},{1,114},{2,113},{3,116},{4,115},{5,118},{6,117},{7,120},{8... | collective-permute-start | bytes 98312 | tf_op jit(solution)/shard_map/ppermute | solution.py:288
  64.6 2.1 %collective-permute-start.16 = (f32[8,64,128]{2,1,0:T(8,128)S(1)}, f32[8,64,128]{2,1,0:T(8,128)S(1)}, u32[]{:S(2)}, u32[]{:S(2)}) collective-permute-start(f32[8,64,128]{2,1,0:T(8,128)S(1)} %pack_close.3.r_2_), channel_id=1, source_target_pairs={{0,1},{1,0},{2,3},{3,2},{4,5},{5,4},{6,7},{7,6},{8,9},{9,8},{10,11... | collective-permute-start | bytes 786440 | tf_op jit(solution)/shard_map/ppermute | solution.py:288

commit v4 on v3

--- a/solution.py
+++ b/solution.py
@@ -22,6 +22,19 @@
     for load in loads:
         load.start()
     me_x, me_y = lax.axis_index("gx"), lax.axis_index("gy")
+
+    wrap_left = jnp.where(me_x == 0, -1.0, 0.0)
+    wrap_right = jnp.where(me_x == sizes[0] - 1, 1.0, 0.0)
+    wrap_low = jnp.where(me_y == 0, -1.0, 0.0)
+    wrap_high = jnp.where(me_y == sizes[1] - 1, 1.0, 0.0)
+    wrap_outer = jnp.where(me_y % 2 == 1, wrap_high, wrap_low)
+    zero = jnp.zeros_like(wrap_outer)
+    sides = [(wrap_left, zero), (wrap_right, zero), (zero, wrap_outer)]
+    sides += [(wrap_left, wrap_outer), (wrap_right, wrap_outer)]
+    for k, (along_x, along_y) in enumerate(sides):
+        angle = jnp.full(turn.shape[1:], kpoint[0] * along_x + kpoint[1] * along_y, F32)
+        turn[2 * k] = jnp.cos(angle)
+        turn[2 * k + 1] = jnp.sin(angle)
 
     reach = 20
     scale = -(-(1 << reach) // total_y)
@@ -47,20 +60,7 @@
             out[i, pl.ds(row, block), block : 2 * block] = (value - high.astype(F32)).astype(BF16)
         return carry
 
-    lax.fori_loop(0, cells, body, 0)
-
-    wrap_left = jnp.where(me_x == 0, -1.0, 0.0)
-    wrap_right = jnp.where(me_x == sizes[0] - 1, 1.0, 0.0)
-    wrap_low = jnp.where(me_y == 0, -1.0, 0.0)
-    wrap_high = jnp.where(me_y == sizes[1] - 1, 1.0, 0.0)
-    wrap_outer = jnp.where(me_y % 2 == 1, wrap_high, wrap_low)
-    zero = jnp.zeros_like(wrap_outer)
-    sides = [(wrap_left, zero), (wrap_right, zero), (zero, wrap_outer)]
-    sides += [(wrap_left, wrap_outer), (wrap_right, wrap_outer)]
-    for k, (along_x, along_y) in enumerate(sides):
-        angle = jnp.full(turn.shape[1:], kpoint[0] * along_x + kpoint[1] * along_y, F32)
-        turn[2 * k] = jnp.cos(angle)
-        turn[2 * k + 1] = jnp.sin(angle)
+    lax.fori_loop(0, cells, body, 0, unroll=2)
 
 
 def put(ext, x, y, value):

time: 88.2 us -> 88.2 us (level)
  no operation moved by 1% of the time
where the time goes in v4:
time: 88.2 us; the launch traced here: 88 us
  starting transfers between devices  38.6 us (44%)
  Pallas kernels  25.7 us (29%)
  blocking collectives  18 us (20%)
  waiting for transfers between devices  4.1 us (5%)
    ppermute x17, starting transfers between devices, send(): return lax.ppermute(value, AXES, move)  38.6 us
    all_to_all x1, blocking collectives, shards(): total = jnp.sum(lax.all_to_all(spread, AXES, 0, 0), axis=0).reshape(-1)  18 us
    pallas_call x1, Pallas kernels, shards(): pl.pallas_call(lambda *r: split_kernel(sizes, shape, *r), out_shape=[jax....  8.64 us
    pallas_call x3, Pallas kernels, inner(): call(lambda *r: inner_kernel(first, shape, *r), 5, [inner_shape, sums_sha...  7.46 us
    pallas_call x3, Pallas kernels, outside(): call(lambda *r: rim_kernel(first, shape, *r), 7 + len(halo), outs, 6, 'ri...  4.7 us
    ppermute x17, waiting for transfers between devices, send(): return lax.ppermute(value, AXES, move)  4.1 us
    pallas_call x3, Pallas kernels, local(): call(lambda *r: local_kernel(shape, *r), 3, [cells_shape(rim)], 6, 'local...  3.41 us
  transfers between devices with their start and end apart: 17, of which 5 were waited for; matrix products, arithmetic and copies ran while one was open for 0% of the time, Pallas kernels for 22%

profile of v4, /device:TPU:1, one launch (start us, length us, event | category | flops | bytes accessed | tf_op | source)
XLA Modules:
  0.0 88.0 jit_solution(5158978168951457990)
XLA Ops:
  0.7 1.1 %edges.1 = (f32[6,64,128]{2,1,0:T(8,128)S(1)}, f32[6,64,128]{2,1,0:T(8,128)S(1)}, f32[6,64,128]{2,1,0:T(8,128)S(1)}) custom-call(f32[6,6,64,128]{3,2,1,0:T(8,128)} %r_0_.3), custom_call_target="tpu_custom_call" | custom-call | tf_op jit(solution)/shard_map/edges/pallas_call | solution.py:306
  1.8 3.8 %collective-permute-start.1 = (f32[6,64,128]{2,1,0:T(8,128)S(1)}, f32[6,64,128]{2,1,0:T(8,128)S(1)}, u32[]{:S(2)}, u32[]{:S(2)}) collective-permute-start(f32[6,64,128]{2,1,0:T(8,128)S(1)} %get-tuple-element.38), channel_id=1, source_target_pairs={{0,16},{1,17},{2,18},{3,19},{4,20},{5,21},{6,22},{7,23},{8,24},{9,... | collective-permute-start | bytes 589832 | tf_op jit(solution)/shard_map/ppermute | solution.py:288
  5.6 2.3 %collective-permute-start.2 = (f32[6,64,128]{2,1,0:T(8,128)S(1)}, f32[6,64,128]{2,1,0:T(8,128)S(1)}, u32[]{:S(2)}, u32[]{:S(2)}) collective-permute-start(f32[6,64,128]{2,1,0:T(8,128)S(1)} %get-tuple-element.39), channel_id=1, source_target_pairs={{0,112},{1,113},{2,114},{3,115},{4,116},{5,117},{6,118},{7,119},{8... | collective-permute-start | bytes 589832 | tf_op jit(solution)/shard_map/ppermute | solution.py:288
  7.9 2.3 %collective-permute-start = (f32[6,64,128]{2,1,0:T(8,128)S(1)}, f32[6,64,128]{2,1,0:T(8,128)S(1)}, u32[]{:S(2)}, u32[]{:S(2)}) collective-permute-start(f32[6,64,128]{2,1,0:T(8,128)S(1)} %get-tuple-element.35), channel_id=1, source_target_pairs={{0,15},{1,2},{2,1},{3,4},{4,3},{5,6},{6,5},{7,8},{8,7},{9,10},{10,... | collective-permute-start | bytes 589832 | tf_op jit(solution)/shard_map/ppermute | solution.py:288
  10.2 8.6 %split.1 = (bf16[36,1152,256]{2,1,0:T(8,128)(2,1)S(1)}, f32[10,32,128]{2,1,0:T(8,128)S(1)}) custom-call(f32[2]{0:T(128)S(1)} %copy-done.3, s32[6,6,9]{2,1,0:T(8,128)S(1)} %copy-done.1, s32[6,6]{1,0:T(8,128)S(1)} %copy-done.2, f32[36,9,128,128]{3,2,1,0:T(8,128)} %bitcast.16), custom_call_target="tpu_custom_call" | custom-call | flops 21233664 | bytes 42467328 | tf_op jit(solution)/shard_map/split/pallas_call | solution.py:314
  18.9 2.8 %collective-permute-start.3 = (f32[8,64,128]{2,1,0:T(8,128)S(1)}, f32[8,64,128]{2,1,0:T(8,128)S(1)}, u32[]{:S(2)}, u32[]{:S(2)}) collective-permute-start(f32[8,64,128]{2,1,0:T(8,128)S(1)} %get-tuple-element.41), channel_id=1, source_target_pairs={{0,1},{1,0},{2,3},{3,2},{4,5},{5,4},{6,7},{7,6},{8,9},{9,8},{10,11... | collective-permute-start | bytes 786440 | tf_op jit(solution)/shard_map/ppermute | solution.py:288
  21.8 2.5 %inner.3 = (f32[16,64,128]{2,1,0:T(8,128)S(1)}, f32[2,32,128]{2,1,0:T(8,128)S(1)}) custom-call(f32[36,64,128]{2,1,0:T(8,128)S(1)} %bitcast.4, bf16[36,1152,256]{2,1,0:T(8,128)(2,1)S(1)} %get-tuple-element.34.r_1_, f32[36,64,128]{2,1,0:T(8,128)S(1)} %bitcast.5, f32[36,64,128]{2,1,0:T(8,128)S(1)} %bitcast.6, f32[6,64,128]{2,1,0:T(8,128)S(1)} %collective-permute-done.r_4_.r_9_), custom_call_target="tpu_custom_call" | custom-call | flops 1207959552 | tf_op jit(solution)/shard_map/inner/pallas_call | solution.py:334
  24.2 1.1 %local.3.r_6_ = f32[20,64,128]{2,1,0:T(8,128)S(1)} custom-call(f32[36,64,128]{2,1,0:T(8,128)S(1)} %bitcast.7, bf16[36,1152,256]{2,1,0:T(8,128)(2,1)S(1)} %get-tuple-element.34.r_1_, f32[2,64,128]{2,1,0:T(8,128)S(1)} %get-tuple-element.40.r_2_), custom_call_target="tpu_custom_call" | custom-call | flops 905969664 | tf_op jit(solution)/shard_map/local/pallas_call | solution.py:340
  25.4 1.3 %rim.3 = (f32[36,64,128]{2,1,0:T(8,128)S(1)}, f32[2,32,128]{2,1,0:T(8,128)S(1)}, f32[6,64,128]{2,1,0:T(8,128)S(1)}, f32[6,64,128]{2,1,0:T(8,128)S(1)}, f32[6,64,...) custom-call(f32[10,32,128]{2,1,0:T(8,128)S(1)} %get-tuple-element.33.r_3_.r, ...), custom_call_target="tpu_custom_call" | custom-call | flops 603979776 | tf_op jit(solution)/shard_map/rim/pallas_call | solution.py:347
  26.7 1.7 %collective-permute-start.5 = (f32[6,64,128]{2,1,0:T(8,128)S(1)}, f32[6,64,128]{2,1,0:T(8,128)S(1)}, u32[]{:S(2)}, u32[]{:S(2)}) collective-permute-start(f32[6,64,128]{2,1,0:T(8,128)S(1)} %get-tuple-element.45), channel_id=1, source_target_pairs={{0,16},{1,17},{2,18},{3,19},{4,20},{5,21},{6,22},{7,23},{8,24},{9,... | collective-permute-start | bytes 589832 | tf_op jit(solution)/shard_map/ppermute | solution.py:288
  28.4 3.4 %collective-permute-start.6 = (f32[6,64,128]{2,1,0:T(8,128)S(1)}, f32[6,64,128]{2,1,0:T(8,128)S(1)}, u32[]{:S(2)}, u32[]{:S(2)}) collective-permute-start(f32[6,64,128]{2,1,0:T(8,128)S(1)} %get-tuple-element.46), channel_id=1, source_target_pairs={{0,112},{1,113},{2,114},{3,115},{4,116},{5,117},{6,118},{7,119},{8... | collective-permute-start | bytes 589832 | tf_op jit(solution)/shard_map/ppermute | solution.py:288
  31.9 2.3 %collective-permute-start.7 = (f32[6,64,128]{2,1,0:T(8,128)S(1)}, f32[6,64,128]{2,1,0:T(8,128)S(1)}, u32[]{:S(2)}, u32[]{:S(2)}) collective-permute-start(f32[6,64,128]{2,1,0:T(8,128)S(1)} %get-tuple-element.47), channel_id=1, source_target_pairs={{0,15},{1,2},{2,1},{3,4},{4,3},{5,6},{6,5},{7,8},{8,7},{9,10},{10,... | collective-permute-start | bytes 589832 | tf_op jit(solution)/shard_map/ppermute | solution.py:288
  34.1 5.1 %collective-permute-start.9 = (f32[1,64,128]{2,1,0:T(8,128)S(1)}, f32[1,64,128]{2,1,0:T(8,128)S(1)}, u32[]{:S(2)}, u32[]{:S(2)}) collective-permute-start(f32[1,64,128]{2,1,0:T(8,128)S(1)} %get-tuple-element.49), channel_id=1, source_target_pairs={{0,127},{1,114},{2,113},{3,116},{4,115},{5,118},{6,117},{7,120},{8... | collective-permute-start | bytes 98312 | tf_op jit(solution)/shard_map/ppermute | solution.py:288
  39.2 2.5 %inner.4 = (f32[16,64,128]{2,1,0:T(8,128)S(1)}, f32[2,32,128]{2,1,0:T(8,128)S(1)}) custom-call(f32[36,64,128]{2,1,0:T(8,128)S(1)} %get-tuple-element.42.r_0_.r_4_.r_3_, bf16[36,1152,256]{2,1,0:T(8,128)(2,1)S(1)} %get-tuple-element.34.r_1_, f32[36,64,128]{2,1,0:T(8,128)S(1)} %bitcast.10, f32[36,64,128]{2,1,0:T(8,128)S(1)} %bitcast.11, ...), custom_call_target="tpu_custom_call" | custom-call | flops 1207959552 | tf_op jit(solution)/shard_map/inner/pallas_call | solution.py:334
  41.7 0.8 collective-permute-done.9.high.r_12_
  42.5 3.1 %collective-permute-start.10 = (f32[8,64,128]{2,1,0:T(8,128)S(1)}, f32[8,64,128]{2,1,0:T(8,128)S(1)}, u32[]{:S(2)}, u32[]{:S(2)}) collective-permute-start(f32[8,64,128]{2,1,0:T(8,128)S(1)} %pack_close.2.r_2_), channel_id=1, source_target_pairs={{0,1},{1,0},{2,3},{3,2},{4,5},{5,4},{6,7},{7,6},{8,9},{9,8},{10,11... | collective-permute-start | bytes 786440 | tf_op jit(solution)/shard_map/ppermute | solution.py:288
  45.6 1.1 %local.4.r_6_ = f32[20,64,128]{2,1,0:T(8,128)S(1)} custom-call(f32[36,64,128]{2,1,0:T(8,128)S(1)} %get-tuple-element.42.r_0_.r_4_.r_3_, bf16[36,1152,256]{2,1,0:T(8,128)(2,1)S(1)} %get-tuple-element.34.r_1_, f32[8,64,128]{2,1,0:T(8,128)S(1)} %pack_close.2.r_2_), custom_call_target="tpu_custom_call" | custom-call | flops 905969664 | tf_op jit(solution)/shard_map/local/pallas_call | solution.py:340
  46.8 1.3 %rim.4 = (f32[36,64,128]{2,1,0:T(8,128)S(1)}, f32[2,32,128]{2,1,0:T(8,128)S(1)}, f32[6,64,128]{2,1,0:T(8,128)S(1)}, f32[6,64,128]{2,1,0:T(8,128)S(1)}, f32[6,64,...) custom-call(f32[10,32,128]{2,1,0:T(8,128)S(1)} %get-tuple-element.33.r_3_.r, ...), custom_call_target="tpu_custom_call" | custom-call | flops 603979776 | tf_op jit(solution)/shard_map/rim/pallas_call | solution.py:347
  48.0 2.5 %collective-permute-start.11 = (f32[6,64,128]{2,1,0:T(8,128)S(1)}, f32[6,64,128]{2,1,0:T(8,128)S(1)}, u32[]{:S(2)}, u32[]{:S(2)}) collective-permute-start(f32[6,64,128]{2,1,0:T(8,128)S(1)} %get-tuple-element.54), channel_id=1, source_target_pairs={{0,16},{1,17},{2,18},{3,19},{4,20},{5,21},{6,22},{7,23},{8,24},{9,... | collective-permute-start | bytes 589832 | tf_op jit(solution)/shard_map/ppermute | solution.py:288
  50.6 2.9 %collective-permute-start.12 = (f32[6,64,128]{2,1,0:T(8,128)S(1)}, f32[6,64,128]{2,1,0:T(8,128)S(1)}, u32[]{:S(2)}, u32[]{:S(2)}) collective-permute-start(f32[6,64,128]{2,1,0:T(8,128)S(1)} %get-tuple-element.55), channel_id=1, source_target_pairs={{0,112},{1,113},{2,114},{3,115},{4,116},{5,117},{6,118},{7,119},{8... | collective-permute-start | bytes 589832 | tf_op jit(solution)/shard_map/ppermute | solution.py:288
  53.5 0.5 collective-permute-start.13
  54.1 4.9 %collective-permute-start.15 = (f32[1,64,128]{2,1,0:T(8,128)S(1)}, f32[1,64,128]{2,1,0:T(8,128)S(1)}, u32[]{:S(2)}, u32[]{:S(2)}) collective-permute-start(f32[1,64,128]{2,1,0:T(8,128)S(1)} %get-tuple-element.58), channel_id=1, source_target_pairs={{0,127},{1,114},{2,113},{3,116},{4,115},{5,118},{6,117},{7,120},{8... | collective-permute-start | bytes 98312 | tf_op jit(solution)/shard_map/ppermute | solution.py:288
  59.0 2.5 %inner.5 = (f32[16,64,128]{2,1,0:T(8,128)S(1)}, f32[2,32,128]{2,1,0:T(8,128)S(1)}) custom-call(f32[36,64,128]{2,1,0:T(8,128)S(1)} %get-tuple-element.51.r_0_.r_4_, bf16[36,1152,256]{2,1,0:T(8,128)(2,1)S(1)} %get-tuple-element.34.r_1_, f32[36,64,128]{2,1,0:T(8,128)S(1)} %bitcast.14, f32[36,64,128]{2,1,0:T(8,128)S(1)} %get-tuple-element.42.r_0_.r_4_.r_3_, ...), custom_call_target="tpu_custom_call" | custom-call | flops 1207959552 | tf_op jit(solution)/shard_map/inner/pallas_call | solution.py:334
  61.5 0.2 collective-permute-done.14.low.r_11_
  61.7 2.6 %collective-permute-done.15.high.r_12_ = f32[1,64,128]{2,1,0:T(8,128)S(1)} collective-permute-done((f32[1,64,128]{2,1,0:T(8,128)S(1)}, f32[1,64,128]{2,1,0:T(8,128)S(1)}, u32[]{:S(2)}, u32[]{:S(2)}) %collective-permute-start.15) | collective-permute-done | bytes 32800 | tf_op jit(solution)/shard_map/ppermute | solution.py:288
  64.4 0.3 collective-permute-done.13.outer.r_9_
  64.7 0.8 collective-permute-start.16
  65.5 1.1 %local.5.r_6_ = f32[20,64,128]{2,1,0:T(8,128)S(1)} custom-call(f32[36,64,128]{2,1,0:T(8,128)S(1)} %get-tuple-element.51.r_0_.r_4_, bf16[36,1152,256]{2,1,0:T(8,128)(2,1)S(1)} %get-tuple-element.34.r_1_, f32[8,64,128]{2,1,0:T(8,128)S(1)} %pack_close.3.r_2_), custom_call_target="tpu_custom_call" | custom-call | flops 905969664 | tf_op jit(solution)/shard_map/local/pallas_call | solution.py:340
  66.7 2.2 %rim.5 = (f32[36,64,128]{2,1,0:T(8,128)}, f32[2,32,128]{2,1,0:T(8,128)S(1)}) custom-call(f32[10,32,128]{2,1,0:T(8,128)S(1)} %get-tuple-element.33.r_3_.r_0_, bf16[36,1152,256]{2,1,0:T(8,128)(2,1)S(1)} %get-tuple-element.34.r_1_, f32[36,64,128]{2,1,0:T(8,128)S(1)} %bitcast.15, f32[36,64,128]{2,1,0:T(8,128)S(1)} %get-tuple-element.42.r_0_.r_4_.r_3_, ...), custom_call_target="tpu_custom_call" | custom-call | flops 603979776 | tf_op jit(solution)/shard_map/rim/pallas_call | solution.py:347
  68.9 0.3 pack.1
  69.2 18.0 %all_to_all.5 = f32[128,2,128]{2,1,0:T(2,128)S(1)} all-to-all(f32[128,2,128]{2,1,0:T(2,128)S(1)} %pack.1), channel_id=1, replica_groups=mesh['gx'=8,'gy'=16] {'gx','gy'}, dimensions={0} | all-to-all | bytes 262144 | tf_op jit(solution)/shard_map/all_to_all | solution.py:390
  87.4 0.6 slice.8
  (29 shorter events, 0.6 us)
Async XLA Ops:
  0.6 9.6 %copy-start.3 = (f32[2]{0:T(128)S(1)}, f32[2]{0:T(128)}, u32[]{:S(2)}) copy-start(f32[2]{0:T(128)} %r_0_.2) | copy-start | bytes 28
  0.6 9.5 %copy-start.2 = (s32[6,6]{1,0:T(8,128)S(1)}, s32[6,6]{1,0:T(8,128)}, u32[]{:S(2)}) copy-start(s32[6,6]{1,0:T(8,128)} %r_2_.1) | copy-start | bytes 436
  0.7 9.5 %copy-start.1 = (s32[6,6,9]{2,1,0:T(8,128)S(1)}, s32[6,6,9]{2,1,0:T(8,128)}, u32[]{:S(2)}) copy-start(s32[6,6,9]{2,1,0:T(8,128)} %r_1_.1) | copy-start | bytes 3892
  1.8 17.1 %collective-permute-start.1 = (f32[6,64,128]{2,1,0:T(8,128)S(1)}, f32[6,64,128]{2,1,0:T(8,128)S(1)}, u32[]{:S(2)}, u32[]{:S(2)}) collective-permute-start(f32[6,64,128]{2,1,0:T(8,128)S(1)} %get-tuple-element.38), channel_id=1, source_target_pairs={{0,16},{1,17},{2,18},{3,19},{4,20},{5,21},{6,22},{7,23},{8,24},{9,... | collective-permute-start | bytes 589832 | tf_op jit(solution)/shard_map/ppermute | solution.py:288
  5.6 13.3 %collective-permute-start.2 = (f32[6,64,128]{2,1,0:T(8,128)S(1)}, f32[6,64,128]{2,1,0:T(8,128)S(1)}, u32[]{:S(2)}, u32[]{:S(2)}) collective-permute-start(f32[6,64,128]{2,1,0:T(8,128)S(1)} %get-tuple-element.39), channel_id=1, source_target_pairs={{0,112},{1,113},{2,114},{3,115},{4,116},{5,117},{6,118},{7,119},{8... | collective-permute-start | bytes 589832 | tf_op jit(solution)/shard_map/ppermute | solution.py:288
  7.9 13.9 %collective-permute-start = (f32[6,64,128]{2,1,0:T(8,128)S(1)}, f32[6,64,128]{2,1,0:T(8,128)S(1)}, u32[]{:S(2)}, u32[]{:S(2)}) collective-permute-start(f32[6,64,128]{2,1,0:T(8,128)S(1)} %get-tuple-element.35), channel_id=1, source_target_pairs={{0,15},{1,2},{2,1},{3,4},{4,3},{5,6},{6,5},{7,8},{8,7},{9,10},{10,... | collective-permute-start | bytes 589832 | tf_op jit(solution)/shard_map/ppermute | solution.py:288
  10.2 8.7 %copy-start = (f32[6,6,64,128]{3,2,1,0:T(8,128)S(1)}, f32[6,6,64,128]{3,2,1,0:T(8,128)}, u32[]{:S(2)}) copy-start(f32[6,6,64,128]{3,2,1,0:T(8,128)} %r_0_.3) | copy-start | bytes 3538948
  18.9 6.5 %collective-permute-start.3 = (f32[8,64,128]{2,1,0:T(8,128)S(1)}, f32[8,64,128]{2,1,0:T(8,128)S(1)}, u32[]{:S(2)}, u32[]{:S(2)}) collective-permute-start(f32[8,64,128]{2,1,0:T(8,128)S(1)} %get-tuple-element.41), channel_id=1, source_target_pairs={{0,1},{1,0},{2,3},{3,2},{4,5},{5,4},{6,7},{7,6},{8,9},{9,8},{10,11... | collective-permute-start | bytes 786440 | tf_op jit(solution)/shard_map/ppermute | solution.py:288
  21.8 3.7 %collective-permute-start.4 = (f32[2,64,128]{2,1,0:T(8,128)S(1)}, f32[2,64,128]{2,1,0:T(8,128)S(1)}, u32[]{:S(2)}, u32[]{:S(2)}) collective-permute-start(f32[2,64,128]{2,1,0:T(8,128)S(1)} %get-tuple-element.40.r_2_), channel_id=1, source_target_pairs={{0,15},{1,2},{2,1},{3,4},{4,3},{5,6},{6,5},{7,8},{8,7},{9,10},{10,... | collective-permute-start | bytes 196616 | tf_op jit(solution)/shard_map/ppermute | solution.py:288
  26.7 15.8 %collective-permute-start.5 = (f32[6,64,128]{2,1,0:T(8,128)S(1)}, f32[6,64,128]{2,1,0:T(8,128)S(1)}, u32[]{:S(2)}, u32[]{:S(2)}) collective-permute-start(f32[6,64,128]{2,1,0:T(8,128)S(1)} %get-tuple-element.45), channel_id=1, source_target_pairs={{0,16},{1,17},{2,18},{3,19},{4,20},{5,21},{6,22},{7,23},{8,24},{9,... | collective-permute-start | bytes 589832 | tf_op jit(solution)/shard_map/ppermute | solution.py:288
  28.4 14.1 %collective-permute-start.6 = (f32[6,64,128]{2,1,0:T(8,128)S(1)}, f32[6,64,128]{2,1,0:T(8,128)S(1)}, u32[]{:S(2)}, u32[]{:S(2)}) collective-permute-start(f32[6,64,128]{2,1,0:T(8,128)S(1)} %get-tuple-element.46), channel_id=1, source_target_pairs={{0,112},{1,113},{2,114},{3,115},{4,116},{5,117},{6,118},{7,119},{8... | collective-permute-start | bytes 589832 | tf_op jit(solution)/shard_map/ppermute | solution.py:288
  31.9 10.7 %collective-permute-start.7 = (f32[6,64,128]{2,1,0:T(8,128)S(1)}, f32[6,64,128]{2,1,0:T(8,128)S(1)}, u32[]{:S(2)}, u32[]{:S(2)}) collective-permute-start(f32[6,64,128]{2,1,0:T(8,128)S(1)} %get-tuple-element.47), channel_id=1, source_target_pairs={{0,15},{1,2},{2,1},{3,4},{4,3},{5,6},{6,5},{7,8},{8,7},{9,10},{10,... | collective-permute-start | bytes 589832 | tf_op jit(solution)/shard_map/ppermute | solution.py:288
  34.1 7.6 %collective-permute-start.8 = (f32[1,64,128]{2,1,0:T(8,128)S(1)}, f32[1,64,128]{2,1,0:T(8,128)S(1)}, u32[]{:S(2)}, u32[]{:S(2)}) collective-permute-start(f32[1,64,128]{2,1,0:T(8,128)S(1)} %get-tuple-element.48), channel_id=1, source_target_pairs={{0,31},{1,18},{2,17},{3,20},{4,19},{5,22},{6,21},{7,24},{8,23},{9,... | collective-permute-start | bytes 98312 | tf_op jit(solution)/shard_map/ppermute | solution.py:288
  34.1 8.4 %collective-permute-start.9 = (f32[1,64,128]{2,1,0:T(8,128)S(1)}, f32[1,64,128]{2,1,0:T(8,128)S(1)}, u32[]{:S(2)}, u32[]{:S(2)}) collective-permute-start(f32[1,64,128]{2,1,0:T(8,128)S(1)} %get-tuple-element.49), channel_id=1, source_target_pairs={{0,127},{1,114},{2,113},{3,116},{4,115},{5,118},{6,117},{7,120},{8... | collective-permute-start | bytes 98312 | tf_op jit(solution)/shard_map/ppermute | solution.py:288
  42.5 4.2 %collective-permute-start.10 = (f32[8,64,128]{2,1,0:T(8,128)S(1)}, f32[8,64,128]{2,1,0:T(8,128)S(1)}, u32[]{:S(2)}, u32[]{:S(2)}) collective-permute-start(f32[8,64,128]{2,1,0:T(8,128)S(1)} %pack_close.2.r_2_), channel_id=1, source_target_pairs={{0,1},{1,0},{2,3},{3,2},{4,5},{5,4},{6,7},{7,6},{8,9},{9,8},{10,11... | collective-permute-start | bytes 786440 | tf_op jit(solution)/shard_map/ppermute | solution.py:288
  48.0 16.3 %collective-permute-start.11 = (f32[6,64,128]{2,1,0:T(8,128)S(1)}, f32[6,64,128]{2,1,0:T(8,128)S(1)}, u32[]{:S(2)}, u32[]{:S(2)}) collective-permute-start(f32[6,64,128]{2,1,0:T(8,128)S(1)} %get-tuple-element.54), channel_id=1, source_target_pairs={{0,16},{1,17},{2,18},{3,19},{4,20},{5,21},{6,22},{7,23},{8,24},{9,... | collective-permute-start | bytes 589832 | tf_op jit(solution)/shard_map/ppermute | solution.py:288
  50.6 13.8 %collective-permute-start.12 = (f32[6,64,128]{2,1,0:T(8,128)S(1)}, f32[6,64,128]{2,1,0:T(8,128)S(1)}, u32[]{:S(2)}, u32[]{:S(2)}) collective-permute-start(f32[6,64,128]{2,1,0:T(8,128)S(1)} %get-tuple-element.55), channel_id=1, source_target_pairs={{0,112},{1,113},{2,114},{3,115},{4,116},{5,117},{6,118},{7,119},{8... | collective-permute-start | bytes 589832 | tf_op jit(solution)/shard_map/ppermute | solution.py:288
  53.5 11.2 %collective-permute-start.13 = (f32[6,64,128]{2,1,0:T(8,128)S(1)}, f32[6,64,128]{2,1,0:T(8,128)S(1)}, u32[]{:S(2)}, u32[]{:S(2)}) collective-permute-start(f32[6,64,128]{2,1,0:T(8,128)S(1)} %get-tuple-element.56), channel_id=1, source_target_pairs={{0,15},{1,2},{2,1},{3,4},{4,3},{5,6},{6,5},{7,8},{8,7},{9,10},{10,... | collective-permute-start | bytes 589832 | tf_op jit(solution)/shard_map/ppermute | solution.py:288
  54.0 7.8 %collective-permute-start.14 = (f32[1,64,128]{2,1,0:T(8,128)S(1)}, f32[1,64,128]{2,1,0:T(8,128)S(1)}, u32[]{:S(2)}, u32[]{:S(2)}) collective-permute-start(f32[1,64,128]{2,1,0:T(8,128)S(1)} %get-tuple-element.57), channel_id=1, source_target_pairs={{0,31},{1,18},{2,17},{3,20},{4,19},{5,22},{6,21},{7,24},{8,23},{9,... | collective-permute-start | bytes 98312 | tf_op jit(solution)/shard_map/ppermute | solution.py:288
  54.1 10.2 %collective-permute-start.15 = (f32[1,64,128]{2,1,0:T(8,128)S(1)}, f32[1,64,128]{2,1,0:T(8,128)S(1)}, u32[]{:S(2)}, u32[]{:S(2)}) collective-permute-start(f32[1,64,128]{2,1,0:T(8,128)S(1)} %get-tuple-element.58), channel_id=1, source_target_pairs={{0,127},{1,114},{2,113},{3,116},{4,115},{5,118},{6,117},{7,120},{8... | collective-permute-start | bytes 98312 | tf_op jit(solution)/shard_map/ppermute | solution.py:288
  64.7 2.0 %collective-permute-start.16 = (f32[8,64,128]{2,1,0:T(8,128)S(1)}, f32[8,64,128]{2,1,0:T(8,128)S(1)}, u32[]{:S(2)}, u32[]{:S(2)}) collective-permute-start(f32[8,64,128]{2,1,0:T(8,128)S(1)} %pack_close.3.r_2_), channel_id=1, source_target_pairs={{0,1},{1,0},{2,3},{3,2},{4,5},{5,4},{6,7},{7,6},{8,9},{9,8},{10,11... | collective-permute-start | bytes 786440 | tf_op jit(solution)/shard_map/ppermute | solution.py:288
